TPU v7x, 128 devices: a whole 4x4x4 slice. The times are simulated.
128 devices in a mesh: dp: 8 (over y, core), queue: 16 (over z, x).
Axes of the slice: x: 4, y: 4, z: 4, core: 2. Of those that a mesh axis runs over, the one named last changes fastest.
Arguments:
- queue_keys: bfloat16 [524288, 768], P(('dp', 'queue')), may hold values from -2.5 to 2.5
- fresh_keys: bfloat16 [1024, 768], P(('dp', 'queue')), may hold values from -4 to 4
- slots: int32 [1024], P(('dp', 'queue')), may hold values from 0 to 524287, as said below
- queries: bfloat16 [1024, 768], P('dp'), may hold values from -40 to 40
- positives: int32 [1024], P('dp'), may hold values from 0 to 1023
Outputs:
- query_grad: float32 [1024, 768], P(('dp', 'queue'))
- mean_loss: float32 [], replicated
- new_queue: bfloat16 [524288, 768], P(('dp', 'queue'))
Inputs may be any that keep to these rules, and one draw needn't show every extreme that they name: The 1024 slots are distinct.
All inputs are finite; a program needn't handle non-finite values.
Results may differ from a plain program's by a relative error of at most 0.0035.
Values may be sent and summed in bfloat16 or wider, within the bound.
A program may use at most 128 MiB of HBM per device.

v0:
```python
import jax
import jax.numpy as jnp
from jax import lax
from jax.sharding import PartitionSpec as P


def score_rows(query_rows, key_rows):
    return lax.dot_general(
        query_rows, key_rows, (((1,), (1,)), ((), ())), preferred_element_type=jnp.float32
    )


def shards(queue_keys, fresh_keys, slots, queries, positives):
    all_queries = lax.all_gather(queries, "dp", axis=0, tiled=True)
    fresh_all, slots_all = (
        lax.all_gather(fresh_keys, ("dp", "queue"), axis=0, tiled=True),
        lax.all_gather(slots, ("dp", "queue"), axis=0, tiled=True),
    )
    queue_scores = score_rows(all_queries, queue_keys)
    fresh_scores = score_rows(all_queries, fresh_keys)
    local_top = jnp.maximum(jnp.max(queue_scores, axis=1), jnp.max(fresh_scores, axis=1))
    row_top = lax.pmax(local_top, ("dp", "queue"))
    queue_exp = jnp.exp(queue_scores - row_top[:, None])
    fresh_exp = jnp.exp(fresh_scores - row_top[:, None])
    local_sum = jnp.sum(queue_exp, axis=1) + jnp.sum(fresh_exp, axis=1)
    sum_exp = lax.psum(local_sum, ("dp", "queue"))
    queue_weights = queue_exp.astype(jnp.bfloat16)
    fresh_weights = fresh_exp.astype(jnp.bfloat16)
    dp_size = lax.axis_size("dp")
    queue_size = lax.axis_size("queue")
    own_rows = all_queries.shape[0] // (dp_size * queue_size)
    pulled = lax.psum_scatter(
        jnp.dot(queue_weights, queue_keys, preferred_element_type=jnp.float32)
        + jnp.dot(fresh_weights, fresh_keys, preferred_element_type=jnp.float32),
        ("dp", "queue"),
        scatter_dimension=0,
        tiled=True,
    )
    queue_index = lax.axis_index("queue")
    device_index = lax.axis_index("dp") * queue_size + queue_index
    row_start = device_index * own_rows
    top_rows = lax.dynamic_slice_in_dim(row_top, row_start, own_rows, 0)
    total_rows = lax.dynamic_slice_in_dim(sum_exp, row_start, own_rows, 0)
    local_start = queue_index * own_rows
    positive_rows = lax.dynamic_slice_in_dim(positives, local_start, own_rows, 0)
    query_rows = lax.dynamic_slice_in_dim(queries, local_start, own_rows, 0)
    positive_keys = jnp.take(fresh_all, positive_rows, axis=0).astype(jnp.float32)
    query_grad = pulled / total_rows[:, None] - positive_keys
    positive_scores = jnp.sum(query_rows.astype(jnp.float32) * positive_keys, axis=1)
    loss_part = jnp.sum(top_rows + jnp.log(total_rows) - positive_scores)
    loss_sum = lax.psum(loss_part, ("dp", "queue"))
    mean_loss = loss_sum / (own_rows * dp_size * queue_size)
    held_rows = queue_keys.shape[0]
    local_slot = slots_all - device_index * held_rows
    inside = (local_slot >= 0) & (local_slot < held_rows)
    target = jnp.where(inside, local_slot, held_rows)
    new_queue = queue_keys.at[target].set(fresh_all, mode="drop")
    return (query_grad, mean_loss, new_queue)


def solution(mesh):
    placed = (
        P(("dp", "queue"), None),
        P(("dp", "queue"), None),
        P(("dp", "queue")),
        P("dp", None),
        P("dp"),
    )
    return jax.shard_map(
        shards,
        mesh=mesh,
        in_specs=placed,
        out_specs=(P(("dp", "queue"), None), P(), P(("dp", "queue"), None)),
        check_vma=False,
    )
```

profile of v0, /device:TPU:1, one launch (start us, length us, event | category | flops | bytes accessed | tf_op | source)
XLA Modules:
  0.0 360.9 jit_solution(16796866037747466775)
XLA Ops:
  7.2 0.0 all-gather.3.cloned.1.call-start
  7.2 5.9 %copy.11 = bf16[4096,768]{1,0:T(8,128)(2,1)} copy(bf16[4096,768]{1,0:T(8,128)(2,1)} %param.5) | data formatting | bytes 12582912
  13.1 0.0 all-gather.3.cloned.1.call-update
  13.1 0.0 all-gather.5.cloned.1.call-start
  13.2 0.7 all-gather.5.cloned.1.call-update
  13.9 0.0 reduce-scatter.2.cloned.1.call-start
  13.9 27.3 %all-gather.3.cloned.1.call-done = bf16[1024,768]{1,0:T(8,128)(2,1)} async-done(((bf16[128,768]{1,0:T(8,128)(2,1)}), bf16[1024,768]{1,0:T(8,128)(2,1)}) %all-gather.3.cloned.1.call-update) | async-done | bytes 1572880 | tf_op jit(solution)/shard_map/all_gather | solution.py:14
  41.3 13.3 %fusion.10 = (f32[1024]{0:T(1024)S(1)}, f32[1024,4096]{1,0:T(8,128)}) fusion(bf16[1024,768]{1,0:T(8,128)(2,1)} %all-gather.3.cloned.1.call-done, bf16[4096,768]{1,0:T(8,128)(2,1)} %copy.11), kind=kOutput, calls=%fused_computation.21 | convolution fusion | flops 6446644224 | bytes 24645632 | tf_op jit(solution)/shard_map/dot_general | solution.py:8
  54.6 0.5 fusion.11
  55.1 64.9 %pmax.7 = f32[1024]{0:T(1024)S(1)} all-reduce(f32[1024]{0:T(1024)S(1)} %max.5), channel_id=1, replica_groups=mesh['dp'=8,'queue'=16] {'dp','queue'}, use_global_device_ids=true, to_apply=%region_2.0 | all-reduce | flops 1024 | bytes 8192 | tf_op jit(solution)/shard_map/pmax | solution.py:22
  120.1 12.3 %fusion.2 = f32[1024,768]{1,0:T(8,128)S(1)} fusion(bf16[4096,768]{1,0:T(8,128)(2,1)} %copy.11, f32[1024,4096]{1,0:T(8,128)} %get-tuple-element.8, f32[1024]{0:T(1024)S(1)} %pmax.7), kind=kOutput, calls=%fused_computation.5 | convolution fusion | flops 6450839552 | bytes 26218496 | tf_op jit(solution)/shard_map/dot_general | solution.py:33
  132.4 2.3 convolution_add_fusion
  134.7 0.0 reduce-scatter.2.cloned.1.call-update
  134.7 0.2 dynamic-update-slice
  135.0 64.1 %all-reduce = s32[1024]{0:T(1024)S(1)} all-reduce(s32[1024]{0:T(1024)S(1)} %dynamic-update-slice), channel_id=1, replica_groups=mesh['dp'=8,'queue'=16] {'dp','queue'}, use_global_device_ids=true, to_apply=%add | all-reduce | flops 1024 | bytes 8192
  199.1 0.1 compare_and_fusion
  199.2 8.2 %fusion = f32[1024]{0:T(1024)S(1)} fusion(f32[1024,4096]{1,0:T(8,128)} %get-tuple-element.8, f32[1024]{0:T(1024)S(1)} %pmax.7), kind=kLoop, calls=%fused_computation.3 | loop fusion | flops 8387584 | bytes 16785408 | tf_op jit(solution)/shard_map/reduce_sum | solution.py:25
  207.4 62.7 %psum.14 = f32[1024]{0:T(1024)S(1)} all-reduce(f32[1024]{0:T(1024)S(1)} %add.34), channel_id=1, replica_groups=mesh['dp'=8,'queue'=16] {'dp','queue'}, use_global_device_ids=true, to_apply=%region_6.0 | all-reduce | flops 1024 | bytes 8192 | tf_op jit(solution)/shard_map/psum | solution.py:26
  270.2 2.2 gather_fusion
  272.4 0.9 fusion.7
  273.3 0.7 subtract_reduce_fusion
  273.9 64.7 %psum.15 = f32[]{:T(128)} all-reduce(f32[]{:T(128)} %get-tuple-element.3), channel_id=1, replica_groups=mesh['dp'=8,'queue'=16] {'dp','queue'}, use_global_device_ids=true, to_apply=%region_9.10 | all-reduce | flops 1 | bytes 8 | tf_op jit(solution)/shard_map/psum | solution.py:51
  339.3 12.4 %scatter_fusion = bf16[4096,768]{1,0:T(8,128)(2,1)} fusion(bf16[4096,768]{1,0:T(8,128)(2,1)} %copy.11, s32[1024]{0:T(1024)S(1)} %compare_select_fusion, bf16[1024,768]{1,0:T(8,128)(2,1)} %all-gather.5.cloned.1.call-done), kind=kCustom, calls=%fused_computation.1 | custom fusion | bytes 4722688 | tf_op jit(solution)/shard_map/scatter | solution.py:57
  351.8 1.4 convert_subtract_fusion
  (16 shorter events, 0.1 us)
Async XLA Ops:
  7.2 34.1 %all-gather.3.cloned.1.call-start = ((), (), s32[]{:S(2)}) async-start(), calls=%async_computation.1 | async-start | bytes 1769472 | tf_op jit(solution)/shard_map/all_gather | solution.py:14
  13.1 257.0 %all-gather.5.cloned.1.call-start = ((), (), s32[]{:S(2)}) async-start(), calls=%async_computation.3 | async-start | bytes 1585152 | tf_op jit(solution)/shard_map/all_gather | solution.py:16
  13.9 40.7 %copy-start.1 = (bf16[8,768]{1,0:T(8,128)(2,1)S(1)}, bf16[8,768]{1,0:T(8,128)(2,1)}, u32[]{:S(2)}) copy-start(bf16[8,768]{1,0:T(8,128)(2,1)} %param.6) | copy-start | bytes 36868
  13.9 337.9 %reduce-scatter.2.cloned.1.call-start = ((), (), s32[]{:S(2)}) async-start(), calls=%async_computation.2 | async-start | bytes 3170304 | tf_op jit(solution)/shard_map/reduce_scatter | solution.py:32
  41.3 13.3 %copy-start = (bf16[1024,768]{1,0:T(8,128)(2,1)S(1)}, bf16[1024,768]{1,0:T(8,128)(2,1)}, u32[]{:S(2)}) copy-start(bf16[1024,768]{1,0:T(8,128)(2,1)} %all-gather.3.cloned.1.call-done) | copy-start | bytes 4718596
  132.3 2.4 copy-start.3
  132.4 66.7 %copy-start.2 = (s32[128]{0:T(128)S(1)}, s32[128]{0:T(128)}, u32[]{:S(2)}) copy-start(s32[128]{0:T(128)} %param.9) | copy-start | bytes 1540
Sparse Core Ops, SparseCore 0:
  13.2 27.9 all-gather.2
  44.0 64.3 all-gather.4
  134.8 205.3 reduce-scatter.1
where the time goes:
time: 362 us; the launch traced here: 361 us
  blocking collectives  256 us (71%)
  matrix products  28.4 us (8%)
  waiting for transfers between devices  28 us (8%)
  local copies, waits for them, and re-layouts  20.8 us (6%)
  between operations  15.6 us (4%)
  other arithmetic  11.4 us (3%)
    pmax x1, blocking collectives, shards(): row_top = lax.pmax(local_top, ('dp', 'queue'))  64.9 us
    psum x1, blocking collectives, shards(): loss_sum = lax.psum(loss_part, ('dp', 'queue'))  64.7 us
    unnamed x1, blocking collectives  64.1 us
    psum x1, blocking collectives, shards(): sum_exp = lax.psum(local_sum, ('dp', 'queue'))  62.7 us
    all_gather x1, waiting for transfers between devices, shards(): all_queries = lax.all_gather(queries, 'dp', axis=0, tiled=True)  27.3 us
    dot_general x2, matrix products, score_rows(): lax.dot_general(query_rows, key_rows, (((1,), (1,)), ((), ())), preferred...  13.8 us
    scatter x1, local copies, waits for them, and re-layouts, shards(): new_queue = queue_keys.at[target].set(fresh_all, mode='drop')  12.4 us
    dot_general x1, matrix products, shards(): jnp.dot(queue_weights, queue_keys, preferred_element_type=jnp.float32)  12.3 us
  transfers between devices with their start and end apart: 3, of which 1 were waited for; matrix products, arithmetic and copies ran while one was open for 15% of the time, Pallas kernels for 0%

commit v1 on v0

v1 whole, which is shorter than its diff:
```python
import functools

import jax
import jax.numpy as jnp
from jax import lax
from jax.experimental import pallas as pl
from jax.experimental.pallas import tpu as pltpu
from jax.sharding import PartitionSpec as P

MESH = pl.DeviceIdType.MESH
STAT = 128


def score_rows(query_rows, key_rows):
    return lax.dot_general(
        query_rows, key_rows, (((1,), (1,)), ((), ())), preferred_element_type=jnp.float32
    )


def _device_index():
    return lax.axis_index("dp") * lax.axis_size("queue") + lax.axis_index("queue")


def _greet_all(n, q, me):
    barrier = pltpu.get_barrier_semaphore()

    def signal(k, carry):
        dst = lax.rem(me + k, n)
        pl.semaphore_signal(
            barrier, inc=1, device_id=(dst // q, lax.rem(dst, q)), device_id_type=MESH
        )
        return carry

    lax.fori_loop(1, n, signal, 0)
    pl.semaphore_wait(barrier, n - 1)


def _send_all(n, q, me, src_of, buf, send_sem, recv_sem):
    def send(k, carry):
        dst = lax.rem(me + k, n)
        pltpu.make_async_remote_copy(
            src_ref=src_of(dst),
            dst_ref=buf.at[me],
            send_sem=send_sem,
            recv_sem=recv_sem,
            device_id=(dst // q, lax.rem(dst, q)),
            device_id_type=MESH,
        ).start()
        return carry

    lax.fori_loop(1, n, send, 0)


def _wait_all(n, q, me, src_all, buf, send_sem, recv_sem):
    total = pltpu.make_async_remote_copy(
        src_ref=src_all.at[pl.ds(0, n - 1)],
        dst_ref=buf.at[pl.ds(0, n - 1)],
        send_sem=send_sem,
        recv_sem=recv_sem,
        device_id=(lax.rem(me + 1, n) // q, lax.rem(lax.rem(me + 1, n), q)),
        device_id_type=MESH,
    )
    total.wait_send()
    total.wait_recv()


def combine_kernel(n, q, d, x_ref, o_ref, buf, send_sem, recv_sem, local_sem):
    me = _device_index()
    _greet_all(n, q, me)
    _send_all(n, q, me, lambda dst: x_ref.at[dst], buf, send_sem, recv_sem)
    mine = pltpu.make_async_copy(x_ref.at[me], buf.at[me], local_sem)
    mine.start()
    mine.wait()
    _wait_all(n, q, me, x_ref, buf, send_sem, recv_sem)

    def top(j, m):
        return jnp.maximum(m, buf[j][:, d:d + 1])

    row_top = lax.fori_loop(0, n, top, jnp.full((o_ref.shape[0], 1), -jnp.inf, jnp.float32))

    def add(j, acc):
        b = buf[j]
        scale = jnp.exp(b[:, d:d + 1] - row_top)
        return acc + b * scale

    acc = lax.fori_loop(0, n, add, jnp.zeros(o_ref.shape, jnp.float32))
    col = lax.broadcasted_iota(jnp.int32, o_ref.shape, 1)
    o_ref[...] = jnp.where(col == d, row_top, acc)


def combine(x, n, q, d):
    rows = x.shape[1]
    width = x.shape[2]
    return pl.pallas_call(
        functools.partial(combine_kernel, n, q, d),
        out_shape=jax.ShapeDtypeStruct((rows, width), jnp.float32),
        in_specs=[pl.BlockSpec(memory_space=pl.ANY)],
        out_specs=pl.BlockSpec(memory_space=pltpu.VMEM),
        scratch_shapes=[
            pltpu.VMEM((n, rows, width), jnp.float32),
            pltpu.SemaphoreType.DMA,
            pltpu.SemaphoreType.DMA,
            pltpu.SemaphoreType.DMA,
        ],
        compiler_params=pltpu.CompilerParams(collective_id=0, has_side_effects=True),
    )(x)


def total_kernel(n, q, x_ref, o_ref, buf, send_sem, recv_sem):
    me = _device_index()
    _greet_all(n, q, me)
    _send_all(n, q, me, lambda dst: x_ref, buf, send_sem, recv_sem)
    _wait_all(n, q, me, buf, buf, send_sem, recv_sem)
    buf[me] = x_ref[...]

    def add(j, acc):
        return acc + buf[j]

    o_ref[...] = lax.fori_loop(0, n, add, jnp.zeros(o_ref.shape, jnp.float32))


def device_total(x, n, q):
    return pl.pallas_call(
        functools.partial(total_kernel, n, q),
        out_shape=jax.ShapeDtypeStruct(x.shape, jnp.float32),
        in_specs=[pl.BlockSpec(memory_space=pltpu.VMEM)],
        out_specs=pl.BlockSpec(memory_space=pltpu.VMEM),
        scratch_shapes=[
            pltpu.VMEM((n,) + x.shape, jnp.float32),
            pltpu.SemaphoreType.DMA,
            pltpu.SemaphoreType.DMA,
        ],
        compiler_params=pltpu.CompilerParams(collective_id=1, has_side_effects=True),
    )(x)


def shards(queue_keys, fresh_keys, slots, queries, positives):
    dp_size = lax.axis_size("dp")
    queue_size = lax.axis_size("queue")
    n = dp_size * queue_size
    d = queries.shape[1]
    all_queries = lax.all_gather(queries, "dp", axis=0, tiled=True)
    fresh_all, slots_all = (
        lax.all_gather(fresh_keys, ("dp", "queue"), axis=0, tiled=True),
        lax.all_gather(slots, ("dp", "queue"), axis=0, tiled=True),
    )
    queue_scores = score_rows(all_queries, queue_keys)
    fresh_scores = score_rows(all_queries, fresh_keys)
    local_top = jnp.maximum(jnp.max(queue_scores, axis=1), jnp.max(fresh_scores, axis=1))
    queue_exp = jnp.exp(queue_scores - local_top[:, None])
    fresh_exp = jnp.exp(fresh_scores - local_top[:, None])
    local_sum = jnp.sum(queue_exp, axis=1) + jnp.sum(fresh_exp, axis=1)
    local_pulled = jnp.dot(
        queue_exp.astype(jnp.bfloat16), queue_keys, preferred_element_type=jnp.float32
    ) + jnp.dot(fresh_exp.astype(jnp.bfloat16), fresh_keys, preferred_element_type=jnp.float32)
    total_rows = all_queries.shape[0]
    own_rows = total_rows // n
    stats = jnp.zeros((total_rows, STAT), jnp.float32)
    stats = stats.at[:, 0].set(local_top).at[:, 1].set(local_sum)
    packed = jnp.concatenate([local_pulled, stats], axis=1).reshape(n, own_rows, d + STAT)
    combined = combine(packed, n, queue_size, d)
    top_rows = combined[:, d]
    sum_rows = combined[:, d + 1]
    pulled = combined[:, :d]

    queue_index = lax.axis_index("queue")
    device_index = _device_index()
    local_start = queue_index * own_rows
    positive_rows = lax.dynamic_slice_in_dim(positives, local_start, own_rows, 0)
    query_rows = lax.dynamic_slice_in_dim(queries, local_start, own_rows, 0)
    positive_keys = jnp.take(fresh_all, positive_rows, axis=0).astype(jnp.float32)
    query_grad = pulled / sum_rows[:, None] - positive_keys
    positive_scores = jnp.sum(query_rows.astype(jnp.float32) * positive_keys, axis=1)
    loss_part = jnp.sum(top_rows + jnp.log(sum_rows) - positive_scores)
    loss_sum = device_total(jnp.full((8, 128), loss_part, jnp.float32), n, queue_size)[0, 0]
    mean_loss = loss_sum / total_rows
    held_rows = queue_keys.shape[0]
    local_slot = slots_all - device_index * held_rows
    inside = (local_slot >= 0) & (local_slot < held_rows)
    target = jnp.where(inside, local_slot, held_rows)
    new_queue = queue_keys.at[target].set(fresh_all, mode="drop")
    return (query_grad, mean_loss, new_queue)


def solution(mesh):
    placed = (
        P(("dp", "queue"), None),
        P(("dp", "queue"), None),
        P(("dp", "queue")),
        P("dp", None),
        P("dp"),
    )
    return jax.shard_map(
        shards,
        mesh=mesh,
        in_specs=placed,
        out_specs=(P(("dp", "queue"), None), P(), P(("dp", "queue"), None)),
        check_vma=False,
    )
```

time: 362 us -> 248 us (0.69)
  blocking collectives: 256 us -> 69.8 us
  Pallas kernels: 0 us -> 87.8 us
  waiting for transfers between devices: 28 us -> 0.74 us
  local copies, waits for them, and re-layouts: 20.8 us -> 29.5 us
  other arithmetic: 11.4 us -> 15.4 us
    psum x2 -> x0, blocking collectives: 127 us -> none  [the longest x1 64.7 us: shards(): loss_sum = lax.psum(loss_part, ('dp', 'queue'))]
    pallas_call x0 -> x2, Pallas kernels: none -> 87.8 us  [the longest x1 70.1 us: combine(): pl.pallas_call(functools.partial(combine_kernel, n, q, d), out_shape=jax....]
    pmax x1 -> x0, blocking collectives: 64.9 us -> none  [shards(): row_top = lax.pmax(local_top, ('dp', 'queue'))]
    all_gather x1, waiting for transfers between devices: 27.3 us -> 0.01 us  [shards(): all_queries = lax.all_gather(queries, 'dp', axis=0, tiled=True)]
    unnamed x1, blocking collectives: 64.1 us -> 69.8 us
    concatenate x0 -> x1, local copies, waits for them, and re-layouts: none -> 5.03 us  [shards(): jnp.concatenate([local_pulled, stats], axis=1)]
  transfers between devices with their start and end apart: 3 -> 2, of which waited for: 1 -> 0; matrix products, arithmetic and copies ran while one was open for 15% -> 19% of each run, Pallas kernels for 0% -> 28%
where the time goes in v1:
time: 248 us; the launch traced here: 247 us
  Pallas kernels  87.8 us (35%)
  blocking collectives  69.8 us (28%)
  local copies, waits for them, and re-layouts  29.5 us (12%)
  matrix products  27.7 us (11%)
  between operations  16 us (6%)
  other arithmetic  15.4 us (6%)
    pallas_call x1, Pallas kernels, combine(): pl.pallas_call(functools.partial(combine_kernel, n, q, d), out_shape=jax....  70.1 us
    unnamed x1, blocking collectives  69.8 us
    pallas_call x1, Pallas kernels, device_total(): pl.pallas_call(functools.partial(total_kernel, n, q), out_shape=jax.Shape...  17.7 us
    dot_general x2, matrix products, score_rows(): lax.dot_general(query_rows, key_rows, (((1,), (1,)), ((), ())), preferred...  14.5 us
    dot_general x1, matrix products, shards(): jnp.dot(queue_exp.astype(jnp.bfloat16), queue_keys, preferred_element_typ...  12.5 us
    scatter x1, local copies, waits for them, and re-layouts, shards(): new_queue = queue_keys.at[target].set(fresh_all, mode='drop')  12.4 us
    reduce_sum x2, other arithmetic, shards(): local_sum = jnp.sum(queue_exp, axis=1) + jnp.sum(fresh_exp, axis=1)  8.28 us
    unnamed x9, local copies, waits for them, and re-layouts  6.16 us
  transfers between devices with their start and end apart: 2, of which 0 were waited for; matrix products, arithmetic and copies ran while one was open for 19% of the time, Pallas kernels for 28%

profile of v1, /device:TPU:1, one launch (start us, length us, event | category | flops | bytes accessed | tf_op | source)
XLA Modules:
  0.0 246.9 jit_solution(8763052503979789362)
XLA Ops:
  7.2 5.9 %copy.14 = bf16[4096,768]{1,0:T(8,128)(2,1)} copy(bf16[4096,768]{1,0:T(8,128)(2,1)} %param.9) | data formatting | bytes 12582912
  13.2 0.7 all-gather.5.cloned.1.call-update
  13.9 0.6 compare_reduce_fusion.1
  14.6 0.6 compare_reduce_fusion
  15.6 69.8 %all-reduce.1 = s32[1024]{0:T(1024)S(1)} all-reduce(s32[1024]{0:T(1024)S(1)} %dynamic-update-slice.6), channel_id=1, replica_groups=mesh['dp'=8,'queue'=16] {'dp','queue'}, use_global_device_ids=true, to_apply=%add.1 | all-reduce | flops 1024 | bytes 8192
  85.4 1.9 fusion.11
  87.3 12.6 %fusion.10 = (f32[1024]{0:T(1024)S(1)}, f32[1024,4096]{1,0:T(8,128)}) fusion(bf16[1024,768]{1,0:T(8,128)(2,1)} %all-gather.3.cloned.1.call-done, bf16[4096,768]{1,0:T(8,128)(2,1)} %copy.14), kind=kOutput, calls=%fused_computation.29 | convolution fusion | flops 6446644224 | bytes 24645632 | tf_op jit(solution)/shard_map/dot_general | solution.py:15
  99.9 0.6 broadcast_select_fusion.1
  100.6 8.3 %fusion = f32[1024]{0:T(1024)S(1)} fusion(f32[1024,4096]{1,0:T(8,128)} %get-tuple-element.36, f32[1024]{0:T(1024)S(1)} %get-tuple-element.32), kind=kLoop, calls=%fused_computation.3 | loop fusion | flops 8387584 | bytes 16785408 | tf_op jit(solution)/shard_map/reduce_sum | solution.py:152
  108.9 0.7 add_select_fusion
  109.6 0.3 scatter.18
  109.8 12.5 %fusion.2 = f32[1024,768]{0,1:T(8,128)S(1)} fusion(bf16[4096,768]{1,0:T(8,128)(2,1)} %copy.14, f32[1024,4096]{1,0:T(8,128)} %get-tuple-element.36, f32[1024]{0:T(1024)S(1)} %get-tuple-element.32), kind=kOutput, calls=%fused_computation.5 | convolution fusion | flops 6450839552 | bytes 26218496 | tf_op jit(solution)/shard_map/dot_general | solution.py:153
  122.4 0.6 convolution_add_fusion
  123.0 2.3 pad_maximum_fusion
  125.3 5.0 %copy.9 = f32[1024,896]{1,0:T(8,128)} copy(f32[1024,896]{0,1:T(8,128)} %pad_maximum_fusion) | data formatting | bytes 7340032 | tf_op jit(solution)/shard_map/concatenate | solution.py:160
  130.3 70.1 %shard_map.76 = f32[8,896]{1,0:T(8,128)} custom-call(f32[128,8,896]{2,1,0:T(8,128)} %bitcast.10), custom_call_target="tpu_custom_call" | custom-call | tf_op jit(solution)/shard_map/pallas_call | solution.py:94
  200.4 1.0 slice_reduce_fusion
  201.4 2.2 gather_fusion
  203.6 1.6 fusion.7
  205.2 0.6 subtract_reduce_fusion
  205.8 1.2 broadcast_in_dim.26.x_ref
  207.0 17.7 %shard_map.77 = f32[8,128]{1,0:T(8,128)} custom-call(f32[8,128]{1,0:T(8,128)} %broadcast_in_dim.26.x_ref), custom_call_target="tpu_custom_call" | custom-call | tf_op jit(solution)/shard_map/pallas_call | solution.py:123
  224.7 1.2 slice.44
  226.5 12.4 %scatter_fusion = bf16[4096,768]{1,0:T(8,128)(2,1)} fusion(bf16[4096,768]{1,0:T(8,128)(2,1)} %copy.14, s32[1024]{0:T(1024)S(1)} %compare_select_fusion, bf16[1024,768]{1,0:T(8,128)(2,1)} %all-gather.5.cloned.1.call-done), kind=kCustom, calls=%fused_computation.1 | custom fusion | bytes 4722688 | tf_op jit(solution)/shard_map/scatter | solution.py:181
  (18 shorter events, 0.5 us)
Async XLA Ops:
  7.2 8.1 %copy-start.2 = (s32[8]{0:T(128)S(1)}, s32[8]{0:T(128)}, u32[]{:S(2)}) copy-start(s32[8]{0:T(128)} %param.11) | copy-start | bytes 100
  7.2 78.2 %copy-start = (bf16[8,768]{1,0:T(8,128)(2,1)S(1)}, bf16[8,768]{1,0:T(8,128)(2,1)}, u32[]{:S(2)}) copy-start(bf16[8,768]{1,0:T(8,128)(2,1)} %param.10) | copy-start | bytes 36868
  7.2 8.0 %copy-start.1 = (s32[128]{0:T(128)S(1)}, s32[128]{0:T(128)}, u32[]{:S(2)}) copy-start(s32[128]{0:T(128)} %param.13) | copy-start | bytes 1540
  7.2 78.2 %all-gather.3.cloned.1.call-start = ((), (), s32[]{:S(2)}) async-start(), calls=%async_computation | async-start | bytes 1769472 | tf_op jit(solution)/shard_map/all_gather | solution.py:142
  13.2 188.2 %all-gather.5.cloned.1.call-start = ((), (), s32[]{:S(2)}) async-start(), calls=%async_computation.1 | async-start | bytes 1585152 | tf_op jit(solution)/shard_map/all_gather | solution.py:144
Sparse Core Ops, SparseCore 0:
  13.3 28.2 all-gather.2
  44.4 64.2 all-gather.4

commit v2 on v0

v2 whole, which is shorter than its diff:
```python
import functools

import jax
import jax.numpy as jnp
from jax import lax
from jax.experimental import pallas as pl
from jax.experimental.pallas import tpu as pltpu
from jax.sharding import PartitionSpec as P

MESH = pl.DeviceIdType.MESH
STAT = 128


def score_rows(query_rows, key_rows):
    return lax.dot_general(
        query_rows, key_rows, (((1,), (1,)), ((), ())), preferred_element_type=jnp.float32
    )


def _device_index():
    return lax.axis_index("dp") * lax.axis_size("queue") + lax.axis_index("queue")


def _wait_bytes(src, dst, send_sem, recv_sem, device_id):
    total = pltpu.make_async_remote_copy(
        src_ref=src, dst_ref=dst, send_sem=send_sem, recv_sem=recv_sem,
        device_id=device_id, device_id_type=MESH,
    )
    total.wait_send()
    total.wait_recv()


def _merge(blocks, d):
    tops = blocks[:, :, d:d + 1]
    top = jnp.max(tops, axis=0)
    return top, jnp.sum(blocks * jnp.exp(tops - top[None]), axis=0)


def combine_kernel(d, x_ref, pos_ref, o_ref, loss_ref, own, pair, merged, gathered,
                   loss_in, loss_pair, sems):
    q = lax.axis_size("queue")
    g = x_ref.shape[1]
    dp = lax.axis_index("dp")
    y, c = dp // 2, lax.rem(dp, 2)
    qi = lax.axis_index("queue")
    me = y * q + qi
    partner = (dp + 1 - 2 * c, qi)

    def peer(k):
        return ((k // q) * 2 + c, lax.rem(k, q))

    barrier = pltpu.get_barrier_semaphore()
    pl.semaphore_signal(barrier, inc=1, device_id=partner, device_id_type=MESH)

    def greet(k, carry):
        pl.semaphore_signal(barrier, inc=1, device_id=peer(lax.rem(me + k, g)), device_id_type=MESH)
        return carry

    lax.fori_loop(1, g, greet, 0)
    pl.semaphore_wait(barrier, g)

    to_pair = pltpu.make_async_remote_copy(
        src_ref=x_ref.at[1 - c], dst_ref=pair, send_sem=sems.at[0], recv_sem=sems.at[1],
        device_id=partner, device_id_type=MESH,
    )
    to_pair.start()
    mine = pltpu.make_async_copy(x_ref.at[c], own, sems.at[2])
    mine.start()
    mine.wait()
    to_pair.wait()

    def merge_pair(k, carry):
        top, acc = _merge(jnp.stack([own[k], pair[k]]), d)
        col = lax.broadcasted_iota(jnp.int32, acc.shape, 1)
        merged[k] = jnp.where(col == d, top, acc)
        return carry

    lax.fori_loop(0, g, merge_pair, 0)

    def send(k, carry):
        dst = lax.rem(me + k, g)
        pltpu.make_async_remote_copy(
            src_ref=merged.at[dst], dst_ref=gathered.at[me], send_sem=sems.at[3],
            recv_sem=sems.at[4], device_id=peer(dst), device_id_type=MESH,
        ).start()
        return carry

    lax.fori_loop(1, g, send, 0)
    gathered[me] = merged[me]
    _wait_bytes(merged.at[pl.ds(0, g - 1)], gathered.at[pl.ds(0, g - 1)], sems.at[3], sems.at[4],
                peer(lax.rem(me + 1, g)))
    def top_of(k, m):
        return jnp.maximum(m, gathered[k][:, d:d + 1])

    top = lax.fori_loop(0, g, top_of, jnp.full((o_ref.shape[0], 1), -jnp.inf, jnp.float32))

    def add_block(k, acc):
        b = gathered[k]
        return acc + b * jnp.exp(b[:, d:d + 1] - top)

    acc = lax.fori_loop(0, g, add_block, jnp.zeros(o_ref.shape, jnp.float32))
    col = lax.broadcasted_iota(jnp.int32, acc.shape, 1)
    o_ref[...] = jnp.where(col == d, top, acc)

    sums = acc[:, d + 1:d + 2]
    part = jnp.sum(top + jnp.log(sums) - pos_ref[:, 0:1])
    tile = jnp.full(loss_ref.shape, part, jnp.float32)
    loss_in[me] = tile

    def send_loss(k, carry):
        dst = lax.rem(me + k, g)
        pltpu.make_async_remote_copy(
            src_ref=loss_in.at[me], dst_ref=loss_in.at[me], send_sem=sems.at[5],
            recv_sem=sems.at[6], device_id=peer(dst), device_id_type=MESH,
        ).start()
        return carry

    lax.fori_loop(1, g, send_loss, 0)
    _wait_bytes(loss_in.at[pl.ds(0, g - 1)], loss_in.at[pl.ds(0, g - 1)], sems.at[5], sems.at[6],
                peer(lax.rem(me + 1, g)))

    def add(k, total):
        return total + loss_in[k]

    core_total = lax.fori_loop(0, g, add, jnp.zeros(loss_ref.shape, jnp.float32))
    loss_pair[c] = core_total
    to_pair_loss = pltpu.make_async_remote_copy(
        src_ref=loss_pair.at[c], dst_ref=loss_pair.at[c], send_sem=sems.at[7], recv_sem=sems.at[8],
        device_id=partner, device_id_type=MESH,
    )
    to_pair_loss.start()
    to_pair_loss.wait()
    loss_ref[...] = loss_pair[0] + loss_pair[1]


def combine(x, pos, d):
    g, rows, width = x.shape[1:]
    return pl.pallas_call(
        functools.partial(combine_kernel, d),
        out_shape=(
            jax.ShapeDtypeStruct((rows, width), jnp.float32),
            jax.ShapeDtypeStruct((8, 128), jnp.float32),
        ),
        in_specs=[pl.BlockSpec(memory_space=pl.ANY), pl.BlockSpec(memory_space=pltpu.VMEM)],
        out_specs=(pl.BlockSpec(memory_space=pltpu.VMEM), pl.BlockSpec(memory_space=pltpu.VMEM)),
        scratch_shapes=[
            pltpu.VMEM((g, rows, width), jnp.float32),
            pltpu.VMEM((g, rows, width), jnp.float32),
            pltpu.VMEM((g, rows, width), jnp.float32),
            pltpu.VMEM((g, rows, width), jnp.float32),
            pltpu.VMEM((g, 8, 128), jnp.float32),
            pltpu.VMEM((2, 8, 128), jnp.float32),
            pltpu.SemaphoreType.DMA((9,)),
        ],
        compiler_params=pltpu.CompilerParams(collective_id=0, has_side_effects=True),
    )(x, pos)


def shards(queue_keys, fresh_keys, slots, queries, positives):
    dp_size = lax.axis_size("dp")
    queue_size = lax.axis_size("queue")
    n = dp_size * queue_size
    d = queries.shape[1]
    gathered = lax.all_gather(queries, "dp", axis=0, tiled=True)
    total_rows = gathered.shape[0]
    own_rows = total_rows // n
    all_queries = gathered.reshape(dp_size // 2, 2, total_rows // dp_size, d)
    all_queries = all_queries.transpose(1, 0, 2, 3).reshape(total_rows, d)
    digits = jnp.stack([slots // 16384, (slots // 128) % 128, slots % 128], axis=1)
    code = jnp.zeros((slots.shape[0], STAT), jnp.bfloat16).at[:, :3].set(digits.astype(jnp.bfloat16))
    fresh_ext = lax.all_gather(
        jnp.concatenate([fresh_keys, code], axis=1), ("dp", "queue"), axis=0, tiled=True
    )
    fresh_all = fresh_ext[:, :d]
    got = fresh_ext[:, d:d + 3].astype(jnp.int32)
    slots_all = got[:, 0] * 16384 + got[:, 1] * 128 + got[:, 2]
    queue_scores = score_rows(all_queries, queue_keys)
    fresh_scores = score_rows(all_queries, fresh_keys)
    local_top = jnp.maximum(jnp.max(queue_scores, axis=1), jnp.max(fresh_scores, axis=1))
    queue_exp = jnp.exp(queue_scores - local_top[:, None])
    fresh_exp = jnp.exp(fresh_scores - local_top[:, None])
    local_sum = jnp.sum(queue_exp, axis=1) + jnp.sum(fresh_exp, axis=1)
    local_pulled = jnp.dot(
        queue_exp.astype(jnp.bfloat16), queue_keys, preferred_element_type=jnp.float32
    ) + jnp.dot(fresh_exp.astype(jnp.bfloat16), fresh_keys, preferred_element_type=jnp.float32)
    stats = jnp.zeros((total_rows, STAT), jnp.float32)
    stats = stats.at[:, 0].set(local_top).at[:, 1].set(local_sum)
    packed = jnp.concatenate([local_pulled, stats], axis=1).reshape(2, n // 2, own_rows, d + STAT)

    queue_index = lax.axis_index("queue")
    device_index = _device_index()
    local_start = queue_index * own_rows
    positive_rows = lax.dynamic_slice_in_dim(positives, local_start, own_rows, 0)
    query_rows = lax.dynamic_slice_in_dim(queries, local_start, own_rows, 0)
    positive_keys = jnp.take(fresh_all, positive_rows, axis=0).astype(jnp.float32)
    positive_scores = jnp.sum(query_rows.astype(jnp.float32) * positive_keys, axis=1)
    pos_tile = jnp.zeros((own_rows, 128), jnp.float32).at[:, 0].set(positive_scores)
    combined, loss_tile = combine(packed, pos_tile, d)
    sum_rows = combined[:, d + 1]
    pulled = combined[:, :d]
    query_grad = pulled / sum_rows[:, None] - positive_keys
    mean_loss = loss_tile[0, 0] / total_rows
    held_rows = queue_keys.shape[0]
    local_slot = slots_all - device_index * held_rows
    inside = (local_slot >= 0) & (local_slot < held_rows)
    target = jnp.where(inside, local_slot, held_rows)
    new_queue = queue_keys.at[target].set(fresh_all, mode="drop")
    return (query_grad, mean_loss, new_queue)


def solution(mesh):
    placed = (
        P(("dp", "queue"), None),
        P(("dp", "queue"), None),
        P(("dp", "queue")),
        P("dp", None),
        P("dp"),
    )
    return jax.shard_map(
        shards,
        mesh=mesh,
        in_specs=placed,
        out_specs=(P(("dp", "queue"), None), P(), P(("dp", "queue"), None)),
        check_vma=False,
    )
```

time: 362 us -> 197 us (0.54)
  blocking collectives: 256 us -> 0 us
  Pallas kernels: 0 us -> 57.4 us
  waiting for transfers between devices: 28 us -> 47.5 us
  local copies, waits for them, and re-layouts: 20.8 us -> 29.9 us
  other arithmetic: 11.4 us -> 18.7 us
    psum x2 -> x0, blocking collectives: 127 us -> none  [the longest x1 64.7 us: shards(): loss_sum = lax.psum(loss_part, ('dp', 'queue'))]
    pmax x1 -> x0, blocking collectives: 64.9 us -> none  [shards(): row_top = lax.pmax(local_top, ('dp', 'queue'))]
    unnamed x1 -> x0, blocking collectives: 64.1 us -> none
    pallas_call x0 -> x1, Pallas kernels: none -> 57.4 us  [combine(): pl.pallas_call(functools.partial(combine_kernel, d), out_shape=(jax.Shape...]
    all_gather x2, waiting for transfers between devices: 27.3 us -> 47.5 us  [the longest x1 24.3 us: shards(): gathered = lax.all_gather(queries, 'dp', axis=0, tiled=True)]
    concatenate x0 -> x1, local copies, waits for them, and re-layouts: none -> 5.04 us  [shards(): jnp.concatenate([local_pulled, stats], axis=1)]
    another operation x0 -> x8, other arithmetic: none -> 4.73 us
    slice x0 -> x3, local copies, waits for them, and re-layouts: none -> 3.7 us  [the longest x1 1.64 us: shards(): fresh_all = fresh_ext[:, :d]]
  transfers between devices with their start and end apart: 3 -> 2, of which waited for: 1 -> 2; matrix products, arithmetic and copies ran while one was open for 15% -> 25% of each run, Pallas kernels for 0% -> 0%
where the time goes in v2:
time: 197 us; the launch traced here: 196 us
  Pallas kernels  57.4 us (29%)
  waiting for transfers between devices  47.5 us (24%)
  local copies, waits for them, and re-layouts  29.9 us (15%)
  matrix products  26.7 us (14%)
  other arithmetic  18.7 us (9%)
  between operations  16 us (8%)
    pallas_call x1, Pallas kernels, combine(): pl.pallas_call(functools.partial(combine_kernel, d), out_shape=(jax.Shape...  57.4 us
    all_gather x1, waiting for transfers between devices, shards(): gathered = lax.all_gather(queries, 'dp', axis=0, tiled=True)  24.3 us
    all_gather x1, waiting for transfers between devices, shards(): lax.all_gather(jnp.concatenate([fresh_keys, code], axis=1), ('dp', 'queue...  23.2 us
    dot_general x2, matrix products, score_rows(): lax.dot_general(query_rows, key_rows, (((1,), (1,)), ((), ())), preferred...  13.5 us
    dot_general x1, matrix products, shards(): jnp.dot(queue_exp.astype(jnp.bfloat16), queue_keys, preferred_element_typ...  12.5 us
    scatter x1, local copies, waits for them, and re-layouts, shards(): new_queue = queue_keys.at[target].set(fresh_all, mode='drop')  11.9 us
    reduce_sum x2, other arithmetic, shards(): local_sum = jnp.sum(queue_exp, axis=1) + jnp.sum(fresh_exp, axis=1)  8.13 us
    unnamed x9, local copies, waits for them, and re-layouts  5.91 us
  transfers between devices with their start and end apart: 2, of which 2 were waited for; matrix products, arithmetic and copies ran while one was open for 25% of the time, Pallas kernels for 0%

profile of v2, /device:TPU:1, one launch (start us, length us, event | category | flops | bytes accessed | tf_op | source)
XLA Modules:
  0.0 196.3 jit_solution(6993605744453289231)
XLA Ops:
  7.2 5.9 %copy.27 = bf16[4096,768]{1,0:T(8,128)(2,1)} copy(bf16[4096,768]{1,0:T(8,128)(2,1)} %param.13) | data formatting | bytes 12582912
  13.5 0.6 compare_reduce_fusion
  14.2 0.7 maximum_select_fusion
  15.5 0.6 compare_reduce_fusion.2
  16.2 0.7 compare_reduce_fusion.1
  17.0 24.3 %all-gather.3.cloned.1.call-done = bf16[1024,768]{1,0:T(8,128)(2,1)} async-done(((bf16[128,768]{1,0:T(8,128)(2,1)}), bf16[1024,768]{1,0:T(8,128)(2,1)}) %all-gather.3.cloned.1.call-update) | async-done | bytes 1572880 | tf_op jit(solution)/shard_map/all_gather | solution.py:164
  41.3 1.5 copy.18
  43.3 13.0 %fusion.23 = (f32[1024]{0:T(1024)S(1)}, f32[1024,4096]{1,0:T(8,128)}) fusion(bf16[1024,768]{1,0:T(8,128)(2,1)S(1)} %bitcast.24, bf16[4096,768]{1,0:T(8,128)(2,1)} %copy.27), kind=kOutput, calls=%fused_computation.61 | convolution fusion | flops 6446644224 | bytes 24645632 | tf_op jit(solution)/shard_map/dot_general | solution.py:15
  56.3 0.6 broadcast_select_fusion.1
  57.1 8.1 %fusion = f32[1024]{0:T(1024)S(1)} fusion(f32[1024,4096]{1,0:T(8,128)} %get-tuple-element.63, f32[1024]{0:T(1024)S(1)} %get-tuple-element.58), kind=kLoop, calls=%fused_computation.3 | loop fusion | flops 8387584 | bytes 16785408 | tf_op jit(solution)/shard_map/reduce_sum | solution.py:182
  65.2 0.7 add_select_fusion
  66.2 12.5 %fusion.2 = f32[1024,768]{0,1:T(8,128)S(1)} fusion(bf16[4096,768]{1,0:T(8,128)(2,1)} %copy.27, f32[1024,4096]{1,0:T(8,128)} %get-tuple-element.63, f32[1024]{0:T(1024)S(1)} %get-tuple-element.58), kind=kOutput, calls=%fused_computation.5 | convolution fusion | flops 6450839552 | bytes 26218496 | tf_op jit(solution)/shard_map/dot_general | solution.py:183
  78.7 0.6 convolution_add_fusion
  79.4 2.3 %pad_maximum_fusion = f32[1024,896]{0,1:T(8,128)} fusion(f32[1024,128]{0,1:T(8,128)S(1)} %scatter.21, f32[1024,768]{0,1:T(8,128)S(1)} %convolution_add_fusion), kind=kLoop, calls=%fused_computation.7 | loop fusion | flops 917504 | bytes 7340032 | tf_op jit(solution)/shard_map/concatenate | solution.py:188
  81.7 5.0 %copy.19 = f32[1024,896]{1,0:T(8,128)} copy(f32[1024,896]{0,1:T(8,128)} %pad_maximum_fusion) | data formatting | bytes 7340032 | tf_op jit(solution)/shard_map/concatenate | solution.py:188
  86.7 23.2 %all-gather.5.cloned.1.call-done = bf16[1024,896]{1,0:T(8,128)(2,1)} async-done(((bf16[8,896]{1,0:T(8,128)(2,1)}), bf16[1024,896]{1,0:T(8,128)(2,1)}) %all-gather.5.cloned.1.call-update) | async-done | bytes 1835024 | tf_op jit(solution)/shard_map/all_gather | solution.py:171
  109.9 1.6 slice.93
  112.1 0.9 fusion.11
  113.0 0.7 fusion.15
  114.4 57.4 %shard_map.76 = (f32[8,896]{1,0:T(8,128)}, f32[8,128]{1,0:T(8,128)}) custom-call(f32[2,64,8,896]{3,2,1,0:T(8,128)} %bitcast.22, f32[8,128]{1,0:T(8,128)} %scatter.30.pos_ref), custom_call_target="tpu_custom_call" | custom-call | tf_op jit(solution)/shard_map/pallas_call | solution.py:138
  171.8 0.9 slice_reduce_fusion
  172.7 1.4 convert_subtract_fusion
  174.1 1.2 slice.86
  176.5 11.9 %scatter_custom_fusion = bf16[4096,768]{1,0:T(8,128)(2,1)} fusion(bf16[4096,768]{1,0:T(8,128)(2,1)} %copy.27, s32[1024]{0:T(1024)S(1)} %fusion.5, bf16[1024,896]{1,0:T(8,128)(2,1)S(1)} %copy-done), kind=kCustom, calls=%fused_computation.59 | custom fusion | bytes 7864320 | tf_op jit(solution)/shard_map/scatter | solution.py:207
  (28 shorter events, 3.8 us)
Async XLA Ops:
  7.2 6.0 %copy-start.2 = (s32[8]{0:T(128)S(1)}, s32[8]{0:T(128)}, u32[]{:S(2)}) copy-start(s32[8]{0:T(128)} %param.15) | copy-start | bytes 100
  7.2 7.7 %copy-start.1 = (bf16[8,768]{1,0:T(8,128)(2,1)S(1)}, bf16[8,768]{1,0:T(8,128)(2,1)}, u32[]{:S(2)}) copy-start(bf16[8,768]{1,0:T(8,128)(2,1)} %param.14) | copy-start | bytes 36868
  7.2 9.7 %copy-start.3 = (s32[128]{0:T(128)S(1)}, s32[128]{0:T(128)}, u32[]{:S(2)}) copy-start(s32[128]{0:T(128)} %param.17) | copy-start | bytes 1540
  7.2 34.1 %all-gather.3.cloned.1.call-start = ((), (), s32[]{:S(2)}) async-start(), calls=%async_computation | async-start | bytes 1769472 | tf_op jit(solution)/shard_map/all_gather | solution.py:164
  13.2 96.7 %all-gather.5.cloned.1.call-start = ((), (), s32[]{:S(2)}) async-start(), calls=%async_computation.1 | async-start | bytes 1849344 | tf_op jit(solution)/shard_map/all_gather | solution.py:171
  109.9 66.0 %copy-start = (bf16[1024,896]{1,0:T(8,128)(2,1)S(1)}, bf16[1024,896]{1,0:T(8,128)(2,1)}, u32[]{:S(2)}) copy-start(bf16[1024,896]{1,0:T(8,128)(2,1)} %all-gather.5.cloned.1.call-done) | copy-start | bytes 5505028
Sparse Core Ops, SparseCore 0:
  13.3 27.9 all-gather.2
  44.7 65.1 all-gather.4

commit v3 on v2

v3 whole, which is shorter than its diff:
```python
import functools

import jax
import jax.numpy as jnp
from jax import lax
from jax.experimental import pallas as pl
from jax.experimental.pallas import tpu as pltpu
from jax.sharding import PartitionSpec as P

MESH = pl.DeviceIdType.MESH
STAT = 128


def score_rows(query_rows, key_rows):
    return lax.dot_general(
        query_rows, key_rows, (((1,), (1,)), ((), ())), preferred_element_type=jnp.float32
    )


def _device_index():
    return lax.axis_index("dp") * lax.axis_size("queue") + lax.axis_index("queue")


def _wait_bytes(src, dst, send_sem, recv_sem, device_id):
    total = pltpu.make_async_remote_copy(
        src_ref=src, dst_ref=dst, send_sem=send_sem, recv_sem=recv_sem,
        device_id=device_id, device_id_type=MESH,
    )
    total.wait_send()
    total.wait_recv()


def combine_kernel(d, p_ref, s_ref, pos_ref, qk_ref, o_ref, loss_ref, nq_ref, own_p, own_s,
                   pair_p, pair_s, merged, gathered, loss_in, loss_pair, sems):
    q = lax.axis_size("queue")
    g = p_ref.shape[1]
    dp = lax.axis_index("dp")
    y, c = dp // 2, lax.rem(dp, 2)
    qi = lax.axis_index("queue")
    me = y * q + qi
    partner = (dp + 1 - 2 * c, qi)

    def peer(k):
        return ((k // q) * 2 + c, lax.rem(k, q))

    queue_copy = pltpu.make_async_copy(qk_ref, nq_ref, sems.at[9])
    queue_copy.start()

    barrier = pltpu.get_barrier_semaphore()
    pl.semaphore_signal(barrier, inc=1, device_id=partner, device_id_type=MESH)

    def greet(k, carry):
        pl.semaphore_signal(barrier, inc=1, device_id=peer(lax.rem(me + k, g)), device_id_type=MESH)
        return carry

    lax.fori_loop(1, g, greet, 0)
    pl.semaphore_wait(barrier, g)

    pair_copies = [
        pltpu.make_async_remote_copy(
            src_ref=src.at[1 - c], dst_ref=dst, send_sem=sems.at[2 * i], recv_sem=sems.at[2 * i + 1],
            device_id=partner, device_id_type=MESH,
        )
        for i, (src, dst) in enumerate(((p_ref, pair_p), (s_ref, pair_s)))
    ]
    for copy in pair_copies:
        copy.start()
    mine = [pltpu.make_async_copy(src.at[c], dst, sems.at[10 + i])
            for i, (src, dst) in enumerate(((p_ref, own_p), (s_ref, own_s)))]
    for copy in mine:
        copy.start()
    for copy in mine + pair_copies:
        copy.wait()

    def merge_pair(k, carry):
        a, b = own_s[k], pair_s[k]
        top = jnp.maximum(a[:, 0:1], b[:, 0:1])
        wa, wb = jnp.exp(a[:, 0:1] - top), jnp.exp(b[:, 0:1] - top)
        merged[k, :, :d] = own_p[k] * wa + pair_p[k] * wb
        col = lax.broadcasted_iota(jnp.int32, a.shape, 1)
        merged[k, :, d:] = jnp.where(col == 0, top, a * wa + b * wb)
        return carry

    lax.fori_loop(0, g, merge_pair, 0)

    def send(k, carry):
        dst = lax.rem(me + k, g)
        pltpu.make_async_remote_copy(
            src_ref=merged.at[dst], dst_ref=gathered.at[me], send_sem=sems.at[4],
            recv_sem=sems.at[5], device_id=peer(dst), device_id_type=MESH,
        ).start()
        return carry

    lax.fori_loop(1, g, send, 0)
    gathered[me] = merged[me]
    _wait_bytes(merged.at[pl.ds(0, g - 1)], gathered.at[pl.ds(0, g - 1)], sems.at[4], sems.at[5],
                peer(lax.rem(me + 1, g)))

    def top_of(k, m):
        return jnp.maximum(m, gathered[k][:, d:d + 1])

    top = lax.fori_loop(0, g, top_of, jnp.full((o_ref.shape[0], 1), -jnp.inf, jnp.float32))

    def add_block(k, acc):
        b = gathered[k]
        return acc + b * jnp.exp(b[:, d:d + 1] - top)

    acc = lax.fori_loop(0, g, add_block, jnp.zeros(o_ref.shape, jnp.float32))
    col = lax.broadcasted_iota(jnp.int32, acc.shape, 1)
    o_ref[...] = jnp.where(col == d, top, acc)

    sums = acc[:, d + 1:d + 2]
    part = jnp.sum(top + jnp.log(sums)) - pos_ref[0:1, 0:1]
    loss_in[me] = jnp.broadcast_to(part, loss_ref.shape)

    def send_loss(k, carry):
        dst = lax.rem(me + k, g)
        pltpu.make_async_remote_copy(
            src_ref=loss_in.at[me], dst_ref=loss_in.at[me], send_sem=sems.at[6],
            recv_sem=sems.at[7], device_id=peer(dst), device_id_type=MESH,
        ).start()
        return carry

    lax.fori_loop(1, g, send_loss, 0)
    _wait_bytes(loss_in.at[pl.ds(0, g - 1)], loss_in.at[pl.ds(0, g - 1)], sems.at[6], sems.at[7],
                peer(lax.rem(me + 1, g)))

    def add(k, total):
        return total + loss_in[k]

    core_total = lax.fori_loop(0, g, add, jnp.zeros(loss_ref.shape, jnp.float32))
    loss_pair[c] = core_total
    to_pair_loss = pltpu.make_async_remote_copy(
        src_ref=loss_pair.at[c], dst_ref=loss_pair.at[c], send_sem=sems.at[8], recv_sem=sems.at[12],
        device_id=partner, device_id_type=MESH,
    )
    to_pair_loss.start()
    to_pair_loss.wait()
    loss_ref[...] = loss_pair[0] + loss_pair[1]
    queue_copy.wait()


def combine(pulled, stats, pos, queue_keys, d):
    g, rows = pulled.shape[1:3]
    width = d + stats.shape[3]
    return pl.pallas_call(
        functools.partial(combine_kernel, d),
        out_shape=(
            jax.ShapeDtypeStruct((rows, width), jnp.float32),
            jax.ShapeDtypeStruct((8, 128), jnp.float32),
            jax.ShapeDtypeStruct(queue_keys.shape, queue_keys.dtype),
        ),
        in_specs=[
            pl.BlockSpec(memory_space=pl.ANY),
            pl.BlockSpec(memory_space=pl.ANY),
            pl.BlockSpec(memory_space=pltpu.VMEM),
            pl.BlockSpec(memory_space=pl.ANY),
        ],
        out_specs=(
            pl.BlockSpec(memory_space=pltpu.VMEM),
            pl.BlockSpec(memory_space=pltpu.VMEM),
            pl.BlockSpec(memory_space=pl.ANY),
        ),
        scratch_shapes=[
            pltpu.VMEM((g, rows, d), jnp.float32),
            pltpu.VMEM((g, rows, width - d), jnp.float32),
            pltpu.VMEM((g, rows, d), jnp.float32),
            pltpu.VMEM((g, rows, width - d), jnp.float32),
            pltpu.VMEM((g, rows, width), jnp.float32),
            pltpu.VMEM((g, rows, width), jnp.float32),
            pltpu.VMEM((g, 8, 128), jnp.float32),
            pltpu.VMEM((2, 8, 128), jnp.float32),
            pltpu.SemaphoreType.DMA((13,)),
        ],
        compiler_params=pltpu.CompilerParams(collective_id=0, has_side_effects=True),
    )(pulled, stats, pos, queue_keys)


def shards(queue_keys, fresh_keys, slots, queries, positives):
    dp_size = lax.axis_size("dp")
    queue_size = lax.axis_size("queue")
    n = dp_size * queue_size
    d = queries.shape[1]
    pos_code = jnp.zeros((queries.shape[0], STAT), jnp.bfloat16)
    pos_code = pos_code.at[:, 0].set((positives // 32).astype(jnp.bfloat16))
    pos_code = pos_code.at[:, 1].set((positives % 32).astype(jnp.bfloat16))
    gathered = lax.all_gather(
        jnp.concatenate([queries, pos_code], axis=1), "dp", axis=0, tiled=True
    )
    total_rows = gathered.shape[0]
    own_rows = total_rows // n
    gathered = gathered.reshape(dp_size // 2, 2, total_rows // dp_size, d + STAT)
    gathered = gathered.transpose(1, 0, 2, 3).reshape(total_rows, d + STAT)
    all_queries = gathered[:, :d]
    pos_digits = gathered[:, d:d + 2].astype(jnp.int32)
    all_positives = pos_digits[:, 0] * 32 + pos_digits[:, 1]
    digits = jnp.stack([slots // 16384, (slots // 128) % 128, slots % 128], axis=1)
    code = jnp.zeros((slots.shape[0], STAT), jnp.bfloat16).at[:, :3].set(digits.astype(jnp.bfloat16))
    fresh_ext = lax.all_gather(
        jnp.concatenate([fresh_keys, code], axis=1), ("dp", "queue"), axis=0, tiled=True
    )
    fresh_all = fresh_ext[:, :d]
    got = fresh_ext[:, d:d + 3].astype(jnp.int32)
    slots_all = got[:, 0] * 16384 + got[:, 1] * 128 + got[:, 2]

    device_index = _device_index()
    queue_scores = score_rows(all_queries, queue_keys)
    fresh_scores = score_rows(all_queries, fresh_keys)
    local_top = jnp.maximum(jnp.max(queue_scores, axis=1), jnp.max(fresh_scores, axis=1))
    queue_exp = jnp.exp(queue_scores - local_top[:, None])
    fresh_exp = jnp.exp(fresh_scores - local_top[:, None])
    local_sum = jnp.sum(queue_exp, axis=1) + jnp.sum(fresh_exp, axis=1)
    local_pulled = jnp.dot(
        queue_exp.astype(jnp.bfloat16), queue_keys, preferred_element_type=jnp.float32
    ) + jnp.dot(fresh_exp.astype(jnp.bfloat16), fresh_keys, preferred_element_type=jnp.float32)
    fresh_ids = device_index * fresh_keys.shape[0] + jnp.arange(fresh_keys.shape[0], dtype=jnp.int32)
    is_positive = all_positives[:, None] == fresh_ids[None, :]
    positive_total = jnp.sum(jnp.where(is_positive, fresh_scores, 0.0))
    stats = jnp.zeros((total_rows, STAT), jnp.float32)
    stats = stats.at[:, 0].set(local_top).at[:, 1].set(local_sum)
    halves = (2, n // 2, own_rows)
    combined, loss_tile, queue_copy = combine(
        local_pulled.reshape(halves + (d,)),
        stats.reshape(halves + (STAT,)),
        jnp.full((8, 128), positive_total, jnp.float32),
        queue_keys,
        d,
    )
    sum_rows = combined[:, d + 1]
    pulled = combined[:, :d]
    queue_index = lax.axis_index("queue")
    local_start = queue_index * own_rows
    positive_rows = lax.dynamic_slice_in_dim(positives, local_start, own_rows, 0)
    positive_keys = jnp.take(fresh_all, positive_rows, axis=0).astype(jnp.float32)
    query_grad = pulled / sum_rows[:, None] - positive_keys
    mean_loss = loss_tile[0, 0] / total_rows
    held_rows = queue_keys.shape[0]
    local_slot = slots_all - device_index * held_rows
    inside = (local_slot >= 0) & (local_slot < held_rows)
    target = jnp.where(inside, local_slot, held_rows)
    new_queue = queue_copy.at[target].set(fresh_all, mode="drop")
    return (query_grad, mean_loss, new_queue)


def solution(mesh):
    placed = (
        P(("dp", "queue"), None),
        P(("dp", "queue"), None),
        P(("dp", "queue")),
        P("dp", None),
        P("dp"),
    )
    return jax.shard_map(
        shards,
        mesh=mesh,
        in_specs=placed,
        out_specs=(P(("dp", "queue"), None), P(), P(("dp", "queue"), None)),
        check_vma=False,
    )
```

time: 197 us -> 309 us (1.57)
  Pallas kernels: 57.4 us -> 193 us
  waiting for transfers between devices: 47.5 us -> 24.1 us
  other arithmetic: 18.7 us -> 22 us
    pallas_call x1, Pallas kernels: 57.4 us -> 193 us  [combine(): pl.pallas_call(functools.partial(combine_kernel, d), out_shape=(jax.Shape...]
    all_gather x1, waiting for transfers between devices: 23.2 us -> 0.01 us  [shards(): lax.all_gather(jnp.concatenate([fresh_keys, code], axis=1), ('dp', 'queue...]
    concatenate x1 -> x0, local copies, waits for them, and re-layouts: 5.04 us -> none  [shards(): jnp.concatenate([local_pulled, stats], axis=1)]
    scatter x2 -> x4, local copies, waits for them, and re-layouts: 12.5 us -> 12 us  [the longest x1 11.8 us: shards(): new_queue = queue_copy.at[target].set(fresh_all, mode='drop')]
    reduce_sum x2 -> x1, other arithmetic: 8.13 us -> 8.1 us  [shards(): local_sum = jnp.sum(queue_exp, axis=1) + jnp.sum(fresh_exp, axis=1)]
  transfers between devices with their start and end apart: 2 -> 2, of which waited for: 2 -> 1; matrix products, arithmetic and copies ran while one was open for 25% -> 15% of each run, Pallas kernels for 0% -> 63%
where the time goes in v3:
time: 309 us; the launch traced here: 308 us
  Pallas kernels  193 us (62%)
  local copies, waits for them, and re-layouts  27.5 us (9%)
  matrix products  25.3 us (8%)
  waiting for transfers between devices  24.1 us (8%)
  other arithmetic  22 us (7%)
  between operations  16 us (5%)
    pallas_call x1, Pallas kernels, combine(): pl.pallas_call(functools.partial(combine_kernel, d), out_shape=(jax.Shape...  193 us
    all_gather x1, waiting for transfers between devices, shards(): lax.all_gather(jnp.concatenate([queries, pos_code], axis=1), 'dp', axis=0...  24.1 us
    dot_general x1, matrix products, shards(): jnp.dot(queue_exp.astype(jnp.bfloat16), queue_keys, preferred_element_typ...  12.3 us
    scatter x1, local copies, waits for them, and re-layouts, shards(): new_queue = queue_copy.at[target].set(fresh_all, mode='drop')  11.8 us
    dot_general x2, matrix products, score_rows(): lax.dot_general(query_rows, key_rows, (((1,), (1,)), ((), ())), preferred...  10.7 us
    reduce_sum x1, other arithmetic, shards(): local_sum = jnp.sum(queue_exp, axis=1) + jnp.sum(fresh_exp, axis=1)  8.1 us
    unnamed x9, local copies, waits for them, and re-layouts  6.84 us
  transfers between devices with their start and end apart: 2, of which 1 were waited for; matrix products, arithmetic and copies ran while one was open for 15% of the time, Pallas kernels for 63%

profile of v3, /device:TPU:1, one launch (start us, length us, event | category | flops | bytes accessed | tf_op | source)
XLA Modules:
  0.0 308.0 jit_solution(3728443395698592760)
XLA Ops:
  7.9 0.7 compare_reduce_fusion.2
  8.6 2.0 fusion.20
  10.7 1.6 pad_maximum_fusion
  14.1 0.7 maximum_select_fusion
  14.8 1.3 fusion.18
  16.1 0.7 compare_and_fusion
  16.9 24.1 %all-gather.3.cloned.1.call-done = bf16[1024,896]{1,0:T(8,128)(2,1)} async-done(((bf16[128,896]{1,0:T(8,128)(2,1)}), bf16[1024,896]{1,0:T(8,128)(2,1)}) %all-gather.3.cloned.1.call-update) | async-done | bytes 1835024 | tf_op jit(solution)/shard_map/all_gather | solution.py:187
  41.0 1.8 copy.18
  43.4 0.9 copy-done.1
  44.3 10.2 %fusion.29 = (f32[1024]{0:T(1024)S(1)}, f32[1024,4096]{1,0:T(8,128)}) fusion(bf16[4096,768]{1,0:T(8,128)(2,1)S(1)} %copy-done.1, bf16[1024,896]{1,0:T(8,128)(2,1)S(1)} %bitcast.26), kind=kOutput, calls=%fused_computation.76 | convolution fusion | flops 6446644224 | bytes 24645632 | tf_op jit(solution)/shard_map/dot_general | solution.py:15
  54.9 0.7 broadcast_select_fusion
  55.6 0.7 select_reduce_fusion
  56.3 8.1 %fusion = f32[1024]{0:T(1024)S(1)} fusion(f32[1024,4096]{1,0:T(8,128)} %get-tuple-element.81, f32[1024]{0:T(1024)S(1)} %get-tuple-element.74), kind=kLoop, calls=%fused_computation.3 | loop fusion | flops 8387584 | bytes 16785408 | tf_op jit(solution)/shard_map/reduce_sum | solution.py:212
  65.4 1.0 copy.19
  66.4 12.3 %fusion.2 = f32[1024,768]{1,0:T(8,128)S(1)} fusion(bf16[4096,768]{1,0:T(8,128)(2,1)} %qk_ref.1, f32[1024,4096]{1,0:T(8,128)} %get-tuple-element.81, f32[1024]{0:T(1024)S(1)} %get-tuple-element.74), kind=kOutput, calls=%fused_computation.5 | convolution fusion | flops 6450839552 | bytes 26218496 | tf_op jit(solution)/shard_map/dot_general | solution.py:213
  78.7 2.3 convolution_add_fusion
  81.0 1.2 broadcast_in_dim.30.pos_ref
  82.2 193.1 %shard_map.76 = (f32[8,896]{1,0:T(8,128)}, f32[8,128]{1,0:T(8,128)}, bf16[4096,768]{1,0:T(8,128)(2,1)}) custom-call(f32[2,64,8,768]{3,2,1,0:T(8,128)} %bitcast.23, f32[2,64,8,128]{3,2,1,0:T(8,128)} %bitcast.27, f32[8,128]{1,0:T(8,128)} %broadcast_in_dim.30.pos_ref, bf16[4096,768]{1,0:T(8,128)(2,1)} %qk_ref.1), custom_call_target="tpu_custom_call" | custom-call | tf_op jit(solution)/shard_map/pallas_call | solution.py:146
  275.3 1.2 slice.117
  277.1 0.9 slice_reduce_fusion
  278.0 1.1 slice_convert_fusion
  279.7 11.8 %scatter_custom_fusion = bf16[4096,768]{1,0:T(8,128)(2,1)} fusion(bf16[4096,768]{1,0:T(8,128)(2,1)} %get-tuple-element.68, s32[1024]{0:T(1024)S(1)} %fusion.9, bf16[1024,896]{1,0:T(8,128)(2,1)S(1)} %copy-done), kind=kCustom, calls=%fused_computation.74 | custom fusion | bytes 7864320 | tf_op jit(solution)/shard_map/scatter | solution.py:241
  291.5 1.4 slice-done
  294.2 5.9 %copy.27 = bf16[4096,768]{1,0:T(8,128)(2,1)} copy(bf16[4096,768]{1,0:T(8,128)(2,1)} %scatter_custom_fusion) | data formatting | bytes 12582912
  (33 shorter events, 6.2 us)
Async XLA Ops:
  7.2 35.6 %copy-start.2 = (bf16[8,768]{1,0:T(8,128)(2,1)S(1)}, bf16[8,768]{1,0:T(8,128)(2,1)}, u32[]{:S(2)}) copy-start(bf16[8,768]{1,0:T(8,128)(2,1)} %param.16) | copy-start | bytes 36868
  7.2 33.8 %all-gather.3.cloned.1.call-start = ((), (), s32[]{:S(2)}) async-start(), calls=%async_computation | async-start | bytes 2064384 | tf_op jit(solution)/shard_map/all_gather | solution.py:187
  12.4 265.6 %all-gather.5.cloned.1.call-start = ((), (), s32[]{:S(2)}) async-start(), calls=%async_computation.1 | async-start | bytes 1849344 | tf_op jit(solution)/shard_map/all_gather | solution.py:199
  41.0 3.3 %copy-start.1 = (bf16[4096,768]{1,0:T(8,128)(2,1)S(1)}, bf16[4096,768]{1,0:T(8,128)(2,1)}, u32[]{:S(2)}) copy-start(bf16[4096,768]{1,0:T(8,128)(2,1)} %qk_ref.1) | copy-start | bytes 18874372
  278.0 1.7 copy-start
  291.5 1.4 slice-start
  291.5 2.0 copy-start.3
Sparse Core Ops, SparseCore 0:
  12.5 28.3 all-gather.2
  44.4 83.8 all-gather.4

commit v4 on v3

--- a/solution.py
+++ b/solution.py
@@ -30,7 +30,7 @@
     total.wait_recv()
 
 
-def combine_kernel(d, p_ref, s_ref, pos_ref, qk_ref, o_ref, loss_ref, nq_ref, own_p, own_s,
+def combine_kernel(d, p_ref, s_ref, pos_ref, o_ref, loss_ref, own_p, own_s,
                    pair_p, pair_s, merged, gathered, loss_in, loss_pair, sems):
     q = lax.axis_size("queue")
     g = p_ref.shape[1]
@@ -42,9 +42,6 @@
 
     def peer(k):
         return ((k // q) * 2 + c, lax.rem(k, q))
-
-    queue_copy = pltpu.make_async_copy(qk_ref, nq_ref, sems.at[9])
-    queue_copy.start()
 
     barrier = pltpu.get_barrier_semaphore()
     pl.semaphore_signal(barrier, inc=1, device_id=partner, device_id_type=MESH)
@@ -137,10 +134,9 @@
     to_pair_loss.start()
     to_pair_loss.wait()
     loss_ref[...] = loss_pair[0] + loss_pair[1]
-    queue_copy.wait()
-
-
-def combine(pulled, stats, pos, queue_keys, d):
+
+
+def combine(pulled, stats, pos, d):
     g, rows = pulled.shape[1:3]
     width = d + stats.shape[3]
     return pl.pallas_call(
@@ -148,18 +144,15 @@
         out_shape=(
             jax.ShapeDtypeStruct((rows, width), jnp.float32),
             jax.ShapeDtypeStruct((8, 128), jnp.float32),
-            jax.ShapeDtypeStruct(queue_keys.shape, queue_keys.dtype),
         ),
         in_specs=[
             pl.BlockSpec(memory_space=pl.ANY),
             pl.BlockSpec(memory_space=pl.ANY),
             pl.BlockSpec(memory_space=pltpu.VMEM),
-            pl.BlockSpec(memory_space=pl.ANY),
         ],
         out_specs=(
             pl.BlockSpec(memory_space=pltpu.VMEM),
             pl.BlockSpec(memory_space=pltpu.VMEM),
-            pl.BlockSpec(memory_space=pl.ANY),
         ),
         scratch_shapes=[
             pltpu.VMEM((g, rows, d), jnp.float32),
@@ -173,7 +166,7 @@
             pltpu.SemaphoreType.DMA((13,)),
         ],
         compiler_params=pltpu.CompilerParams(collective_id=0, has_side_effects=True),
-    )(pulled, stats, pos, queue_keys)
+    )(pulled, stats, pos)
 
 
 def shards(queue_keys, fresh_keys, slots, queries, positives):
@@ -219,11 +212,10 @@
     stats = jnp.zeros((total_rows, STAT), jnp.float32)
     stats = stats.at[:, 0].set(local_top).at[:, 1].set(local_sum)
     halves = (2, n // 2, own_rows)
-    combined, loss_tile, queue_copy = combine(
+    combined, loss_tile = combine(
         local_pulled.reshape(halves + (d,)),
         stats.reshape(halves + (STAT,)),
         jnp.full((8, 128), positive_total, jnp.float32),
-        queue_keys,
         d,
     )
     sum_rows = combined[:, d + 1]
@@ -238,7 +230,7 @@
     local_slot = slots_all - device_index * held_rows
     inside = (local_slot >= 0) & (local_slot < held_rows)
     target = jnp.where(inside, local_slot, held_rows)
-    new_queue = queue_copy.at[target].set(fresh_all, mode="drop")
+    new_queue = queue_keys.at[target].set(fresh_all, mode="drop")
     return (query_grad, mean_loss, new_queue)
 
 

time: 309 us -> 175 us (0.57)
  Pallas kernels: 193 us -> 60.9 us
  other arithmetic: 22 us -> 18.2 us
    pallas_call x1, Pallas kernels: 193 us -> 60.9 us  [combine(): pl.pallas_call(functools.partial(combine_kernel, d), out_shape=(jax.Shape...]
    unnamed x9 -> x15, local copies, waits for them, and re-layouts: 6.84 us -> 6.92 us
  transfers between devices with their start and end apart: 2 -> 2, of which waited for: 1 -> 1; matrix products, arithmetic and copies ran while one was open for 15% -> 26% of each run, Pallas kernels for 63% -> 35%
where the time goes in v4:
time: 175 us; the launch traced here: 174 us
  Pallas kernels  60.9 us (35%)
  local copies, waits for them, and re-layouts  27.6 us (16%)
  waiting for transfers between devices  26.1 us (15%)
  matrix products  25.3 us (14%)
  other arithmetic  18.2 us (10%)
  between operations  16.1 us (9%)
    pallas_call x1, Pallas kernels, combine(): pl.pallas_call(functools.partial(combine_kernel, d), out_shape=(jax.Shape...  60.9 us
    all_gather x1, waiting for transfers between devices, shards(): lax.all_gather(jnp.concatenate([queries, pos_code], axis=1), 'dp', axis=0...  26.1 us
    dot_general x1, matrix products, shards(): jnp.dot(queue_exp.astype(jnp.bfloat16), queue_keys, preferred_element_typ...  12.3 us
    scatter x1, local copies, waits for them, and re-layouts, shards(): new_queue = queue_keys.at[target].set(fresh_all, mode='drop')  11.8 us
    dot_general x2, matrix products, score_rows(): lax.dot_general(query_rows, key_rows, (((1,), (1,)), ((), ())), preferred...  10.7 us
    reduce_sum x1, other arithmetic, shards(): local_sum = jnp.sum(queue_exp, axis=1) + jnp.sum(fresh_exp, axis=1)  8.1 us
    unnamed x15, local copies, waits for them, and re-layouts  6.92 us
    another operation x7, other arithmetic  5.4 us
  transfers between devices with their start and end apart: 2, of which 1 were waited for; matrix products, arithmetic and copies ran while one was open for 26% of the time, Pallas kernels for 35%

profile of v4, /device:TPU:1, one launch (start us, length us, event | category | flops | bytes accessed | tf_op | source)
XLA Modules:
  0.0 174.3 jit_solution(193543643064044656)
XLA Ops:
  7.3 5.9 %copy.27 = bf16[4096,768]{1,0:T(8,128)(2,1)} copy(bf16[4096,768]{1,0:T(8,128)(2,1)} %param.15) | data formatting | bytes 12582912
  13.8 0.7 compare_reduce_fusion.2
  14.6 1.3 fusion.20
  16.1 0.7 pad_maximum_fusion
  17.8 0.7 maximum_select_fusion
  19.3 26.1 %all-gather.3.cloned.1.call-done = bf16[1024,896]{1,0:T(8,128)(2,1)} async-done(((bf16[128,896]{1,0:T(8,128)(2,1)}), bf16[1024,896]{1,0:T(8,128)(2,1)}) %all-gather.3.cloned.1.call-update) | async-done | bytes 1835024 | tf_op jit(solution)/shard_map/all_gather | solution.py:180
  45.4 1.8 %copy.18 = bf16[2,4,128,896]{3,2,1,0:T(8,128)(2,1)S(1)} copy(bf16[2,4,128,896]{3,2,0,1:T(8,128)(2,1)} %bitcast.28) | data formatting | bytes 3670016 | tf_op jit(solution)/shard_map/transpose | solution.py:186
  47.8 0.9 copy-done.1
  48.7 10.2 %fusion.29 = (f32[1024]{0:T(1024)S(1)}, f32[1024,4096]{1,0:T(8,128)}) fusion(bf16[4096,768]{1,0:T(8,128)(2,1)S(1)} %copy-done.1, bf16[1024,896]{1,0:T(8,128)(2,1)S(1)} %bitcast.26), kind=kOutput, calls=%fused_computation.76 | convolution fusion | flops 6446644224 | bytes 24645632 | tf_op jit(solution)/shard_map/dot_general | solution.py:15
  59.3 0.7 broadcast_select_fusion
  60.1 0.7 select_reduce_fusion
  60.7 8.1 %fusion = f32[1024]{0:T(1024)S(1)} fusion(f32[1024,4096]{1,0:T(8,128)} %get-tuple-element.79, f32[1024]{0:T(1024)S(1)} %get-tuple-element.72), kind=kLoop, calls=%fused_computation.3 | loop fusion | flops 8387584 | bytes 16785408 | tf_op jit(solution)/shard_map/reduce_sum | solution.py:205
  68.9 0.7 add_select_fusion
  69.8 1.0 copy.19
  70.8 12.3 %fusion.2 = f32[1024,768]{1,0:T(8,128)S(1)} fusion(bf16[4096,768]{1,0:T(8,128)(2,1)} %copy.27, f32[1024,4096]{1,0:T(8,128)} %get-tuple-element.79, f32[1024]{0:T(1024)S(1)} %get-tuple-element.72), kind=kOutput, calls=%fused_computation.5 | convolution fusion | flops 6450839552 | bytes 26218496 | tf_op jit(solution)/shard_map/dot_general | solution.py:206
  83.1 2.3 %convolution_add_fusion = f32[1024,768]{1,0:T(8,128)} fusion(f32[1024,768]{1,0:T(8,128)S(1)} %fusion.2, bf16[8,768]{1,0:T(8,128)(2,1)S(1)} %copy-done.3, f32[1024,8]{0,1:T(8,128)S(1)} %get-tuple-element.81, f32[1024]{0:T(1024)S(1)} %get-tuple-element.72), kind=kOutput, calls=%fused_computation.7 | convolution fusion | flops 13385728 | bytes 6340608 | tf_op jit(solution)/shard_map/dot_general | solution.py:208
  85.4 1.2 broadcast_in_dim.30.pos_ref
  86.6 60.9 %shard_map.76 = (f32[8,896]{1,0:T(8,128)}, f32[8,128]{1,0:T(8,128)}) custom-call(f32[2,64,8,768]{3,2,1,0:T(8,128)} %bitcast.23, f32[2,64,8,128]{3,2,1,0:T(8,128)} %bitcast.27, f32[8,128]{1,0:T(8,128)} %broadcast_in_dim.30.pos_ref), custom_call_target="tpu_custom_call" | custom-call | tf_op jit(solution)/shard_map/pallas_call | solution.py:142
  147.5 1.2 slice.117
  149.4 0.9 slice_reduce_fusion
  150.3 1.4 slice-done
  152.3 1.0 slice_convert_fusion
  153.8 0.7 convert_subtract_fusion
  154.5 11.8 %scatter_custom_fusion = bf16[4096,768]{1,0:T(8,128)(2,1)} fusion(bf16[4096,768]{1,0:T(8,128)(2,1)} %copy.27, s32[1024]{0:T(1024)S(1)} %fusion.9, bf16[1024,896]{1,0:T(8,128)(2,1)S(1)} %copy-done), kind=kCustom, calls=%fused_computation.74 | custom fusion | bytes 7864320 | tf_op jit(solution)/shard_map/scatter | solution.py:233
  (39 shorter events, 4.9 us)
Async XLA Ops:
  7.2 7.4 %copy-start.5 = (s32[128]{0:T(128)S(1)}, s32[128]{0:T(128)}, u32[]{:S(2)}) copy-start(s32[128]{0:T(128)} %param.19) | copy-start | bytes 1540
  7.2 8.9 %copy-start.2 = (bf16[128,768]{1,0:T(8,128)(2,1)S(1)}, bf16[128,768]{1,0:T(8,128)(2,1)}, u32[]{:S(2)}) copy-start(bf16[128,768]{1,0:T(8,128)(2,1)} %param.18) | copy-start | bytes 589828
  7.2 9.7 %copy-start.6 = (s32[8]{0:T(128)S(1)}, s32[8]{0:T(128)}, u32[]{:S(2)}) copy-start(s32[8]{0:T(128)} %param.17) | copy-start | bytes 100
  7.2 11.4 %copy-start.3 = (bf16[8,768]{1,0:T(8,128)(2,1)S(1)}, bf16[8,768]{1,0:T(8,128)(2,1)}, u32[]{:S(2)}) copy-start(bf16[8,768]{1,0:T(8,128)(2,1)} %param.16) | copy-start | bytes 36868
  7.2 38.2 %all-gather.3.cloned.1.call-start = ((), (), s32[]{:S(2)}) async-start(), calls=%async_computation | async-start | bytes 2064384 | tf_op jit(solution)/shard_map/all_gather | solution.py:180
  16.8 133.4 %all-gather.5.cloned.1.call-start = ((), (), s32[]{:S(2)}) async-start(), calls=%async_computation.1 | async-start | bytes 1849344 | tf_op jit(solution)/shard_map/all_gather | solution.py:192
  45.4 3.3 %copy-start.1 = (bf16[4096,768]{1,0:T(8,128)(2,1)S(1)}, bf16[4096,768]{1,0:T(8,128)(2,1)}, u32[]{:S(2)}) copy-start(bf16[4096,768]{1,0:T(8,128)(2,1)} %copy.27) | copy-start | bytes 18874372
  147.5 6.2 %copy-start.4 = (f32[8,896]{1,0:T(8,128)S(1)}, f32[8,896]{1,0:T(8,128)}, u32[]{:S(2)}) copy-start(f32[8,896]{1,0:T(8,128)} %get-tuple-element.65) | copy-start | bytes 86020
  150.3 1.4 slice-start
  150.3 4.2 %copy-start = (bf16[1024,896]{1,0:T(8,128)(2,1)S(1)}, bf16[1024,896]{1,0:T(8,128)(2,1)}, u32[]{:S(2)}) copy-start(bf16[1024,896]{1,0:T(8,128)(2,1)} %all-gather.5.cloned.1.call-done) | copy-start | bytes 5505028
Sparse Core Ops, SparseCore 0:
  16.9 28.3 all-gather.2
  48.8 83.9 all-gather.4

commit v5 on v4

--- a/solution.py
+++ b/solution.py
@@ -228,9 +228,10 @@
     mean_loss = loss_tile[0, 0] / total_rows
     held_rows = queue_keys.shape[0]
     local_slot = slots_all - device_index * held_rows
-    inside = (local_slot >= 0) & (local_slot < held_rows)
-    target = jnp.where(inside, local_slot, held_rows)
-    new_queue = queue_keys.at[target].set(fresh_all, mode="drop")
+    picks = jnp.arange(held_rows, dtype=jnp.int32)[:, None] == local_slot[None, :]
+    inserted = jnp.dot(picks.astype(jnp.bfloat16), fresh_all, preferred_element_type=jnp.float32)
+    replaced = jnp.any(picks, axis=1)
+    new_queue = jnp.where(replaced[:, None], inserted.astype(jnp.bfloat16), queue_keys)
     return (query_grad, mean_loss, new_queue)
 
 

time: 175 us -> 173 us (0.989)
  local copies, waits for them, and re-layouts: 27.6 us -> 8.94 us
  matrix products: 25.3 us -> 38.1 us
  other arithmetic: 18.2 us -> 24.6 us
  waiting for transfers between devices: 26.1 us -> 24.1 us
    scatter x1 -> x0, local copies, waits for them, and re-layouts: 11.8 us -> none  [shards(): new_queue = queue_keys.at[target].set(fresh_all, mode='drop')]
    dot_general x0 -> x1, matrix products: none -> 11.8 us  [shards(): jnp.dot(picks.astype(jnp.bfloat16), fresh_all, preferred_element_type=jnp...]
    unnamed x15 -> x4, local copies, waits for them, and re-layouts: 6.92 us -> 0.01 us
    all_gather x1, waiting for transfers between devices: 26.1 us -> 24.1 us  [shards(): lax.all_gather(jnp.concatenate([queries, pos_code], axis=1), 'dp', axis=0...]
    reduce_or x0 -> x1, other arithmetic: none -> 1.97 us  [shards(): replaced = jnp.any(picks, axis=1)]
  transfers between devices with their start and end apart: 2 -> 2, of which waited for: 1 -> 1; matrix products, arithmetic and copies ran while one was open for 26% -> 28% of each run, Pallas kernels for 35% -> 35%
where the time goes in v5:
time: 173 us
  Pallas kernels  61 us (35%)
  matrix products  38.1 us (22%)
  other arithmetic  24.6 us (14%)
  waiting for transfers between devices  24.1 us (14%)
  between operations  16 us (9%)
  local copies, waits for them, and re-layouts  8.94 us (5%)
    pallas_call x1, Pallas kernels, combine(): pl.pallas_call(functools.partial(combine_kernel, d), out_shape=(jax.Shape...  61 us
    all_gather x1, waiting for transfers between devices, shards(): lax.all_gather(jnp.concatenate([queries, pos_code], axis=1), 'dp', axis=0...  24.1 us
    dot_general x1, matrix products, shards(): jnp.dot(queue_exp.astype(jnp.bfloat16), queue_keys, preferred_element_typ...  12.3 us
    dot_general x2, matrix products, score_rows(): lax.dot_general(query_rows, key_rows, (((1,), (1,)), ((), ())), preferred...  11.8 us
    dot_general x1, matrix products, shards(): jnp.dot(picks.astype(jnp.bfloat16), fresh_all, preferred_element_type=jnp...  11.8 us
    reduce_sum x1, other arithmetic, shards(): local_sum = jnp.sum(queue_exp, axis=1) + jnp.sum(fresh_exp, axis=1)  8.1 us
    another operation x7, other arithmetic  6.06 us
  transfers between devices with their start and end apart: 2, of which 1 were waited for; matrix products, arithmetic and copies ran while one was open for 28% of the time, Pallas kernels for 35%

profile of v5, /device:TPU:1, one launch (start us, length us, event | category | flops | bytes accessed | tf_op | source)
XLA Modules:
  0.0 172.8 jit_solution(14074705125731111260)
XLA Ops:
  7.8 0.7 compare_reduce_fusion.2
  8.6 2.0 %fusion.24 = (bf16[128,1]{0,1:T(2,128)(2,1)S(1)}, bf16[128,1]{0,1:T(2,128)(2,1)S(1)}) fusion(pred[]{:T(512)} %compare_reduce_fusion.1, s32[128]{0:T(128)} %param.19, pred[]{:T(512)} %compare_reduce_fusion.2), kind=kLoop, calls=%fused_computation.67 | loop fusion | flops 2944 | bytes 1026 | tf_op jit(solution)/shard_map/reshape.160
  10.7 1.6 pad_maximum_fusion
  14.1 0.7 maximum_select_fusion
  14.8 1.3 fusion.22
  16.1 0.7 compare_and_fusion
  16.9 24.1 %all-gather.3.cloned.1.call-done = bf16[1024,896]{1,0:T(8,128)(2,1)} async-done(((bf16[128,896]{1,0:T(8,128)(2,1)}), bf16[1024,896]{1,0:T(8,128)(2,1)}) %all-gather.3.cloned.1.call-update) | async-done | bytes 1835024 | tf_op jit(solution)/shard_map/all_gather | solution.py:180
  41.0 1.8 %copy.24 = bf16[2,4,128,896]{3,2,1,0:T(8,128)(2,1)S(1)} copy(bf16[2,4,128,896]{3,2,0,1:T(8,128)(2,1)} %bitcast.28) | data formatting | bytes 3670016 | tf_op jit(solution)/shard_map/transpose | solution.py:186
  42.8 1.6 fusion.33
  44.4 10.2 %fusion.32 = (f32[1024]{0:T(1024)S(1)}, f32[1024,4096]{1,0:T(8,128)}) fusion(bf16[4096,768]{1,0:T(8,128)(2,1)S(1)} %copy-done.1, bf16[1024,896]{1,0:T(8,128)(2,1)S(1)} %bitcast.26), kind=kOutput, calls=%fused_computation.79 | convolution fusion | flops 6446644224 | bytes 24645632 | tf_op jit(solution)/shard_map/dot_general | solution.py:15
  55.0 0.7 broadcast_select_fusion.1
  56.4 8.1 %fusion.2 = f32[1024]{0:T(1024)S(1)} fusion(f32[1024,4096]{1,0:T(8,128)} %get-tuple-element.79, f32[1024]{0:T(1024)S(1)} %get-tuple-element.72), kind=kLoop, calls=%fused_computation.5 | loop fusion | flops 8387584 | bytes 16785408 | tf_op jit(solution)/shard_map/reduce_sum | solution.py:205
  65.5 1.0 copy.25
  66.5 12.3 %fusion.4 = f32[1024,768]{1,0:T(8,128)S(1)} fusion(bf16[4096,768]{1,0:T(8,128)(2,1)} %param.15, f32[1024,4096]{1,0:T(8,128)} %get-tuple-element.79, f32[1024]{0:T(1024)S(1)} %get-tuple-element.72), kind=kOutput, calls=%fused_computation.7 | convolution fusion | flops 6450839552 | bytes 26218496 | tf_op jit(solution)/shard_map/dot_general | solution.py:206
  78.8 2.3 %convolution_add_fusion = f32[1024,768]{1,0:T(8,128)} fusion(f32[1024,768]{1,0:T(8,128)S(1)} %fusion.4, bf16[8,768]{1,0:T(8,128)(2,1)S(1)} %copy-done, f32[1024,8]{0,1:T(8,128)S(1)} %get-tuple-element.81, f32[1024]{0:T(1024)S(1)} %get-tuple-element.72), kind=kOutput, calls=%fused_computation.12 | convolution fusion | flops 13385728 | bytes 6340608 | tf_op jit(solution)/shard_map/dot_general | solution.py:208
  81.1 1.2 broadcast_in_dim.38.pos_ref
  82.3 61.0 %shard_map.76 = (f32[8,896]{1,0:T(8,128)}, f32[8,128]{1,0:T(8,128)}) custom-call(f32[2,64,8,768]{3,2,1,0:T(8,128)} %bitcast.23, f32[2,64,8,128]{3,2,1,0:T(8,128)} %bitcast.27, f32[8,128]{1,0:T(8,128)} %broadcast_in_dim.38.pos_ref), custom_call_target="tpu_custom_call" | custom-call | tf_op jit(solution)/shard_map/pallas_call | solution.py:142
  143.3 1.2 slice.117
  145.2 0.9 slice_reduce_fusion
  146.0 1.0 slice_convert_fusion
  147.6 2.0 %fusion.1 = pred[4096]{0:T(1024)(128)(4,1)S(1)} fusion(s32[1024]{0:T(1024)S(1)} %fusion.14), kind=kLoop, calls=%fused_computation.3 | loop fusion | flops 8384512 | bytes 8192 | tf_op jit(solution)/shard_map/reduce_or | solution.py:233
  149.5 1.5 slice.128
  151.6 1.4 convert_subtract_fusion
  153.0 11.8 %broadcast_select_fusion = bf16[4096,768]{1,0:T(8,128)(2,1)} fusion(bf16[4096,768]{1,0:T(8,128)(2,1)} %param.15, pred[4096]{0:T(1024)(128)(4,1)S(1)} %fusion.1, s32[1024]{0:T(1024)S(1)} %fusion.14, bf16[1024,896]{1,0:T(8,128)(2,1)} %all-gather.5.cloned.1.call-done), kind=kOutput, calls=%fused_computation.11 | convolution fusion | flops 6452936704 | bytes 14163968 | tf_op jit(solution)/shard_map/dot_general | solution.py:232
  (28 shorter events, 5.7 us)
Async XLA Ops:
  7.2 33.8 %all-gather.3.cloned.1.call-start = ((), (), s32[]{:S(2)}) async-start(), calls=%async_computation | async-start | bytes 2064384 | tf_op jit(solution)/shard_map/all_gather | solution.py:180
  12.4 133.6 %all-gather.5.cloned.1.call-start = ((), (), s32[]{:S(2)}) async-start(), calls=%async_computation.1 | async-start | bytes 1849344 | tf_op jit(solution)/shard_map/all_gather | solution.py:192
  41.0 3.4 %copy-start.1 = (bf16[4096,768]{1,0:T(8,128)(2,1)S(1)}, bf16[4096,768]{1,0:T(8,128)(2,1)}, u32[]{:S(2)}) copy-start(bf16[4096,768]{1,0:T(8,128)(2,1)} %param.15) | copy-start | bytes 18874372
  66.5 12.3 %copy-start = (bf16[8,768]{1,0:T(8,128)(2,1)S(1)}, bf16[8,768]{1,0:T(8,128)(2,1)}, u32[]{:S(2)}) copy-start(bf16[8,768]{1,0:T(8,128)(2,1)} %param.16) | copy-start | bytes 36868
Sparse Core Ops, SparseCore 0:
  12.5 28.3 all-gather.2
  44.4 83.8 all-gather.4

commit v6 on v5

--- a/solution.py
+++ b/solution.py
@@ -28,6 +28,62 @@
     )
     total.wait_send()
     total.wait_recv()
+
+
+def gather_kernel(x_ref, o_ref, buf, sems):
+    dp = lax.axis_index("dp")
+    y, c = dp // 2, lax.rem(dp, 2)
+    ys = lax.axis_size("dp") // 2
+    qi = lax.axis_index("queue")
+    partner = (dp + 1 - 2 * c, qi)
+
+    def along(k):
+        return (lax.rem(y + k, ys) * 2 + c, qi)
+
+    barrier = pltpu.get_barrier_semaphore()
+    pl.semaphore_signal(barrier, inc=1, device_id=partner, device_id_type=MESH)
+    for k in range(1, ys):
+        pl.semaphore_signal(barrier, inc=1, device_id=along(k), device_id_type=MESH)
+    pl.semaphore_wait(barrier, ys)
+
+    mine = pltpu.make_async_copy(x_ref, buf.at[c, y], sems.at[4])
+    mine.start()
+    first = [
+        pltpu.make_async_remote_copy(
+            src_ref=x_ref, dst_ref=buf.at[c, y], send_sem=sems.at[0], recv_sem=sems.at[1],
+            device_id=dst, device_id_type=MESH,
+        )
+        for dst in [partner] + [along(k) for k in range(1, ys)]
+    ]
+    for copy in first:
+        copy.start()
+    _wait_bytes(buf.at[0], buf.at[0], sems.at[0], sems.at[1], partner)
+    mine.wait()
+    second = [
+        pltpu.make_async_remote_copy(
+            src_ref=buf.at[c, lax.rem(y + k, ys)], dst_ref=buf.at[c, lax.rem(y + k, ys)],
+            send_sem=sems.at[2], recv_sem=sems.at[3], device_id=partner, device_id_type=MESH,
+        )
+        for k in range(1, ys)
+    ]
+    for copy in second:
+        copy.start()
+    _wait_bytes(buf.at[0, pl.ds(0, ys - 1)], buf.at[0, pl.ds(0, ys - 1)], sems.at[2], sems.at[3], partner)
+    o_ref[...] = buf[...]
+
+
+def gather_dp(x, ys):
+    return pl.pallas_call(
+        gather_kernel,
+        out_shape=jax.ShapeDtypeStruct((2, ys) + x.shape, x.dtype),
+        in_specs=[pl.BlockSpec(memory_space=pltpu.VMEM)],
+        out_specs=pl.BlockSpec(memory_space=pltpu.VMEM),
+        scratch_shapes=[
+            pltpu.VMEM((2, ys) + x.shape, x.dtype),
+            pltpu.SemaphoreType.DMA((5,)),
+        ],
+        compiler_params=pltpu.CompilerParams(collective_id=1, has_side_effects=True),
+    )(x)
 
 
 def combine_kernel(d, p_ref, s_ref, pos_ref, o_ref, loss_ref, own_p, own_s,
@@ -177,13 +233,10 @@
     pos_code = jnp.zeros((queries.shape[0], STAT), jnp.bfloat16)
     pos_code = pos_code.at[:, 0].set((positives // 32).astype(jnp.bfloat16))
     pos_code = pos_code.at[:, 1].set((positives % 32).astype(jnp.bfloat16))
-    gathered = lax.all_gather(
-        jnp.concatenate([queries, pos_code], axis=1), "dp", axis=0, tiled=True
-    )
-    total_rows = gathered.shape[0]
+    gathered = gather_dp(jnp.concatenate([queries, pos_code], axis=1), dp_size // 2)
+    total_rows = dp_size * queries.shape[0]
     own_rows = total_rows // n
-    gathered = gathered.reshape(dp_size // 2, 2, total_rows // dp_size, d + STAT)
-    gathered = gathered.transpose(1, 0, 2, 3).reshape(total_rows, d + STAT)
+    gathered = gathered.reshape(total_rows, d + STAT)
     all_queries = gathered[:, :d]
     pos_digits = gathered[:, d:d + 2].astype(jnp.int32)
     all_positives = pos_digits[:, 0] * 32 + pos_digits[:, 1]

time: 173 us -> 171 us (0.988)
  waiting for transfers between devices: 24.1 us -> 0.03 us
  Pallas kernels: 61 us -> 81.1 us
  matrix products: 38.1 us -> 40.9 us
    all_gather x1 -> x0, waiting for transfers between devices: 24.1 us -> none  [shards(): lax.all_gather(jnp.concatenate([queries, pos_code], axis=1), 'dp', axis=0...]
    pallas_call x0 -> x1, Pallas kernels: none -> 20.5 us  [gather_dp(): pl.pallas_call(gather_kernel, out_shape=jax.ShapeDtypeStruct((2, ys) + x....]
    dot_general x2, matrix products: 11.8 us -> 14.5 us  [score_rows(): lax.dot_general(query_rows, key_rows, (((1,), (1,)), ((), ())), preferred...]
    transpose x1 -> x0, local copies, waits for them, and re-layouts: 1.8 us -> none  [shards(): gathered = gathered.transpose(1, 0, 2, 3).reshape(total_rows, d + STAT)]
  transfers between devices with their start and end apart: 2 -> 1, of which waited for: 1 -> 0; matrix products, arithmetic and copies ran while one was open for 28% -> 30% of each run, Pallas kernels for 35% -> 48%
where the time goes in v6:
time: 171 us; the launch traced here: 170 us
  Pallas kernels  81.1 us (47%)
  matrix products  40.9 us (24%)
  other arithmetic  23.5 us (14%)
  between operations  16 us (9%)
  local copies, waits for them, and re-layouts  8.55 us (5%)
    pallas_call x1, Pallas kernels, combine(): pl.pallas_call(functools.partial(combine_kernel, d), out_shape=(jax.Shape...  60.5 us
    pallas_call x1, Pallas kernels, gather_dp(): pl.pallas_call(gather_kernel, out_shape=jax.ShapeDtypeStruct((2, ys) + x....  20.5 us
    dot_general x2, matrix products, score_rows(): lax.dot_general(query_rows, key_rows, (((1,), (1,)), ((), ())), preferred...  14.5 us
    dot_general x1, matrix products, shards(): jnp.dot(queue_exp.astype(jnp.bfloat16), queue_keys, preferred_element_typ...  12.4 us
    dot_general x1, matrix products, shards(): jnp.dot(picks.astype(jnp.bfloat16), fresh_all, preferred_element_type=jnp...  11.8 us
    reduce_sum x1, other arithmetic, shards(): local_sum = jnp.sum(queue_exp, axis=1) + jnp.sum(fresh_exp, axis=1)  8.09 us
    another operation x7, other arithmetic  6.05 us
  transfers between devices with their start and end apart: 1, of which 0 were waited for; matrix products, arithmetic and copies ran while one was open for 30% of the time, Pallas kernels for 48%

profile of v6, /device:TPU:1, one launch (start us, length us, event | category | flops | bytes accessed | tf_op | source)
XLA Modules:
  0.0 170.1 jit_solution(4154574436438826595)
XLA Ops:
  8.8 0.7 maximum_select_fusion
  9.5 1.3 fusion.21
  11.5 0.7 compare_reduce_fusion.2
  12.2 2.0 %fusion.23 = (bf16[128,1]{0,1:T(2,128)(2,1)S(1)}, bf16[128,1]{0,1:T(2,128)(2,1)S(1)}) fusion(pred[]{:T(512)} %compare_reduce_fusion.1, s32[128]{0:T(128)} %param.19, pred[]{:T(512)} %compare_reduce_fusion.2), kind=kLoop, calls=%fused_computation.65 | loop fusion | flops 2944 | bytes 1026 | tf_op jit(solution)/shard_map/reshape.159
  14.7 1.6 pad_maximum_fusion.x_ref
  16.3 20.5 %shard_map.76 = bf16[2,4,128,896]{3,2,1,0:T(8,128)(2,1)} custom-call(bf16[128,896]{1,0:T(8,128)(2,1)} %pad_maximum_fusion.x_ref), custom_call_target="tpu_custom_call" | custom-call | tf_op jit(solution)/shard_map/pallas_call | solution.py:76
  36.9 1.9 %fusion.32 = (f32[1024]{0:T(1024)S(1)}, f32[1024,8]{0,1:T(8,128)S(1)}) fusion(bf16[8,768]{1,0:T(8,128)(2,1)} %param.16, bf16[1024,896]{1,0:T(8,128)(2,1)} %bitcast.22), kind=kOutput, calls=%fused_computation.78 | convolution fusion | flops 12590080 | bytes 1622016 | tf_op jit(solution)/shard_map/dot_general | solution.py:15
  38.8 1.0 slice.125
  39.8 12.6 %fusion.31 = (f32[1024]{0:T(1024)S(1)}, f32[1024,4096]{1,0:T(8,128)}) fusion(bf16[4096,768]{1,0:T(8,128)(2,1)} %param.15, bf16[1024,896]{1,0:T(8,128)(2,1)} %bitcast.24), kind=kOutput, calls=%fused_computation.77 | convolution fusion | flops 6446644224 | bytes 24645632 | tf_op jit(solution)/shard_map/dot_general | solution.py:15
  52.5 0.7 broadcast_select_fusion.1
  53.2 8.1 %fusion.2 = f32[1024]{0:T(1024)S(1)} fusion(f32[1024,4096]{1,0:T(8,128)} %get-tuple-element.79, f32[1024]{0:T(1024)S(1)} %get-tuple-element.72), kind=kLoop, calls=%fused_computation.5 | loop fusion | flops 8387584 | bytes 16785408 | tf_op jit(solution)/shard_map/reduce_sum | solution.py:258
  61.4 0.7 select_reduce_fusion
  63.1 1.0 copy.22
  64.1 12.4 %fusion.4 = f32[1024,768]{1,0:T(8,128)S(1)} fusion(bf16[4096,768]{1,0:T(8,128)(2,1)} %param.15, f32[1024,4096]{1,0:T(8,128)} %get-tuple-element.79, f32[1024]{0:T(1024)S(1)} %get-tuple-element.72), kind=kOutput, calls=%fused_computation.7 | convolution fusion | flops 6450839552 | bytes 26218496 | tf_op jit(solution)/shard_map/dot_general | solution.py:259
  76.4 2.3 %convolution_add_fusion = f32[1024,768]{1,0:T(8,128)} fusion(f32[1024,768]{1,0:T(8,128)S(1)} %fusion.4, bf16[8,768]{1,0:T(8,128)(2,1)S(1)} %copy-done, f32[1024,8]{0,1:T(8,128)S(1)} %get-tuple-element.81, f32[1024]{0:T(1024)S(1)} %get-tuple-element.72), kind=kOutput, calls=%fused_computation.12 | convolution fusion | flops 13385728 | bytes 6340608 | tf_op jit(solution)/shard_map/dot_general | solution.py:261
  78.8 1.2 broadcast_in_dim.38.pos_ref
  80.0 60.5 %shard_map.77 = (f32[8,896]{1,0:T(8,128)}, f32[8,128]{1,0:T(8,128)}) custom-call(f32[2,64,8,768]{3,2,1,0:T(8,128)} %bitcast.21, f32[2,64,8,128]{3,2,1,0:T(8,128)} %bitcast.25, f32[8,128]{1,0:T(8,128)} %broadcast_in_dim.38.pos_ref), custom_call_target="tpu_custom_call" | custom-call | tf_op jit(solution)/shard_map/pallas_call | solution.py:198
  140.5 1.2 slice.117
  142.4 0.9 slice_reduce_fusion
  143.3 1.0 slice_convert_fusion
  144.8 2.0 %fusion.1 = pred[4096]{0:T(1024)(128)(4,1)S(1)} fusion(s32[1024]{0:T(1024)S(1)} %fusion.14), kind=kLoop, calls=%fused_computation.3 | loop fusion | flops 8384512 | bytes 8192 | tf_op jit(solution)/shard_map/reduce_or | solution.py:286
  146.8 1.5 slice.128
  148.9 1.4 convert_subtract_fusion
  150.3 11.8 %broadcast_select_fusion = bf16[4096,768]{1,0:T(8,128)(2,1)} fusion(bf16[4096,768]{1,0:T(8,128)(2,1)} %param.15, pred[4096]{0:T(1024)(128)(4,1)S(1)} %fusion.1, s32[1024]{0:T(1024)S(1)} %fusion.14, bf16[1024,896]{1,0:T(8,128)(2,1)} %all-gather.2.cloned.1.call-done), kind=kOutput, calls=%fused_computation.11 | convolution fusion | flops 6452936704 | bytes 14163968 | tf_op jit(solution)/shard_map/dot_general | solution.py:285
  (28 shorter events, 5.1 us)
Async XLA Ops:
  7.2 136.2 %all-gather.2.cloned.1.call-start = ((), (), s32[]{:S(2)}) async-start(), calls=%async_computation | async-start | bytes 1849344 | tf_op jit(solution)/shard_map/all_gather | solution.py:245
  64.1 12.4 %copy-start = (bf16[8,768]{1,0:T(8,128)(2,1)S(1)}, bf16[8,768]{1,0:T(8,128)(2,1)}, u32[]{:S(2)}) copy-start(bf16[8,768]{1,0:T(8,128)(2,1)} %param.16) | copy-start | bytes 36868
  76.4 65.9 %copy-start.1 = (s32[128]{0:T(128)S(1)}, s32[128]{0:T(128)}, u32[]{:S(2)}) copy-start(s32[128]{0:T(128)} %param.19) | copy-start | bytes 1540
Sparse Core Ops, SparseCore 0:
  11.4 68.8 all-gather.1

commit v7 on v6

--- a/solution.py
+++ b/solution.py
@@ -86,28 +86,46 @@
     )(x)
 
 
-def combine_kernel(d, p_ref, s_ref, pos_ref, o_ref, loss_ref, own_p, own_s,
-                   pair_p, pair_s, merged, gathered, loss_in, loss_pair, sems):
-    q = lax.axis_size("queue")
+def _merge(blocks, at):
+    top = blocks[0][:, at:at + 1]
+    for b in blocks[1:]:
+        top = jnp.maximum(top, b[:, at:at + 1])
+    acc = blocks[0] * jnp.exp(blocks[0][:, at:at + 1] - top)
+    for b in blocks[1:]:
+        acc = acc + b * jnp.exp(b[:, at:at + 1] - top)
+    col = lax.broadcasted_iota(jnp.int32, acc.shape, 1)
+    return jnp.where(col == at, top, acc)
+
+
+TREES = (("x", "z", "y"), ("z", "y", "x"), ("y", "x", "z"))
+
+
+def combine_kernel(d, side, p_ref, s_ref, pos_ref, o_ref, loss_ref, own_p, own_s, pair_p, pair_s,
+                   send1, recv1, send2, recv2, send3, recv3, loss_buf, loss_pair, sems):
+    r = side
+    part = d // len(TREES)
     g = p_ref.shape[1]
     dp = lax.axis_index("dp")
     y, c = dp // 2, lax.rem(dp, 2)
     qi = lax.axis_index("queue")
-    me = y * q + qi
+    mine_at = {"y": y, "z": qi // r, "x": lax.rem(qi, r)}
     partner = (dp + 1 - 2 * c, qi)
 
-    def peer(k):
-        return ((k // q) * 2 + c, lax.rem(k, q))
+    def device(at):
+        return (at["y"] * 2 + c, at["z"] * r + at["x"])
+
+    def along(axis, j):
+        at = dict(mine_at)
+        at[axis] = j
+        return device(at)
 
     barrier = pltpu.get_barrier_semaphore()
     pl.semaphore_signal(barrier, inc=1, device_id=partner, device_id_type=MESH)
-
-    def greet(k, carry):
-        pl.semaphore_signal(barrier, inc=1, device_id=peer(lax.rem(me + k, g)), device_id_type=MESH)
-        return carry
-
-    lax.fori_loop(1, g, greet, 0)
-    pl.semaphore_wait(barrier, g)
+    for axis in ("x", "z", "y"):
+        for k in range(1, r):
+            pl.semaphore_signal(barrier, inc=1, device_id=along(axis, lax.rem(mine_at[axis] + k, r)),
+                                device_id_type=MESH)
+    pl.semaphore_wait(barrier, 1 + 3 * (r - 1))
 
     pair_copies = [
         pltpu.make_async_remote_copy(
@@ -118,7 +136,7 @@
     ]
     for copy in pair_copies:
         copy.start()
-    mine = [pltpu.make_async_copy(src.at[c], dst, sems.at[10 + i])
+    mine = [pltpu.make_async_copy(src.at[c], dst, sems.at[4 + i])
             for i, (src, dst) in enumerate(((p_ref, own_p), (s_ref, own_s)))]
     for copy in mine:
         copy.start()
@@ -129,62 +147,100 @@
         a, b = own_s[k], pair_s[k]
         top = jnp.maximum(a[:, 0:1], b[:, 0:1])
         wa, wb = jnp.exp(a[:, 0:1] - top), jnp.exp(b[:, 0:1] - top)
-        merged[k, :, :d] = own_p[k] * wa + pair_p[k] * wb
+        pulled = own_p[k] * wa + pair_p[k] * wb
         col = lax.broadcasted_iota(jnp.int32, a.shape, 1)
-        merged[k, :, d:] = jnp.where(col == 0, top, a * wa + b * wb)
+        stats = jnp.where(col == 0, top, a * wa + b * wb)
+        at = {"y": k // (r * r), "z": lax.rem(k // r, r), "x": lax.rem(k, r)}
+        for t, (a1, a2, a3) in enumerate(TREES):
+            slot = at[a2] * r + at[a3]
+            send1[t, at[a1], slot, :, :part] = pulled[:, t * part:(t + 1) * part]
+            send1[t, at[a1], slot, :, part:] = stats
         return carry
 
     lax.fori_loop(0, g, merge_pair, 0)
 
-    def send(k, carry):
-        dst = lax.rem(me + k, g)
-        pltpu.make_async_remote_copy(
-            src_ref=merged.at[dst], dst_ref=gathered.at[me], send_sem=sems.at[4],
-            recv_sem=sems.at[5], device_id=peer(dst), device_id_type=MESH,
-        ).start()
+    def level(lvl, send, recv, blocks):
+        sent = []
+        for t, axes in enumerate(TREES):
+            axis = axes[lvl]
+            me_a = mine_at[axis]
+            for k in range(1, r):
+                dst = lax.rem(me_a + k, r)
+                copy = pltpu.make_async_remote_copy(
+                    src_ref=send.at[t, pl.ds(dst * blocks, blocks)], dst_ref=recv.at[t, me_a],
+                    send_sem=sems.at[6 + 2 * (3 * lvl + t)], recv_sem=sems.at[7 + 2 * (3 * lvl + t)],
+                    device_id=along(axis, dst), device_id_type=MESH,
+                )
+                copy.start()
+            recv[t, me_a] = send[t, pl.ds(me_a * blocks, blocks)]
+            sent.append(axis)
+        for t, axis in enumerate(sent):
+            _wait_bytes(recv.at[t, pl.ds(0, r - 1)], recv.at[t, pl.ds(0, r - 1)],
+                        sems.at[6 + 2 * (3 * lvl + t)], sems.at[7 + 2 * (3 * lvl + t)],
+                        along(axis, lax.rem(mine_at[axis] + 1, r)))
+
+    def run_level1():
+        sent_axes = []
+        for t, axes in enumerate(TREES):
+            axis = axes[0]
+            me_a = mine_at[axis]
+            for k in range(1, r):
+                dst = lax.rem(me_a + k, r)
+                pltpu.make_async_remote_copy(
+                    src_ref=send1.at[t, dst], dst_ref=recv1.at[t, me_a],
+                    send_sem=sems.at[6 + 2 * t], recv_sem=sems.at[7 + 2 * t],
+                    device_id=along(axis, dst), device_id_type=MESH,
+                ).start()
+            recv1[t, me_a] = send1[t, me_a]
+            sent_axes.append(axis)
+        for t, axis in enumerate(sent_axes):
+            _wait_bytes(send1.at[t, pl.ds(0, r - 1)], recv1.at[t, pl.ds(0, r - 1)],
+                        sems.at[6 + 2 * t], sems.at[7 + 2 * t],
+                        along(axis, lax.rem(mine_at[axis] + 1, r)))
+
+    run_level1()
+
+    def merge1(b, carry):
+        for t in range(len(TREES)):
+            send2[t, b] = _merge([recv1[t, i, b] for i in range(r)], part)
         return carry
 
-    lax.fori_loop(1, g, send, 0)
-    gathered[me] = merged[me]
-    _wait_bytes(merged.at[pl.ds(0, g - 1)], gathered.at[pl.ds(0, g - 1)], sems.at[4], sems.at[5],
-                peer(lax.rem(me + 1, g)))
-
-    def top_of(k, m):
-        return jnp.maximum(m, gathered[k][:, d:d + 1])
-
-    top = lax.fori_loop(0, g, top_of, jnp.full((o_ref.shape[0], 1), -jnp.inf, jnp.float32))
-
-    def add_block(k, acc):
-        b = gathered[k]
-        return acc + b * jnp.exp(b[:, d:d + 1] - top)
-
-    acc = lax.fori_loop(0, g, add_block, jnp.zeros(o_ref.shape, jnp.float32))
-    col = lax.broadcasted_iota(jnp.int32, acc.shape, 1)
-    o_ref[...] = jnp.where(col == d, top, acc)
-
-    sums = acc[:, d + 1:d + 2]
-    part = jnp.sum(top + jnp.log(sums)) - pos_ref[0:1, 0:1]
-    loss_in[me] = jnp.broadcast_to(part, loss_ref.shape)
-
-    def send_loss(k, carry):
-        dst = lax.rem(me + k, g)
-        pltpu.make_async_remote_copy(
-            src_ref=loss_in.at[me], dst_ref=loss_in.at[me], send_sem=sems.at[6],
-            recv_sem=sems.at[7], device_id=peer(dst), device_id_type=MESH,
-        ).start()
-        return carry
-
-    lax.fori_loop(1, g, send_loss, 0)
-    _wait_bytes(loss_in.at[pl.ds(0, g - 1)], loss_in.at[pl.ds(0, g - 1)], sems.at[6], sems.at[7],
-                peer(lax.rem(me + 1, g)))
-
-    def add(k, total):
-        return total + loss_in[k]
-
-    core_total = lax.fori_loop(0, g, add, jnp.zeros(loss_ref.shape, jnp.float32))
-    loss_pair[c] = core_total
+    lax.fori_loop(0, r * r, merge1, 0)
+    level(1, send2, recv2, r)
+
+    for t in range(len(TREES)):
+        for a3 in range(r):
+            send3[t, a3] = _merge([recv2[t, i, a3] for i in range(r)], part)
+    level(2, send3, recv3, 1)
+
+    finals = [_merge([recv3[t, i, 0] for i in range(r)], part) for t in range(len(TREES))]
+    stats = finals[0][:, part:]
+    for t in range(len(TREES)):
+        o_ref[:, t * part:(t + 1) * part] = finals[t][:, :part]
+    o_ref[:, d:] = stats
+    top = stats[:, 0:1]
+    sums = stats[:, 1:2]
+
+    total = jnp.broadcast_to(jnp.sum(top + jnp.log(sums)) - pos_ref[0:1, 0:1], loss_ref.shape)
+    for n_axis, axis in enumerate(("x", "z", "y")):
+        me_a = mine_at[axis]
+        loss_buf[n_axis, me_a] = total
+        for k in range(1, r):
+            dst = lax.rem(me_a + k, r)
+            pltpu.make_async_remote_copy(
+                src_ref=loss_buf.at[n_axis, me_a], dst_ref=loss_buf.at[n_axis, me_a],
+                send_sem=sems.at[24 + 2 * n_axis], recv_sem=sems.at[25 + 2 * n_axis],
+                device_id=along(axis, dst), device_id_type=MESH,
+            ).start()
+        _wait_bytes(loss_buf.at[n_axis, pl.ds(0, r - 1)], loss_buf.at[n_axis, pl.ds(0, r - 1)],
+                    sems.at[24 + 2 * n_axis], sems.at[25 + 2 * n_axis],
+                    along(axis, lax.rem(me_a + 1, r)))
+        total = loss_buf[n_axis, 0]
+        for i in range(1, r):
+            total = total + loss_buf[n_axis, i]
+    loss_pair[c] = total
     to_pair_loss = pltpu.make_async_remote_copy(
-        src_ref=loss_pair.at[c], dst_ref=loss_pair.at[c], send_sem=sems.at[8], recv_sem=sems.at[12],
+        src_ref=loss_pair.at[c], dst_ref=loss_pair.at[c], send_sem=sems.at[30], recv_sem=sems.at[31],
         device_id=partner, device_id_type=MESH,
     )
     to_pair_loss.start()
@@ -192,11 +248,13 @@
     loss_ref[...] = loss_pair[0] + loss_pair[1]
 
 
-def combine(pulled, stats, pos, d):
+def combine(pulled, stats, pos, d, side):
     g, rows = pulled.shape[1:3]
     width = d + stats.shape[3]
+    trees = len(TREES)
+    block = (rows, d // trees + STAT)
     return pl.pallas_call(
-        functools.partial(combine_kernel, d),
+        functools.partial(combine_kernel, d, side),
         out_shape=(
             jax.ShapeDtypeStruct((rows, width), jnp.float32),
             jax.ShapeDtypeStruct((8, 128), jnp.float32),
@@ -215,11 +273,15 @@
             pltpu.VMEM((g, rows, width - d), jnp.float32),
             pltpu.VMEM((g, rows, d), jnp.float32),
             pltpu.VMEM((g, rows, width - d), jnp.float32),
-            pltpu.VMEM((g, rows, width), jnp.float32),
-            pltpu.VMEM((g, rows, width), jnp.float32),
-            pltpu.VMEM((g, 8, 128), jnp.float32),
+            pltpu.VMEM((trees, side, side * side) + block, jnp.float32),
+            pltpu.VMEM((trees, side, side * side) + block, jnp.float32),
+            pltpu.VMEM((trees, side * side) + block, jnp.float32),
+            pltpu.VMEM((trees, side, side) + block, jnp.float32),
+            pltpu.VMEM((trees, side) + block, jnp.float32),
+            pltpu.VMEM((trees, side, 1) + block, jnp.float32),
+            pltpu.VMEM((3, side, 8, 128), jnp.float32),
             pltpu.VMEM((2, 8, 128), jnp.float32),
-            pltpu.SemaphoreType.DMA((13,)),
+            pltpu.SemaphoreType.DMA((32,)),
         ],
         compiler_params=pltpu.CompilerParams(collective_id=0, has_side_effects=True),
     )(pulled, stats, pos)
@@ -229,6 +291,7 @@
     dp_size = lax.axis_size("dp")
     queue_size = lax.axis_size("queue")
     n = dp_size * queue_size
+    assert queue_size == (dp_size // 2) ** 2
     d = queries.shape[1]
     pos_code = jnp.zeros((queries.shape[0], STAT), jnp.bfloat16)
     pos_code = pos_code.at[:, 0].set((positives // 32).astype(jnp.bfloat16))
@@ -270,6 +333,7 @@
         stats.reshape(halves + (STAT,)),
         jnp.full((8, 128), positive_total, jnp.float32),
         d,
+        dp_size // 2,
     )
     sum_rows = combined[:, d + 1]
     pulled = combined[:, :d]

time: 171 us -> 159 us (0.930)
  Pallas kernels: 81.1 us -> 69.8 us
    pallas_call x1, Pallas kernels: 60.5 us -> 49.2 us  [combine(): pl.pallas_call(functools.partial(combine_kernel, d, side), out_shape=(jax...]
  transfers between devices with their start and end apart: 1 -> 1, of which waited for: 0 -> 0; matrix products, arithmetic and copies ran while one was open for 30% -> 32% of each run, Pallas kernels for 48% -> 44%
where the time goes in v7:
time: 159 us
  Pallas kernels  69.8 us (44%)
  matrix products  40.9 us (26%)
  other arithmetic  23.5 us (15%)
  between operations  16 us (10%)
  local copies, waits for them, and re-layouts  8.55 us (5%)
    pallas_call x1, Pallas kernels, combine(): pl.pallas_call(functools.partial(combine_kernel, d, side), out_shape=(jax...  49.2 us
    pallas_call x1, Pallas kernels, gather_dp(): pl.pallas_call(gather_kernel, out_shape=jax.ShapeDtypeStruct((2, ys) + x....  20.5 us
    dot_general x2, matrix products, score_rows(): lax.dot_general(query_rows, key_rows, (((1,), (1,)), ((), ())), preferred...  14.5 us
    dot_general x1, matrix products, shards(): jnp.dot(queue_exp.astype(jnp.bfloat16), queue_keys, preferred_element_typ...  12.4 us
    dot_general x1, matrix products, shards(): jnp.dot(picks.astype(jnp.bfloat16), fresh_all, preferred_element_type=jnp...  11.8 us
    reduce_sum x1, other arithmetic, shards(): local_sum = jnp.sum(queue_exp, axis=1) + jnp.sum(fresh_exp, axis=1)  8.09 us
    another operation x7, other arithmetic  6.05 us
  transfers between devices with their start and end apart: 1, of which 0 were waited for; matrix products, arithmetic and copies ran while one was open for 32% of the time, Pallas kernels for 44%

profile of v7, /device:TPU:1, one launch (start us, length us, event | category | flops | bytes accessed | tf_op | source)
XLA Modules:
  0.0 158.8 jit_solution(12628615550070775857)
XLA Ops:
  8.8 0.7 maximum_select_fusion
  9.5 1.3 fusion.21
  11.5 0.7 compare_reduce_fusion.2
  12.2 2.0 %fusion.23 = (bf16[128,1]{0,1:T(2,128)(2,1)S(1)}, bf16[128,1]{0,1:T(2,128)(2,1)S(1)}) fusion(pred[]{:T(512)} %compare_reduce_fusion.1, s32[128]{0:T(128)} %param.19, pred[]{:T(512)} %compare_reduce_fusion.2), kind=kLoop, calls=%fused_computation.65 | loop fusion | flops 2944 | bytes 1026 | tf_op jit(solution)/shard_map/reshape.159
  14.7 1.6 %pad_maximum_fusion.x_ref = bf16[128,896]{1,0:T(8,128)(2,1)} fusion(bf16[128,128]{1,0:T(8,128)(2,1)S(1)} %scatter.19, bf16[128,768]{1,0:T(8,128)(2,1)} %param.18), kind=kLoop, calls=%fused_computation.24 | loop fusion | flops 458752 | bytes 458752 | tf_op jit(solution)/shard_map/concatenate | solution.py:299
  16.3 20.5 %shard_map.76 = bf16[2,4,128,896]{3,2,1,0:T(8,128)(2,1)} custom-call(bf16[128,896]{1,0:T(8,128)(2,1)} %pad_maximum_fusion.x_ref), custom_call_target="tpu_custom_call" | custom-call | tf_op jit(solution)/shard_map/pallas_call | solution.py:76
  36.9 1.9 %fusion.32 = (f32[1024]{0:T(1024)S(1)}, f32[1024,8]{0,1:T(8,128)S(1)}) fusion(bf16[8,768]{1,0:T(8,128)(2,1)} %param.16, bf16[1024,896]{1,0:T(8,128)(2,1)} %bitcast.22), kind=kOutput, calls=%fused_computation.78 | convolution fusion | flops 12590080 | bytes 1622016 | tf_op jit(solution)/shard_map/dot_general | solution.py:15
  38.8 1.0 slice.125
  39.8 12.6 %fusion.31 = (f32[1024]{0:T(1024)S(1)}, f32[1024,4096]{1,0:T(8,128)}) fusion(bf16[4096,768]{1,0:T(8,128)(2,1)} %param.15, bf16[1024,896]{1,0:T(8,128)(2,1)} %bitcast.24), kind=kOutput, calls=%fused_computation.77 | convolution fusion | flops 6446644224 | bytes 24645632 | tf_op jit(solution)/shard_map/dot_general | solution.py:15
  52.5 0.7 broadcast_select_fusion.1
  53.2 8.1 %fusion.2 = f32[1024]{0:T(1024)S(1)} fusion(f32[1024,4096]{1,0:T(8,128)} %get-tuple-element.79, f32[1024]{0:T(1024)S(1)} %get-tuple-element.72), kind=kLoop, calls=%fused_computation.5 | loop fusion | flops 8387584 | bytes 16785408 | tf_op jit(solution)/shard_map/reduce_sum | solution.py:321
  61.4 0.7 select_reduce_fusion
  63.1 1.0 copy.22
  64.1 12.4 %fusion.4 = f32[1024,768]{1,0:T(8,128)S(1)} fusion(bf16[4096,768]{1,0:T(8,128)(2,1)} %param.15, f32[1024,4096]{1,0:T(8,128)} %get-tuple-element.79, f32[1024]{0:T(1024)S(1)} %get-tuple-element.72), kind=kOutput, calls=%fused_computation.7 | convolution fusion | flops 6450839552 | bytes 26218496 | tf_op jit(solution)/shard_map/dot_general | solution.py:322
  76.4 2.3 %convolution_add_fusion = f32[1024,768]{1,0:T(8,128)} fusion(f32[1024,768]{1,0:T(8,128)S(1)} %fusion.4, bf16[8,768]{1,0:T(8,128)(2,1)S(1)} %copy-done, f32[1024,8]{0,1:T(8,128)S(1)} %get-tuple-element.81, f32[1024]{0:T(1024)S(1)} %get-tuple-element.72), kind=kOutput, calls=%fused_computation.12 | convolution fusion | flops 13385728 | bytes 6340608 | tf_op jit(solution)/shard_map/dot_general | solution.py:324
  78.8 1.2 broadcast_in_dim.38.pos_ref
  80.0 49.2 %shard_map.77 = (f32[8,896]{1,0:T(8,128)}, f32[8,128]{1,0:T(8,128)}) custom-call(f32[2,64,8,768]{3,2,1,0:T(8,128)} %bitcast.21, f32[2,64,8,128]{3,2,1,0:T(8,128)} %bitcast.25, f32[8,128]{1,0:T(8,128)} %broadcast_in_dim.38.pos_ref), custom_call_target="tpu_custom_call" | custom-call | tf_op jit(solution)/shard_map/pallas_call | solution.py:256
  129.2 1.2 slice.117
  131.2 0.9 slice_reduce_fusion
  132.1 1.0 slice_convert_fusion
  133.6 2.0 %fusion.1 = pred[4096]{0:T(1024)(128)(4,1)S(1)} fusion(s32[1024]{0:T(1024)S(1)} %fusion.14), kind=kLoop, calls=%fused_computation.3 | loop fusion | flops 8384512 | bytes 8192 | tf_op jit(solution)/shard_map/reduce_or | solution.py:350
  135.5 1.5 slice.128
  137.6 1.4 convert_subtract_fusion
  139.1 11.8 %broadcast_select_fusion = bf16[4096,768]{1,0:T(8,128)(2,1)} fusion(bf16[4096,768]{1,0:T(8,128)(2,1)} %param.15, pred[4096]{0:T(1024)(128)(4,1)S(1)} %fusion.1, s32[1024]{0:T(1024)S(1)} %fusion.14, bf16[1024,896]{1,0:T(8,128)(2,1)} %all-gather.2.cloned.1.call-done), kind=kOutput, calls=%fused_computation.11 | convolution fusion | flops 6452936704 | bytes 14163968 | tf_op jit(solution)/shard_map/dot_general | solution.py:349
  (28 shorter events, 5.1 us)
Async XLA Ops:
  7.2 124.9 %all-gather.2.cloned.1.call-start = ((), (), s32[]{:S(2)}) async-start(), calls=%async_computation | async-start | bytes 1849344 | tf_op jit(solution)/shard_map/all_gather | solution.py:308
  64.1 12.4 %copy-start = (bf16[8,768]{1,0:T(8,128)(2,1)S(1)}, bf16[8,768]{1,0:T(8,128)(2,1)}, u32[]{:S(2)}) copy-start(bf16[8,768]{1,0:T(8,128)(2,1)} %param.16) | copy-start | bytes 36868
  76.4 54.6 %copy-start.1 = (s32[128]{0:T(128)S(1)}, s32[128]{0:T(128)}, u32[]{:S(2)}) copy-start(s32[128]{0:T(128)} %param.19) | copy-start | bytes 1540
Sparse Core Ops, SparseCore 0:
  11.4 68.8 all-gather.1

commit v8 on v7

--- a/solution.py
+++ b/solution.py
@@ -9,6 +9,7 @@
 
 MESH = pl.DeviceIdType.MESH
 STAT = 128
+FRESH_HELD = 8
 
 
 def score_rows(query_rows, key_rows):
@@ -28,6 +29,46 @@
     )
     total.wait_send()
     total.wait_recv()
+
+
+def partial_kernel(q_ref, k_ref, f_ref, p_ref, s_ref):
+    q = q_ref[...]
+    dims = (((1,), (1,)), ((), ()))
+    scores = lax.dot_general(q, k_ref[...], dims, preferred_element_type=jnp.float32)
+    fresh = lax.dot_general(q, f_ref[...], dims, preferred_element_type=jnp.float32)
+    held = lax.broadcasted_iota(jnp.int32, fresh.shape, 1) < FRESH_HELD
+    fresh = jnp.where(held, fresh, -jnp.inf)
+    top = jnp.maximum(jnp.max(scores, axis=1, keepdims=True), jnp.max(fresh, axis=1, keepdims=True))
+    weights = jnp.exp(scores - top)
+    fresh_weights = jnp.exp(fresh - top)
+    total = jnp.sum(weights, axis=1, keepdims=True) + jnp.sum(fresh_weights, axis=1, keepdims=True)
+    p_ref[...] = jnp.dot(
+        weights.astype(jnp.bfloat16), k_ref[...], preferred_element_type=jnp.float32
+    ) + jnp.dot(fresh_weights.astype(jnp.bfloat16), f_ref[...], preferred_element_type=jnp.float32)
+    col = lax.broadcasted_iota(jnp.int32, s_ref.shape, 1)
+    s_ref[...] = jnp.where(col == 0, top, jnp.where(col == 1, total, 0.0))
+
+
+def local_partials(queries, keys, fresh_padded, block):
+    rows, d = queries.shape
+    return pl.pallas_call(
+        partial_kernel,
+        grid=(rows // block,),
+        out_shape=(
+            jax.ShapeDtypeStruct((rows, d), jnp.float32),
+            jax.ShapeDtypeStruct((rows, STAT), jnp.float32),
+        ),
+        in_specs=[
+            pl.BlockSpec((block, d), lambda i: (i, 0)),
+            pl.BlockSpec(keys.shape, lambda i: (0, 0)),
+            pl.BlockSpec(fresh_padded.shape, lambda i: (0, 0)),
+        ],
+        out_specs=(
+            pl.BlockSpec((block, d), lambda i: (i, 0)),
+            pl.BlockSpec((block, STAT), lambda i: (i, 0)),
+        ),
+        compiler_params=pltpu.CompilerParams(vmem_limit_bytes=60 * 1024 * 1024),
+    )(queries, keys, fresh_padded)
 
 
 def gather_kernel(x_ref, o_ref, buf, sems):
@@ -291,6 +332,7 @@
     dp_size = lax.axis_size("dp")
     queue_size = lax.axis_size("queue")
     n = dp_size * queue_size
+    assert fresh_keys.shape[0] == FRESH_HELD
     assert queue_size == (dp_size // 2) ** 2
     d = queries.shape[1]
     pos_code = jnp.zeros((queries.shape[0], STAT), jnp.bfloat16)
@@ -313,20 +355,12 @@
     slots_all = got[:, 0] * 16384 + got[:, 1] * 128 + got[:, 2]
 
     device_index = _device_index()
-    queue_scores = score_rows(all_queries, queue_keys)
+    fresh_padded = jnp.zeros((STAT, d), fresh_keys.dtype).at[:fresh_keys.shape[0]].set(fresh_keys)
+    local_pulled, stats = local_partials(all_queries, queue_keys, fresh_padded, min(256, total_rows))
     fresh_scores = score_rows(all_queries, fresh_keys)
-    local_top = jnp.maximum(jnp.max(queue_scores, axis=1), jnp.max(fresh_scores, axis=1))
-    queue_exp = jnp.exp(queue_scores - local_top[:, None])
-    fresh_exp = jnp.exp(fresh_scores - local_top[:, None])
-    local_sum = jnp.sum(queue_exp, axis=1) + jnp.sum(fresh_exp, axis=1)
-    local_pulled = jnp.dot(
-        queue_exp.astype(jnp.bfloat16), queue_keys, preferred_element_type=jnp.float32
-    ) + jnp.dot(fresh_exp.astype(jnp.bfloat16), fresh_keys, preferred_element_type=jnp.float32)
     fresh_ids = device_index * fresh_keys.shape[0] + jnp.arange(fresh_keys.shape[0], dtype=jnp.int32)
     is_positive = all_positives[:, None] == fresh_ids[None, :]
     positive_total = jnp.sum(jnp.where(is_positive, fresh_scores, 0.0))
-    stats = jnp.zeros((total_rows, STAT), jnp.float32)
-    stats = stats.at[:, 0].set(local_top).at[:, 1].set(local_sum)
     halves = (2, n // 2, own_rows)
     combined, loss_tile = combine(
         local_pulled.reshape(halves + (d,)),

time: 159 us -> 156 us (0.981)
  Pallas kernels: 69.8 us -> 105 us
  matrix products: 40.9 us -> 12.5 us
  other arithmetic: 23.5 us -> 13 us
    pallas_call x0 -> x1, Pallas kernels: none -> 35.3 us  [local_partials(): pl.pallas_call(partial_kernel, grid=(rows // block,), out_shape=(jax.Shap...]
    dot_general x2 -> x0, matrix products: 14.7 us -> none  [the longest x1 12.4 us: shards(): jnp.dot(queue_exp.astype(jnp.bfloat16), queue_keys, preferred_element_typ...]
    dot_general x2 -> x1, matrix products: 14.5 us -> 1.12 us  [score_rows(): lax.dot_general(query_rows, key_rows, (((1,), (1,)), ((), ())), preferred...]
    reduce_sum x2 -> x0, other arithmetic: 8.78 us -> none  [the longest x1 8.09 us: shards(): local_sum = jnp.sum(queue_exp, axis=1) + jnp.sum(fresh_exp, axis=1)]
    slice x1, local copies, waits for them, and re-layouts: 0.97 us -> 2.69 us  [shards(): all_queries = gathered[:, :d]]
    another operation x7 -> x5, other arithmetic: 6.05 us -> 4.6 us
  transfers between devices with their start and end apart: 1 -> 1, of which waited for: 0 -> 0; matrix products, arithmetic and copies ran while one was open for 32% -> 9% of each run, Pallas kernels for 44% -> 68%
where the time goes in v8:
time: 156 us; the launch traced here: 155 us
  Pallas kernels  105 us (67%)
  between operations  16 us (10%)
  other arithmetic  13 us (8%)
  matrix products  12.5 us (8%)
  local copies, waits for them, and re-layouts  8.72 us (6%)
    pallas_call x1, Pallas kernels, combine(): pl.pallas_call(functools.partial(combine_kernel, d, side), out_shape=(jax...  49.1 us
    pallas_call x1, Pallas kernels, local_partials(): pl.pallas_call(partial_kernel, grid=(rows // block,), out_shape=(jax.Shap...  35.3 us
    pallas_call x1, Pallas kernels, gather_dp(): pl.pallas_call(gather_kernel, out_shape=jax.ShapeDtypeStruct((2, ys) + x....  20.6 us
    dot_general x1, matrix products, shards(): jnp.dot(picks.astype(jnp.bfloat16), fresh_all, preferred_element_type=jnp...  11.3 us
    another operation x5, other arithmetic  4.6 us
  transfers between devices with their start and end apart: 1, of which 0 were waited for; matrix products, arithmetic and copies ran while one was open for 9% of the time, Pallas kernels for 68%

profile of v8, /device:TPU:1, one launch (start us, length us, event | category | flops | bytes accessed | tf_op | source)
XLA Modules:
  0.0 155.2 jit_solution(7581400384183742988)
XLA Ops:
  7.2 0.6 compare_reduce_fusion
  7.8 0.7 convert_bitcast_fusion
  8.8 0.7 maximum_select_fusion
  9.5 1.3 fusion.10
  10.9 0.6 compare_reduce_fusion.2
  11.5 0.6 compare_reduce_fusion.1
  12.2 2.0 %fusion.12 = (bf16[128,1]{0,1:T(2,128)(2,1)S(1)}, bf16[128,1]{0,1:T(2,128)(2,1)S(1)}) fusion(pred[]{:T(512)} %compare_reduce_fusion.1, s32[128]{0:T(128)} %param.17, pred[]{:T(512)} %compare_reduce_fusion.2), kind=kLoop, calls=%fused_computation.52 | loop fusion | flops 2944 | bytes 1026 | tf_op jit(solution)/shard_map/reshape.128
  14.4 1.4 scatter.16.f_ref
  16.0 1.6 %pad_maximum_fusion.x_ref = bf16[128,896]{1,0:T(8,128)(2,1)} fusion(bf16[128,128]{1,0:T(8,128)(2,1)S(1)} %scatter.15, bf16[128,768]{1,0:T(8,128)(2,1)} %param.16), kind=kLoop, calls=%fused_computation.20 | loop fusion | flops 458752 | bytes 458752 | tf_op jit(solution)/shard_map/concatenate | solution.py:341
  17.6 20.6 %shard_map.76 = bf16[2,4,128,896]{3,2,1,0:T(8,128)(2,1)} custom-call(bf16[128,896]{1,0:T(8,128)(2,1)} %pad_maximum_fusion.x_ref), custom_call_target="tpu_custom_call" | custom-call | tf_op jit(solution)/shard_map/pallas_call | solution.py:117
  38.2 2.7 %slice.111.q_ref = bf16[1024,768]{1,0:T(8,128)(2,1)} slice(bf16[1024,896]{1,0:T(8,128)(2,1)} %bitcast.15), slice={[0:1024], [0:768]} | slice | bytes 3145728 | tf_op jit(solution)/shard_map/slice | solution.py:345
  40.9 35.3 %shard_map.77 = (f32[1024,768]{1,0:T(8,128)}, f32[1024,128]{1,0:T(8,128)}) custom-call(bf16[1024,768]{1,0:T(8,128)(2,1)} %slice.111.q_ref, bf16[4096,768]{1,0:T(8,128)(2,1)} %k_ref.1, bf16[128,768]{1,0:T(8,128)(2,1)} %scatter.16.f_ref), custom_call_target="tpu_custom_call" | custom-call | tf_op jit(solution)/shard_map/pallas_call | solution.py:54
  76.3 0.4 fusion.8
  76.6 1.1 fusion.4
  77.8 1.2 broadcast_in_dim.36.pos_ref
  79.0 49.1 %shard_map.78 = (f32[8,896]{1,0:T(8,128)}, f32[8,128]{1,0:T(8,128)}) custom-call(f32[2,64,8,768]{3,2,1,0:T(8,128)} %bitcast.18, f32[2,64,8,128]{3,2,1,0:T(8,128)} %bitcast.19, f32[8,128]{1,0:T(8,128)} %broadcast_in_dim.36.pos_ref), custom_call_target="tpu_custom_call" | custom-call | tf_op jit(solution)/shard_map/pallas_call | solution.py:297
  128.1 1.2 slice.104
  130.1 0.9 slice_reduce_fusion
  131.0 1.2 slice_convert_fusion
  132.1 0.5 fusion.6
  132.6 2.0 %fusion.1 = pred[4096]{0:T(1024)(128)(4,1)S(1)} fusion(s32[1024]{0:T(1024)S(1)} %fusion.6), kind=kLoop, calls=%fused_computation.3 | loop fusion | flops 8384512 | bytes 8192 | tf_op jit(solution)/shard_map/reduce_or | solution.py:384
  134.6 0.6 gather_fusion
  135.2 0.7 convert_subtract_fusion
  135.9 11.3 %broadcast_select_fusion = bf16[4096,768]{1,0:T(8,128)(2,1)} fusion(bf16[4096,768]{1,0:T(8,128)(2,1)} %k_ref.1, pred[4096]{0:T(1024)(128)(4,1)S(1)} %fusion.1, s32[1024]{0:T(1024)S(1)} %fusion.6, bf16[1024,896]{1,0:T(8,128)(2,1)S(1)} %copy-done.1), kind=kOutput, calls=%fused_computation.6 | convolution fusion | flops 6452936704 | bytes 14163968 | tf_op jit(solution)/shard_map/dot_general | solution.py:383
  (26 shorter events, 1.0 us)
Async XLA Ops:
  7.2 123.8 %all-gather.2.cloned.1.call-start = ((), (), s32[]{:S(2)}) async-start(), calls=%async_computation | async-start | bytes 1849344 | tf_op jit(solution)/shard_map/all_gather | solution.py:350
  40.9 35.3 %copy-start = (bf16[2,4,128,896]{3,2,1,0:T(8,128)(2,1)S(1)}, bf16[2,4,128,896]{3,2,1,0:T(8,128)(2,1)}, u32[]{:S(2)}) copy-start(bf16[2,4,128,896]{3,2,1,0:T(8,128)(2,1)} %shard_map.76) | copy-start | bytes 5505028
  40.9 35.7 %copy-start.2 = (bf16[8,768]{1,0:T(8,128)(2,1)S(1)}, bf16[8,768]{1,0:T(8,128)(2,1)}, u32[]{:S(2)}) copy-start(bf16[8,768]{1,0:T(8,128)(2,1)} %param.14) | copy-start | bytes 36868
  76.2 53.7 %copy-start.4 = (s32[128]{0:T(128)S(1)}, s32[128]{0:T(128)}, u32[]{:S(2)}) copy-start(s32[128]{0:T(128)} %param.17) | copy-start | bytes 1540
  128.1 7.1 %copy-start.3 = (f32[8,896]{1,0:T(8,128)S(1)}, f32[8,896]{1,0:T(8,128)}, u32[]{:S(2)}) copy-start(f32[8,896]{1,0:T(8,128)} %get-tuple-element.57) | copy-start | bytes 86020
  130.9 3.7 %slice-start = ((bf16[1024,896]{1,0:T(8,128)(2,1)}), bf16[1024,768]{1,0:T(8,128)(2,1)S(1)}, s32[]{:S(2)}) async-start(bf16[1024,896]{1,0:T(8,128)(2,1)} %all-gather.2.cloned.1.call-done), calls=%async_computation.1 | async-start | bytes 3145728 | tf_op jit(solution)/shard_map/slice | solution.py:353
  131.0 4.9 %copy-start.1 = (bf16[1024,896]{1,0:T(8,128)(2,1)S(1)}, bf16[1024,896]{1,0:T(8,128)(2,1)}, u32[]{:S(2)}) copy-start(bf16[1024,896]{1,0:T(8,128)(2,1)} %all-gather.2.cloned.1.call-done) | copy-start | bytes 5505028
Sparse Core Ops, SparseCore 0:
  11.4 69.0 all-gather.1

commit v9 on v8

--- a/solution.py
+++ b/solution.py
@@ -32,7 +32,7 @@
 
 
 def partial_kernel(q_ref, k_ref, f_ref, p_ref, s_ref):
-    q = q_ref[...]
+    q = q_ref[:, :k_ref.shape[1]]
     dims = (((1,), (1,)), ((), ()))
     scores = lax.dot_general(q, k_ref[...], dims, preferred_element_type=jnp.float32)
     fresh = lax.dot_general(q, f_ref[...], dims, preferred_element_type=jnp.float32)
@@ -50,7 +50,8 @@
 
 
 def local_partials(queries, keys, fresh_padded, block):
-    rows, d = queries.shape
+    rows, width = queries.shape
+    d = keys.shape[1]
     return pl.pallas_call(
         partial_kernel,
         grid=(rows // block,),
@@ -59,7 +60,7 @@
             jax.ShapeDtypeStruct((rows, STAT), jnp.float32),
         ),
         in_specs=[
-            pl.BlockSpec((block, d), lambda i: (i, 0)),
+            pl.BlockSpec((block, width), lambda i: (i, 0)),
             pl.BlockSpec(keys.shape, lambda i: (0, 0)),
             pl.BlockSpec(fresh_padded.shape, lambda i: (0, 0)),
         ],
@@ -356,7 +357,7 @@
 
     device_index = _device_index()
     fresh_padded = jnp.zeros((STAT, d), fresh_keys.dtype).at[:fresh_keys.shape[0]].set(fresh_keys)
-    local_pulled, stats = local_partials(all_queries, queue_keys, fresh_padded, min(256, total_rows))
+    local_pulled, stats = local_partials(gathered, queue_keys, fresh_padded, min(256, total_rows))
     fresh_scores = score_rows(all_queries, fresh_keys)
     fresh_ids = device_index * fresh_keys.shape[0] + jnp.arange(fresh_keys.shape[0], dtype=jnp.int32)
     is_positive = all_positives[:, None] == fresh_ids[None, :]

time: 156 us -> 153 us (0.981)
  local copies, waits for them, and re-layouts: 8.72 us -> 6.02 us
    slice x1 -> x0, local copies, waits for them, and re-layouts: 2.69 us -> none  [shards(): all_queries = gathered[:, :d]]
  transfers between devices with their start and end apart: 1 -> 1, of which waited for: 0 -> 0; matrix products, arithmetic and copies ran while one was open for 9% -> 8% of each run, Pallas kernels for 68% -> 69%
where the time goes in v9:
time: 153 us
  Pallas kernels  105 us (69%)
  between operations  16 us (10%)
  other arithmetic  13 us (8%)
  matrix products  12.5 us (8%)
  local copies, waits for them, and re-layouts  6.02 us (4%)
    pallas_call x1, Pallas kernels, combine(): pl.pallas_call(functools.partial(combine_kernel, d, side), out_shape=(jax...  49.1 us
    pallas_call x1, Pallas kernels, local_partials(): pl.pallas_call(partial_kernel, grid=(rows // block,), out_shape=(jax.Shap...  35.3 us
    pallas_call x1, Pallas kernels, gather_dp(): pl.pallas_call(gather_kernel, out_shape=jax.ShapeDtypeStruct((2, ys) + x....  20.6 us
    dot_general x1, matrix products, shards(): jnp.dot(picks.astype(jnp.bfloat16), fresh_all, preferred_element_type=jnp...  11.3 us
    another operation x5, other arithmetic  4.6 us
  transfers between devices with their start and end apart: 1, of which 0 were waited for; matrix products, arithmetic and copies ran while one was open for 8% of the time, Pallas kernels for 69%

profile of v9, /device:TPU:1, one launch (start us, length us, event | category | flops | bytes accessed | tf_op | source)
XLA Modules:
  0.0 152.5 jit_solution(17152045967749217174)
XLA Ops:
  7.2 0.6 compare_reduce_fusion
  7.8 0.7 convert_bitcast_fusion
  8.8 0.7 maximum_select_fusion
  9.5 1.3 fusion.17
  10.9 0.6 compare_reduce_fusion.2
  11.5 0.6 compare_reduce_fusion.1
  12.2 2.0 %fusion.19 = (bf16[128,1]{0,1:T(2,128)(2,1)S(1)}, bf16[128,1]{0,1:T(2,128)(2,1)S(1)}) fusion(pred[]{:T(512)} %compare_reduce_fusion.1, s32[128]{0:T(128)} %param.17, pred[]{:T(512)} %compare_reduce_fusion.2), kind=kLoop, calls=%fused_computation.54 | loop fusion | flops 2944 | bytes 1026 | tf_op jit(solution)/shard_map/reshape.128
  14.4 1.4 scatter.16.f_ref
  15.8 0.2 scatter.15
  16.0 1.6 %pad_maximum_fusion.x_ref = bf16[128,896]{1,0:T(8,128)(2,1)} fusion(bf16[128,128]{1,0:T(8,128)(2,1)S(1)} %scatter.15, bf16[128,768]{1,0:T(8,128)(2,1)} %param.16), kind=kLoop, calls=%fused_computation.22 | loop fusion | flops 458752 | bytes 458752 | tf_op jit(solution)/shard_map/concatenate | solution.py:342
  17.6 20.6 %shard_map.76 = bf16[2,4,128,896]{3,2,1,0:T(8,128)(2,1)} custom-call(bf16[128,896]{1,0:T(8,128)(2,1)} %pad_maximum_fusion.x_ref), custom_call_target="tpu_custom_call" | custom-call | tf_op jit(solution)/shard_map/pallas_call | solution.py:118
  38.2 35.3 %shard_map.77 = (f32[1024,768]{1,0:T(8,128)}, f32[1024,128]{1,0:T(8,128)}) custom-call(bf16[1024,896]{1,0:T(8,128)(2,1)} %bitcast.15, bf16[4096,768]{1,0:T(8,128)(2,1)} %k_ref.1, bf16[128,768]{1,0:T(8,128)(2,1)} %scatter.16.f_ref), custom_call_target="tpu_custom_call" | custom-call | tf_op jit(solution)/shard_map/pallas_call | solution.py:55
  73.6 0.4 fusion.15
  74.0 1.1 fusion.9
  75.1 1.2 broadcast_in_dim.36.pos_ref
  76.3 49.1 %shard_map.78 = (f32[8,896]{1,0:T(8,128)}, f32[8,128]{1,0:T(8,128)}) custom-call(f32[2,64,8,768]{3,2,1,0:T(8,128)} %bitcast.18, f32[2,64,8,128]{3,2,1,0:T(8,128)} %bitcast.19, f32[8,128]{1,0:T(8,128)} %broadcast_in_dim.36.pos_ref), custom_call_target="tpu_custom_call" | custom-call | tf_op jit(solution)/shard_map/pallas_call | solution.py:298
  125.5 1.2 slice.104
  127.4 0.9 slice_reduce_fusion
  128.3 1.2 slice_convert_fusion
  129.5 0.5 fusion.13
  130.0 2.0 %fusion.1 = pred[4096]{0:T(1024)(128)(4,1)S(1)} fusion(s32[1024]{0:T(1024)S(1)} %fusion.13), kind=kLoop, calls=%fused_computation.3 | loop fusion | flops 8384512 | bytes 8192 | tf_op jit(solution)/shard_map/reduce_or | solution.py:385
  132.0 0.6 gather_fusion
  132.5 0.7 convert_subtract_fusion
  133.2 11.3 %broadcast_select_fusion = bf16[4096,768]{1,0:T(8,128)(2,1)} fusion(bf16[4096,768]{1,0:T(8,128)(2,1)} %k_ref.1, pred[4096]{0:T(1024)(128)(4,1)S(1)} %fusion.1, s32[1024]{0:T(1024)S(1)} %fusion.13, bf16[1024,896]{1,0:T(8,128)(2,1)S(1)} %copy-done.1), kind=kOutput, calls=%fused_computation.6 | convolution fusion | flops 6452936704 | bytes 14163968 | tf_op jit(solution)/shard_map/dot_general | solution.py:384
  (25 shorter events, 0.8 us)
Async XLA Ops:
  7.2 121.1 %all-gather.2.cloned.1.call-start = ((), (), s32[]{:S(2)}) async-start(), calls=%async_computation | async-start | bytes 1849344 | tf_op jit(solution)/shard_map/all_gather | solution.py:351
  38.2 35.3 %copy-start = (bf16[2,4,128,896]{3,2,1,0:T(8,128)(2,1)S(1)}, bf16[2,4,128,896]{3,2,1,0:T(8,128)(2,1)}, u32[]{:S(2)}) copy-start(bf16[2,4,128,896]{3,2,1,0:T(8,128)(2,1)} %shard_map.76) | copy-start | bytes 5505028
  38.2 35.8 %copy-start.2 = (bf16[8,768]{1,0:T(8,128)(2,1)S(1)}, bf16[8,768]{1,0:T(8,128)(2,1)}, u32[]{:S(2)}) copy-start(bf16[8,768]{1,0:T(8,128)(2,1)} %param.14) | copy-start | bytes 36868
  73.6 53.7 %copy-start.4 = (s32[128]{0:T(128)S(1)}, s32[128]{0:T(128)}, u32[]{:S(2)}) copy-start(s32[128]{0:T(128)} %param.17) | copy-start | bytes 1540
  125.5 7.1 %copy-start.3 = (f32[8,896]{1,0:T(8,128)S(1)}, f32[8,896]{1,0:T(8,128)}, u32[]{:S(2)}) copy-start(f32[8,896]{1,0:T(8,128)} %get-tuple-element.57) | copy-start | bytes 86020
  128.3 3.7 %slice-start = ((bf16[1024,896]{1,0:T(8,128)(2,1)}), bf16[1024,768]{1,0:T(8,128)(2,1)S(1)}, s32[]{:S(2)}) async-start(bf16[1024,896]{1,0:T(8,128)(2,1)} %all-gather.2.cloned.1.call-done), calls=%async_computation.1 | async-start | bytes 3145728 | tf_op jit(solution)/shard_map/slice | solution.py:354
  128.3 4.9 %copy-start.1 = (bf16[1024,896]{1,0:T(8,128)(2,1)S(1)}, bf16[1024,896]{1,0:T(8,128)(2,1)}, u32[]{:S(2)}) copy-start(bf16[1024,896]{1,0:T(8,128)(2,1)} %all-gather.2.cloned.1.call-done) | copy-start | bytes 5505028
Sparse Core Ops, SparseCore 0:
  11.4 69.0 all-gather.1

commit v10 on v9

--- a/solution.py
+++ b/solution.py
@@ -142,8 +142,9 @@
 TREES = (("x", "z", "y"), ("z", "y", "x"), ("y", "x", "z"))
 
 
-def combine_kernel(d, side, p_ref, s_ref, pos_ref, o_ref, loss_ref, own_p, own_s, pair_p, pair_s,
-                   send1, recv1, send2, recv2, send3, recv3, loss_buf, loss_pair, sems):
+def combine_kernel(d, side, p_ref, s_ref, pos_ref, f_ref, o_ref, loss_ref, fresh_out, own_p, own_s,
+                   pair_p, pair_s, send1, recv1, send2, recv2, send3, recv3, loss_buf, loss_pair,
+                   fbuf, sems):
     r = side
     part = d // len(TREES)
     g = p_ref.shape[1]
@@ -168,6 +169,20 @@
             pl.semaphore_signal(barrier, inc=1, device_id=along(axis, lax.rem(mine_at[axis] + k, r)),
                                 device_id_type=MESH)
     pl.semaphore_wait(barrier, 1 + 3 * (r - 1))
+
+    yi, zi, xi = mine_at["y"], mine_at["z"], mine_at["x"]
+    own_fresh = pltpu.make_async_copy(f_ref, fbuf.at[yi, c, zi, xi], sems.at[40])
+    own_fresh.start()
+
+    def fresh_round(i, axis, src, dst_of):
+        for k in range(1, r):
+            dst = lax.rem(mine_at[axis] + k, r)
+            pltpu.make_async_remote_copy(
+                src_ref=src, dst_ref=dst_of(), send_sem=sems.at[32 + 2 * i], recv_sem=sems.at[33 + 2 * i],
+                device_id=along(axis, dst), device_id_type=MESH,
+            ).start()
+
+    fresh_round(0, "x", f_ref, lambda: fbuf.at[yi, c, zi, xi])
 
     pair_copies = [
         pltpu.make_async_remote_copy(
@@ -184,6 +199,10 @@
         copy.start()
     for copy in mine + pair_copies:
         copy.wait()
+    own_fresh.wait()
+    _wait_bytes(fbuf.at[0, 0, 0, pl.ds(0, r - 1)], fbuf.at[0, 0, 0, pl.ds(0, r - 1)],
+                sems.at[32], sems.at[33], along("x", lax.rem(xi + 1, r)))
+    fresh_round(1, "z", fbuf.at[yi, c, zi], lambda: fbuf.at[yi, c, zi])
 
     def merge_pair(k, carry):
         a, b = own_s[k], pair_s[k]
@@ -200,6 +219,9 @@
         return carry
 
     lax.fori_loop(0, g, merge_pair, 0)
+    _wait_bytes(fbuf.at[0, 0, pl.ds(0, r - 1)], fbuf.at[0, 0, pl.ds(0, r - 1)],
+                sems.at[34], sems.at[35], along("z", lax.rem(zi + 1, r)))
+    fresh_round(2, "y", fbuf.at[yi, c], lambda: fbuf.at[yi, c])
 
     def level(lvl, send, recv, blocks):
         sent = []
@@ -248,6 +270,13 @@
         return carry
 
     lax.fori_loop(0, r * r, merge1, 0)
+    _wait_bytes(fbuf.at[pl.ds(0, r - 1), 0], fbuf.at[pl.ds(0, r - 1), 0],
+                sems.at[36], sems.at[37], along("y", lax.rem(yi + 1, r)))
+    for j in range(r):
+        pltpu.make_async_remote_copy(
+            src_ref=fbuf.at[j, c], dst_ref=fbuf.at[j, c], send_sem=sems.at[38], recv_sem=sems.at[39],
+            device_id=partner, device_id_type=MESH,
+        ).start()
     level(1, send2, recv2, r)
 
     for t in range(len(TREES)):
@@ -288,9 +317,11 @@
     to_pair_loss.start()
     to_pair_loss.wait()
     loss_ref[...] = loss_pair[0] + loss_pair[1]
-
-
-def combine(pulled, stats, pos, d, side):
+    _wait_bytes(fbuf.at[:, 0], fbuf.at[:, 0], sems.at[38], sems.at[39], partner)
+    fresh_out[...] = fbuf[...]
+
+
+def combine(pulled, stats, pos, fresh, d, side):
     g, rows = pulled.shape[1:3]
     width = d + stats.shape[3]
     trees = len(TREES)
@@ -300,13 +331,16 @@
         out_shape=(
             jax.ShapeDtypeStruct((rows, width), jnp.float32),
             jax.ShapeDtypeStruct((8, 128), jnp.float32),
+            jax.ShapeDtypeStruct((side, 2, side, side) + fresh.shape, fresh.dtype),
         ),
         in_specs=[
             pl.BlockSpec(memory_space=pl.ANY),
             pl.BlockSpec(memory_space=pl.ANY),
             pl.BlockSpec(memory_space=pltpu.VMEM),
+            pl.BlockSpec(memory_space=pltpu.VMEM),
         ],
         out_specs=(
+            pl.BlockSpec(memory_space=pltpu.VMEM),
             pl.BlockSpec(memory_space=pltpu.VMEM),
             pl.BlockSpec(memory_space=pltpu.VMEM),
         ),
@@ -323,10 +357,11 @@
             pltpu.VMEM((trees, side, 1) + block, jnp.float32),
             pltpu.VMEM((3, side, 8, 128), jnp.float32),
             pltpu.VMEM((2, 8, 128), jnp.float32),
-            pltpu.SemaphoreType.DMA((32,)),
+            pltpu.VMEM((side, 2, side, side) + fresh.shape, fresh.dtype),
+            pltpu.SemaphoreType.DMA((41,)),
         ],
         compiler_params=pltpu.CompilerParams(collective_id=0, has_side_effects=True),
-    )(pulled, stats, pos)
+    )(pulled, stats, pos, fresh)
 
 
 def shards(queue_keys, fresh_keys, slots, queries, positives):
@@ -348,12 +383,7 @@
     all_positives = pos_digits[:, 0] * 32 + pos_digits[:, 1]
     digits = jnp.stack([slots // 16384, (slots // 128) % 128, slots % 128], axis=1)
     code = jnp.zeros((slots.shape[0], STAT), jnp.bfloat16).at[:, :3].set(digits.astype(jnp.bfloat16))
-    fresh_ext = lax.all_gather(
-        jnp.concatenate([fresh_keys, code], axis=1), ("dp", "queue"), axis=0, tiled=True
-    )
-    fresh_all = fresh_ext[:, :d]
-    got = fresh_ext[:, d:d + 3].astype(jnp.int32)
-    slots_all = got[:, 0] * 16384 + got[:, 1] * 128 + got[:, 2]
+    fresh_block = jnp.concatenate([fresh_keys, code], axis=1)
 
     device_index = _device_index()
     fresh_padded = jnp.zeros((STAT, d), fresh_keys.dtype).at[:fresh_keys.shape[0]].set(fresh_keys)
@@ -363,13 +393,18 @@
     is_positive = all_positives[:, None] == fresh_ids[None, :]
     positive_total = jnp.sum(jnp.where(is_positive, fresh_scores, 0.0))
     halves = (2, n // 2, own_rows)
-    combined, loss_tile = combine(
+    combined, loss_tile, fresh_ext = combine(
         local_pulled.reshape(halves + (d,)),
         stats.reshape(halves + (STAT,)),
         jnp.full((8, 128), positive_total, jnp.float32),
+        fresh_block,
         d,
         dp_size // 2,
     )
+    fresh_ext = fresh_ext.reshape(n * fresh_keys.shape[0], d + STAT)
+    fresh_all = fresh_ext[:, :d]
+    got = fresh_ext[:, d:d + 3].astype(jnp.int32)
+    slots_all = got[:, 0] * 16384 + got[:, 1] * 128 + got[:, 2]
     sum_rows = combined[:, d + 1]
     pulled = combined[:, :d]
     queue_index = lax.axis_index("queue")

time: 153 us -> 153 us (level)
  between operations: 16 us -> 2.53 us
  Pallas kernels: 105 us -> 116 us
    pallas_call x1, Pallas kernels: 49.1 us -> 59.9 us  [combine(): pl.pallas_call(functools.partial(combine_kernel, d, side), out_shape=(jax...]
  transfers between devices with their start and end apart: 1 -> 0, of which waited for: 0 -> 0; matrix products, arithmetic and copies ran while one was open for 8% -> 0% of each run, Pallas kernels for 69% -> 0%
where the time goes in v10:
time: 153 us
  Pallas kernels  116 us (76%)
  other arithmetic  14.5 us (9%)
  matrix products  13.9 us (9%)
  local copies, waits for them, and re-layouts  6.23 us (4%)
  between operations  2.53 us (2%)
    pallas_call x1, Pallas kernels, combine(): pl.pallas_call(functools.partial(combine_kernel, d, side), out_shape=(jax...  59.9 us
    pallas_call x1, Pallas kernels, local_partials(): pl.pallas_call(partial_kernel, grid=(rows // block,), out_shape=(jax.Shap...  35.2 us
    pallas_call x1, Pallas kernels, gather_dp(): pl.pallas_call(gather_kernel, out_shape=jax.ShapeDtypeStruct((2, ys) + x....  20.5 us
    dot_general x1, matrix products, shards(): jnp.dot(picks.astype(jnp.bfloat16), fresh_all, preferred_element_type=jnp...  11.3 us
    another operation x5, other arithmetic  4.6 us

profile of v10, /device:TPU:1, one launch (start us, length us, event | category | flops | bytes accessed | tf_op | source)
XLA Modules:
  0.0 152.7 jit_solution(9905063316803073481)
XLA Ops:
  0.6 0.6 compare_reduce_fusion.2
  1.3 0.6 compare_reduce_fusion.1
  1.9 0.6 compare_reduce_fusion
  2.6 2.0 %fusion.19 = (bf16[128,1]{0,1:T(2,128)(2,1)S(1)}, bf16[128,1]{0,1:T(2,128)(2,1)S(1)}) fusion(pred[]{:T(512)} %compare_reduce_fusion.1, s32[128]{0:T(128)} %param.17, pred[]{:T(512)} %compare_reduce_fusion.2), kind=kLoop, calls=%fused_computation.54 | loop fusion | flops 2944 | bytes 1026 | tf_op jit(solution)/shard_map/reshape.129
  4.5 0.7 compare_and_fusion
  5.3 0.7 convert_bitcast_fusion
  6.2 0.7 maximum_select_fusion
  7.0 1.3 fusion.17.f_ref
  8.7 1.6 %pad_maximum_fusion.x_ref = bf16[128,896]{1,0:T(8,128)(2,1)} fusion(bf16[128,128]{1,0:T(8,128)(2,1)S(1)} %scatter.15, bf16[128,768]{1,0:T(8,128)(2,1)} %param.16), kind=kLoop, calls=%fused_computation.22 | loop fusion | flops 458752 | bytes 458752 | tf_op jit(solution)/shard_map/concatenate | solution.py:377
  10.4 1.4 scatter.16.f_ref
  11.8 20.5 %shard_map.76 = bf16[2,4,128,896]{3,2,1,0:T(8,128)(2,1)} custom-call(bf16[128,896]{1,0:T(8,128)(2,1)} %pad_maximum_fusion.x_ref), custom_call_target="tpu_custom_call" | custom-call | tf_op jit(solution)/shard_map/pallas_call | solution.py:118
  32.2 1.0 slice_convert_fusion.1
  33.6 2.5 %fusion.9 = f32[]{:T(128)} fusion(bf16[8,768]{1,0:T(8,128)(2,1)S(1)} %copy-done.1, bf16[1024,896]{1,0:T(8,128)(2,1)} %bitcast.17, s32[1024]{0:T(1024)S(1)} %fusion.15, s32[8]{0:T(128)S(1)} %iota_add_fusion), kind=kOutput, calls=%fused_computation.10 | convolution fusion | flops 12607487 | bytes 1589284 | tf_op jit(solution)/shard_map/dot_general | solution.py:16
  36.2 1.2 broadcast_in_dim.36.pos_ref
  37.4 35.2 %shard_map.77 = (f32[1024,768]{1,0:T(8,128)}, f32[1024,128]{1,0:T(8,128)}) custom-call(bf16[1024,896]{1,0:T(8,128)(2,1)} %bitcast.18, bf16[4096,768]{1,0:T(8,128)(2,1)} %k_ref.1, bf16[128,768]{1,0:T(8,128)(2,1)} %scatter.16.f_ref), custom_call_target="tpu_custom_call" | custom-call | tf_op jit(solution)/shard_map/pallas_call | solution.py:55
  72.6 59.9 %shard_map.78 = (f32[8,896]{1,0:T(8,128)}, f32[8,128]{1,0:T(8,128)}, bf16[4,2,4,4,8,896]{5,4,3,2,1,0:T(8,128)(2,1)}) custom-call(f32[2,64,8,768]{3,2,1,0:T(8,128)} %bitcast.19, f32[2,64,8,128]{3,2,1,0:T(8,128)} %bitcast.23, f32[8,128]{1,0:T(8,128)} %broadcast_in_dim.36.pos_ref, bf16[8,896]{1,0:T(8,128)(2,1)} %fusion.17.f_ref), custom_call_target="tpu_custom_call" | custom-call | tf_op jit(solution)/shard_map/pallas_call | solution.py:329
  132.5 1.3 slice.104
  134.4 0.9 slice_reduce_fusion
  135.3 1.0 slice_convert_fusion
  136.3 0.5 fusion.13
  136.8 2.0 %fusion.1 = pred[4096]{0:T(1024)(128)(4,1)S(1)} fusion(s32[1024]{0:T(1024)S(1)} %fusion.13), kind=kLoop, calls=%fused_computation.3 | loop fusion | flops 8384512 | bytes 8192 | tf_op jit(solution)/shard_map/reduce_or | solution.py:420
  138.9 0.6 gather_fusion
  139.5 0.7 convert_subtract_fusion
  140.2 11.3 %broadcast_select_fusion = bf16[4096,768]{1,0:T(8,128)(2,1)} fusion(bf16[4096,768]{1,0:T(8,128)(2,1)} %k_ref.1, pred[4096]{0:T(1024)(128)(4,1)S(1)} %fusion.1, s32[1024]{0:T(1024)S(1)} %fusion.13, bf16[1024,896]{1,0:T(8,128)(2,1)S(1)} %bitcast.22), kind=kOutput, calls=%fused_computation.6 | convolution fusion | flops 6452936704 | bytes 14163968 | tf_op jit(solution)/shard_map/dot_general | solution.py:419
  (17 shorter events, 1.2 us)
Async XLA Ops:
  0.6 33.0 %copy-start.1 = (bf16[8,768]{1,0:T(8,128)(2,1)S(1)}, bf16[8,768]{1,0:T(8,128)(2,1)}, u32[]{:S(2)}) copy-start(bf16[8,768]{1,0:T(8,128)(2,1)} %param.14) | copy-start | bytes 36868
  132.4 6.3 %copy-start = (bf16[4,2,4,4,8,896]{5,4,3,2,1,0:T(8,128)(2,1)S(1)}, bf16[4,2,4,4,8,896]{5,4,3,2,1,0:T(8,128)(2,1)}, u32[]{:S(2)}) copy-start(bf16[4,2,4,4,8,896]{5,4,3,2,1,0:T(8,128)(2,1)} %get-tuple-element.59) | copy-start | bytes 5505028
  132.5 7.0 %copy-start.2 = (f32[8,896]{1,0:T(8,128)S(1)}, f32[8,896]{1,0:T(8,128)}, u32[]{:S(2)}) copy-start(f32[8,896]{1,0:T(8,128)} %get-tuple-element.58) | copy-start | bytes 86020

commit v11 on v10

--- a/solution.py
+++ b/solution.py
@@ -219,9 +219,6 @@
         return carry
 
     lax.fori_loop(0, g, merge_pair, 0)
-    _wait_bytes(fbuf.at[0, 0, pl.ds(0, r - 1)], fbuf.at[0, 0, pl.ds(0, r - 1)],
-                sems.at[34], sems.at[35], along("z", lax.rem(zi + 1, r)))
-    fresh_round(2, "y", fbuf.at[yi, c], lambda: fbuf.at[yi, c])
 
     def level(lvl, send, recv, blocks):
         sent = []
@@ -270,18 +267,14 @@
         return carry
 
     lax.fori_loop(0, r * r, merge1, 0)
-    _wait_bytes(fbuf.at[pl.ds(0, r - 1), 0], fbuf.at[pl.ds(0, r - 1), 0],
-                sems.at[36], sems.at[37], along("y", lax.rem(yi + 1, r)))
-    for j in range(r):
-        pltpu.make_async_remote_copy(
-            src_ref=fbuf.at[j, c], dst_ref=fbuf.at[j, c], send_sem=sems.at[38], recv_sem=sems.at[39],
-            device_id=partner, device_id_type=MESH,
-        ).start()
+    _wait_bytes(fbuf.at[0, 0, pl.ds(0, r - 1)], fbuf.at[0, 0, pl.ds(0, r - 1)],
+                sems.at[34], sems.at[35], along("z", lax.rem(zi + 1, r)))
     level(1, send2, recv2, r)
 
     for t in range(len(TREES)):
         for a3 in range(r):
             send3[t, a3] = _merge([recv2[t, i, a3] for i in range(r)], part)
+    fresh_round(2, "y", fbuf.at[yi, c], lambda: fbuf.at[yi, c])
     level(2, send3, recv3, 1)
 
     finals = [_merge([recv3[t, i, 0] for i in range(r)], part) for t in range(len(TREES))]
@@ -309,6 +302,13 @@
         total = loss_buf[n_axis, 0]
         for i in range(1, r):
             total = total + loss_buf[n_axis, i]
+    _wait_bytes(fbuf.at[pl.ds(0, r - 1), 0], fbuf.at[pl.ds(0, r - 1), 0],
+                sems.at[36], sems.at[37], along("y", lax.rem(yi + 1, r)))
+    for j in range(r):
+        pltpu.make_async_remote_copy(
+            src_ref=fbuf.at[j, c], dst_ref=fbuf.at[j, c], send_sem=sems.at[38], recv_sem=sems.at[39],
+            device_id=partner, device_id_type=MESH,
+        ).start()
     loss_pair[c] = total
     to_pair_loss = pltpu.make_async_remote_copy(
         src_ref=loss_pair.at[c], dst_ref=loss_pair.at[c], send_sem=sems.at[30], recv_sem=sems.at[31],

time: 153 us -> 153 us (level)
  no operation moved by 1% of the time
where the time goes in v11:
time: 153 us
  Pallas kernels  116 us (76%)
  other arithmetic  14.5 us (9%)
  matrix products  13.9 us (9%)
  local copies, waits for them, and re-layouts  6.23 us (4%)
  between operations  2.53 us (2%)
    pallas_call x1, Pallas kernels, combine(): pl.pallas_call(functools.partial(combine_kernel, d, side), out_shape=(jax...  60.1 us
    pallas_call x1, Pallas kernels, local_partials(): pl.pallas_call(partial_kernel, grid=(rows // block,), out_shape=(jax.Shap...  35.2 us
    pallas_call x1, Pallas kernels, gather_dp(): pl.pallas_call(gather_kernel, out_shape=jax.ShapeDtypeStruct((2, ys) + x....  20.5 us
    dot_general x1, matrix products, shards(): jnp.dot(picks.astype(jnp.bfloat16), fresh_all, preferred_element_type=jnp...  11.3 us
    another operation x5, other arithmetic  4.6 us

profile of v11, /device:TPU:1, one launch (start us, length us, event | category | flops | bytes accessed | tf_op | source)
XLA Modules:
  0.0 152.9 jit_solution(12102391127606727506)
XLA Ops:
  0.6 0.6 compare_reduce_fusion.2
  1.3 0.6 compare_reduce_fusion.1
  1.9 0.6 compare_reduce_fusion
  2.6 2.0 %fusion.19 = (bf16[128,1]{0,1:T(2,128)(2,1)S(1)}, bf16[128,1]{0,1:T(2,128)(2,1)S(1)}) fusion(pred[]{:T(512)} %compare_reduce_fusion.1, s32[128]{0:T(128)} %param.17, pred[]{:T(512)} %compare_reduce_fusion.2), kind=kLoop, calls=%fused_computation.54 | loop fusion | flops 2944 | bytes 1026 | tf_op jit(solution)/shard_map/reshape.129
  4.5 0.7 compare_and_fusion
  5.3 0.7 convert_bitcast_fusion
  6.2 0.7 maximum_select_fusion
  7.0 1.3 fusion.17.f_ref
  8.7 1.6 %pad_maximum_fusion.x_ref = bf16[128,896]{1,0:T(8,128)(2,1)} fusion(bf16[128,128]{1,0:T(8,128)(2,1)S(1)} %scatter.15, bf16[128,768]{1,0:T(8,128)(2,1)} %param.16), kind=kLoop, calls=%fused_computation.22 | loop fusion | flops 458752 | bytes 458752 | tf_op jit(solution)/shard_map/concatenate | solution.py:377
  10.4 1.4 scatter.16.f_ref
  11.8 20.5 %shard_map.76 = bf16[2,4,128,896]{3,2,1,0:T(8,128)(2,1)} custom-call(bf16[128,896]{1,0:T(8,128)(2,1)} %pad_maximum_fusion.x_ref), custom_call_target="tpu_custom_call" | custom-call | tf_op jit(solution)/shard_map/pallas_call | solution.py:118
  32.2 1.0 slice_convert_fusion.1
  33.6 2.5 %fusion.9 = f32[]{:T(128)} fusion(bf16[8,768]{1,0:T(8,128)(2,1)S(1)} %copy-done.1, bf16[1024,896]{1,0:T(8,128)(2,1)} %bitcast.17, s32[1024]{0:T(1024)S(1)} %fusion.15, s32[8]{0:T(128)S(1)} %iota_add_fusion), kind=kOutput, calls=%fused_computation.10 | convolution fusion | flops 12607487 | bytes 1589284 | tf_op jit(solution)/shard_map/dot_general | solution.py:16
  36.2 1.2 broadcast_in_dim.36.pos_ref
  37.4 35.2 %shard_map.77 = (f32[1024,768]{1,0:T(8,128)}, f32[1024,128]{1,0:T(8,128)}) custom-call(bf16[1024,896]{1,0:T(8,128)(2,1)} %bitcast.18, bf16[4096,768]{1,0:T(8,128)(2,1)} %k_ref.1, bf16[128,768]{1,0:T(8,128)(2,1)} %scatter.16.f_ref), custom_call_target="tpu_custom_call" | custom-call | tf_op jit(solution)/shard_map/pallas_call | solution.py:55
  72.6 60.1 %shard_map.78 = (f32[8,896]{1,0:T(8,128)}, f32[8,128]{1,0:T(8,128)}, bf16[4,2,4,4,8,896]{5,4,3,2,1,0:T(8,128)(2,1)}) custom-call(f32[2,64,8,768]{3,2,1,0:T(8,128)} %bitcast.19, f32[2,64,8,128]{3,2,1,0:T(8,128)} %bitcast.23, f32[8,128]{1,0:T(8,128)} %broadcast_in_dim.36.pos_ref, bf16[8,896]{1,0:T(8,128)(2,1)} %fusion.17.f_ref), custom_call_target="tpu_custom_call" | custom-call | tf_op jit(solution)/shard_map/pallas_call | solution.py:329
  132.7 1.3 slice.104
  134.7 0.9 slice_reduce_fusion
  135.5 1.0 slice_convert_fusion
  136.5 0.5 fusion.13
  137.0 2.0 %fusion.1 = pred[4096]{0:T(1024)(128)(4,1)S(1)} fusion(s32[1024]{0:T(1024)S(1)} %fusion.13), kind=kLoop, calls=%fused_computation.3 | loop fusion | flops 8384512 | bytes 8192 | tf_op jit(solution)/shard_map/reduce_or | solution.py:420
  139.1 0.6 gather_fusion
  139.7 0.7 convert_subtract_fusion
  140.4 11.3 %broadcast_select_fusion = bf16[4096,768]{1,0:T(8,128)(2,1)} fusion(bf16[4096,768]{1,0:T(8,128)(2,1)} %k_ref.1, pred[4096]{0:T(1024)(128)(4,1)S(1)} %fusion.1, s32[1024]{0:T(1024)S(1)} %fusion.13, bf16[1024,896]{1,0:T(8,128)(2,1)S(1)} %bitcast.22), kind=kOutput, calls=%fused_computation.6 | convolution fusion | flops 6452936704 | bytes 14163968 | tf_op jit(solution)/shard_map/dot_general | solution.py:419
  (17 shorter events, 1.2 us)
Async XLA Ops:
  0.6 33.0 %copy-start.1 = (bf16[8,768]{1,0:T(8,128)(2,1)S(1)}, bf16[8,768]{1,0:T(8,128)(2,1)}, u32[]{:S(2)}) copy-start(bf16[8,768]{1,0:T(8,128)(2,1)} %param.14) | copy-start | bytes 36868
  132.7 6.3 %copy-start = (bf16[4,2,4,4,8,896]{5,4,3,2,1,0:T(8,128)(2,1)S(1)}, bf16[4,2,4,4,8,896]{5,4,3,2,1,0:T(8,128)(2,1)}, u32[]{:S(2)}) copy-start(bf16[4,2,4,4,8,896]{5,4,3,2,1,0:T(8,128)(2,1)} %get-tuple-element.59) | copy-start | bytes 5505028
  132.7 7.0 %copy-start.2 = (f32[8,896]{1,0:T(8,128)S(1)}, f32[8,896]{1,0:T(8,128)}, u32[]{:S(2)}) copy-start(f32[8,896]{1,0:T(8,128)} %get-tuple-element.58) | copy-start | bytes 86020

commit v12 on v9

--- a/solution.py
+++ b/solution.py
@@ -10,6 +10,7 @@
 MESH = pl.DeviceIdType.MESH
 STAT = 128
 FRESH_HELD = 8
+KEY_CHUNK = 512
 
 
 def score_rows(query_rows, key_rows):
@@ -39,12 +40,18 @@
     held = lax.broadcasted_iota(jnp.int32, fresh.shape, 1) < FRESH_HELD
     fresh = jnp.where(held, fresh, -jnp.inf)
     top = jnp.maximum(jnp.max(scores, axis=1, keepdims=True), jnp.max(fresh, axis=1, keepdims=True))
-    weights = jnp.exp(scores - top)
     fresh_weights = jnp.exp(fresh - top)
-    total = jnp.sum(weights, axis=1, keepdims=True) + jnp.sum(fresh_weights, axis=1, keepdims=True)
-    p_ref[...] = jnp.dot(
-        weights.astype(jnp.bfloat16), k_ref[...], preferred_element_type=jnp.float32
-    ) + jnp.dot(fresh_weights.astype(jnp.bfloat16), f_ref[...], preferred_element_type=jnp.float32)
+    total = jnp.sum(fresh_weights, axis=1, keepdims=True)
+    acc = jnp.dot(fresh_weights.astype(jnp.bfloat16), f_ref[...], preferred_element_type=jnp.float32)
+    chunk = min(KEY_CHUNK, k_ref.shape[0])
+    for j in range(k_ref.shape[0] // chunk):
+        weights = jnp.exp(scores[:, j * chunk:(j + 1) * chunk] - top)
+        total = total + jnp.sum(weights, axis=1, keepdims=True)
+        acc = acc + jnp.dot(
+            weights.astype(jnp.bfloat16), k_ref[j * chunk:(j + 1) * chunk, :],
+            preferred_element_type=jnp.float32,
+        )
+    p_ref[...] = acc
     col = lax.broadcasted_iota(jnp.int32, s_ref.shape, 1)
     s_ref[...] = jnp.where(col == 0, top, jnp.where(col == 1, total, 0.0))
 

time: 153 us -> 144 us (0.941)
  Pallas kernels: 105 us -> 95.5 us
    pallas_call x1, Pallas kernels: 35.3 us -> 25.5 us  [local_partials(): pl.pallas_call(partial_kernel, grid=(rows // block,), out_shape=(jax.Shap...]
  transfers between devices with their start and end apart: 1 -> 1, of which waited for: 0 -> 0; matrix products, arithmetic and copies ran while one was open for 8% -> 8% of each run, Pallas kernels for 69% -> 67%
where the time goes in v12:
time: 144 us; the launch traced here: 143 us
  Pallas kernels  95.5 us (66%)
  between operations  16 us (11%)
  other arithmetic  13 us (9%)
  matrix products  12.5 us (9%)
  local copies, waits for them, and re-layouts  6.02 us (4%)
    pallas_call x1, Pallas kernels, combine(): pl.pallas_call(functools.partial(combine_kernel, d, side), out_shape=(jax...  49.5 us
    pallas_call x1, Pallas kernels, local_partials(): pl.pallas_call(partial_kernel, grid=(rows // block,), out_shape=(jax.Shap...  25.5 us
    pallas_call x1, Pallas kernels, gather_dp(): pl.pallas_call(gather_kernel, out_shape=jax.ShapeDtypeStruct((2, ys) + x....  20.6 us
    dot_general x1, matrix products, shards(): jnp.dot(picks.astype(jnp.bfloat16), fresh_all, preferred_element_type=jnp...  11.3 us
    another operation x5, other arithmetic  4.6 us
  transfers between devices with their start and end apart: 1, of which 0 were waited for; matrix products, arithmetic and copies ran while one was open for 8% of the time, Pallas kernels for 67%

profile of v12, /device:TPU:1, one launch (start us, length us, event | category | flops | bytes accessed | tf_op | source)
XLA Modules:
  0.0 143.1 jit_solution(11947275442099566712)
XLA Ops:
  7.2 0.6 compare_reduce_fusion
  7.8 0.7 convert_bitcast_fusion
  8.8 0.7 maximum_select_fusion
  9.5 1.3 fusion.17
  10.9 0.6 compare_reduce_fusion.2
  11.5 0.6 compare_reduce_fusion.1
  12.2 2.0 %fusion.19 = (bf16[128,1]{0,1:T(2,128)(2,1)S(1)}, bf16[128,1]{0,1:T(2,128)(2,1)S(1)}) fusion(pred[]{:T(512)} %compare_reduce_fusion.1, s32[128]{0:T(128)} %param.17, pred[]{:T(512)} %compare_reduce_fusion.2), kind=kLoop, calls=%fused_computation.54 | loop fusion | flops 2944 | bytes 1026 | tf_op jit(solution)/shard_map/reshape.128
  14.4 1.4 scatter.16.f_ref
  15.8 0.2 scatter.15
  16.0 1.6 %pad_maximum_fusion.x_ref = bf16[128,896]{1,0:T(8,128)(2,1)} fusion(bf16[128,128]{1,0:T(8,128)(2,1)S(1)} %scatter.15, bf16[128,768]{1,0:T(8,128)(2,1)} %param.16), kind=kLoop, calls=%fused_computation.22 | loop fusion | flops 458752 | bytes 458752 | tf_op jit(solution)/shard_map/concatenate | solution.py:349
  17.6 20.6 %shard_map.76 = bf16[2,4,128,896]{3,2,1,0:T(8,128)(2,1)} custom-call(bf16[128,896]{1,0:T(8,128)(2,1)} %pad_maximum_fusion.x_ref), custom_call_target="tpu_custom_call" | custom-call | tf_op jit(solution)/shard_map/pallas_call | solution.py:125
  38.2 25.5 %shard_map.77 = (f32[1024,768]{1,0:T(8,128)}, f32[1024,128]{1,0:T(8,128)}) custom-call(bf16[1024,896]{1,0:T(8,128)(2,1)} %bitcast.15, bf16[4096,768]{1,0:T(8,128)(2,1)} %k_ref.1, bf16[128,768]{1,0:T(8,128)(2,1)} %scatter.16.f_ref), custom_call_target="tpu_custom_call" | custom-call | tf_op jit(solution)/shard_map/pallas_call | solution.py:62
  63.8 0.4 fusion.15
  64.2 1.1 fusion.9
  65.3 1.2 broadcast_in_dim.36.pos_ref
  66.5 49.5 %shard_map.78 = (f32[8,896]{1,0:T(8,128)}, f32[8,128]{1,0:T(8,128)}) custom-call(f32[2,64,8,768]{3,2,1,0:T(8,128)} %bitcast.18, f32[2,64,8,128]{3,2,1,0:T(8,128)} %bitcast.19, f32[8,128]{1,0:T(8,128)} %broadcast_in_dim.36.pos_ref), custom_call_target="tpu_custom_call" | custom-call | tf_op jit(solution)/shard_map/pallas_call | solution.py:305
  116.0 1.2 slice.104
  117.9 0.9 slice_reduce_fusion
  118.8 1.2 slice_convert_fusion
  120.0 0.5 fusion.13
  120.5 2.0 %fusion.1 = pred[4096]{0:T(1024)(128)(4,1)S(1)} fusion(s32[1024]{0:T(1024)S(1)} %fusion.13), kind=kLoop, calls=%fused_computation.3 | loop fusion | flops 8384512 | bytes 8192 | tf_op jit(solution)/shard_map/reduce_or | solution.py:392
  122.5 0.6 gather_fusion
  123.1 0.7 convert_subtract_fusion
  123.8 11.3 %broadcast_select_fusion = bf16[4096,768]{1,0:T(8,128)(2,1)} fusion(bf16[4096,768]{1,0:T(8,128)(2,1)} %k_ref.1, pred[4096]{0:T(1024)(128)(4,1)S(1)} %fusion.1, s32[1024]{0:T(1024)S(1)} %fusion.13, bf16[1024,896]{1,0:T(8,128)(2,1)S(1)} %copy-done.1), kind=kOutput, calls=%fused_computation.6 | convolution fusion | flops 6452936704 | bytes 14163968 | tf_op jit(solution)/shard_map/dot_general | solution.py:391
  (25 shorter events, 0.8 us)
Async XLA Ops:
  7.2 111.6 %all-gather.2.cloned.1.call-start = ((), (), s32[]{:S(2)}) async-start(), calls=%async_computation | async-start | bytes 1849344 | tf_op jit(solution)/shard_map/all_gather | solution.py:358
  38.2 25.5 %copy-start = (bf16[2,4,128,896]{3,2,1,0:T(8,128)(2,1)S(1)}, bf16[2,4,128,896]{3,2,1,0:T(8,128)(2,1)}, u32[]{:S(2)}) copy-start(bf16[2,4,128,896]{3,2,1,0:T(8,128)(2,1)} %shard_map.76) | copy-start | bytes 5505028
  38.2 26.0 %copy-start.2 = (bf16[8,768]{1,0:T(8,128)(2,1)S(1)}, bf16[8,768]{1,0:T(8,128)(2,1)}, u32[]{:S(2)}) copy-start(bf16[8,768]{1,0:T(8,128)(2,1)} %param.14) | copy-start | bytes 36868
  63.8 54.1 %copy-start.4 = (s32[128]{0:T(128)S(1)}, s32[128]{0:T(128)}, u32[]{:S(2)}) copy-start(s32[128]{0:T(128)} %param.17) | copy-start | bytes 1540
  116.0 7.1 %copy-start.3 = (f32[8,896]{1,0:T(8,128)S(1)}, f32[8,896]{1,0:T(8,128)}, u32[]{:S(2)}) copy-start(f32[8,896]{1,0:T(8,128)} %get-tuple-element.57) | copy-start | bytes 86020
  118.8 3.7 %slice-start = ((bf16[1024,896]{1,0:T(8,128)(2,1)}), bf16[1024,768]{1,0:T(8,128)(2,1)S(1)}, s32[]{:S(2)}) async-start(bf16[1024,896]{1,0:T(8,128)(2,1)} %all-gather.2.cloned.1.call-done), calls=%async_computation.1 | async-start | bytes 3145728 | tf_op jit(solution)/shard_map/slice | solution.py:361
  118.8 4.9 %copy-start.1 = (bf16[1024,896]{1,0:T(8,128)(2,1)S(1)}, bf16[1024,896]{1,0:T(8,128)(2,1)}, u32[]{:S(2)}) copy-start(bf16[1024,896]{1,0:T(8,128)(2,1)} %all-gather.2.cloned.1.call-done) | copy-start | bytes 5505028
Sparse Core Ops, SparseCore 0:
  11.4 69.0 all-gather.1

commit v13 on v12

--- a/solution.py
+++ b/solution.py
@@ -364,7 +364,7 @@
 
     device_index = _device_index()
     fresh_padded = jnp.zeros((STAT, d), fresh_keys.dtype).at[:fresh_keys.shape[0]].set(fresh_keys)
-    local_pulled, stats = local_partials(gathered, queue_keys, fresh_padded, min(256, total_rows))
+    local_pulled, stats = local_partials(gathered, queue_keys, fresh_padded, min(512, total_rows))
     fresh_scores = score_rows(all_queries, fresh_keys)
     fresh_ids = device_index * fresh_keys.shape[0] + jnp.arange(fresh_keys.shape[0], dtype=jnp.int32)
     is_positive = all_positives[:, None] == fresh_ids[None, :]

time: 144 us -> 143 us (level)
  no operation moved by 1% of the time
where the time goes in v13:
time: 143 us
  Pallas kernels  95.2 us (67%)
  between operations  16 us (11%)
  other arithmetic  13 us (9%)
  matrix products  12.5 us (9%)
  local copies, waits for them, and re-layouts  6.02 us (4%)
    pallas_call x1, Pallas kernels, combine(): pl.pallas_call(functools.partial(combine_kernel, d, side), out_shape=(jax...  49.4 us
    pallas_call x1, Pallas kernels, local_partials(): pl.pallas_call(partial_kernel, grid=(rows // block,), out_shape=(jax.Shap...  25.2 us
    pallas_call x1, Pallas kernels, gather_dp(): pl.pallas_call(gather_kernel, out_shape=jax.ShapeDtypeStruct((2, ys) + x....  20.6 us
    dot_general x1, matrix products, shards(): jnp.dot(picks.astype(jnp.bfloat16), fresh_all, preferred_element_type=jnp...  11.3 us
    another operation x5, other arithmetic  4.6 us
  transfers between devices with their start and end apart: 1, of which 0 were waited for; matrix products, arithmetic and copies ran while one was open for 8% of the time, Pallas kernels for 67%

profile of v13, /device:TPU:1, one launch (start us, length us, event | category | flops | bytes accessed | tf_op | source)
XLA Modules:
  0.0 142.7 jit_solution(14620823630403250798)
XLA Ops:
  7.2 0.6 compare_reduce_fusion
  7.8 0.7 convert_bitcast_fusion
  8.8 0.7 maximum_select_fusion
  9.5 1.3 fusion.17
  10.9 0.6 compare_reduce_fusion.2
  11.5 0.6 compare_reduce_fusion.1
  12.2 2.0 %fusion.19 = (bf16[128,1]{0,1:T(2,128)(2,1)S(1)}, bf16[128,1]{0,1:T(2,128)(2,1)S(1)}) fusion(pred[]{:T(512)} %compare_reduce_fusion.1, s32[128]{0:T(128)} %param.17, pred[]{:T(512)} %compare_reduce_fusion.2), kind=kLoop, calls=%fused_computation.54 | loop fusion | flops 2944 | bytes 1026 | tf_op jit(solution)/shard_map/reshape.128
  14.4 1.4 scatter.16.f_ref
  15.8 0.2 scatter.15
  16.0 1.6 %pad_maximum_fusion.x_ref = bf16[128,896]{1,0:T(8,128)(2,1)} fusion(bf16[128,128]{1,0:T(8,128)(2,1)S(1)} %scatter.15, bf16[128,768]{1,0:T(8,128)(2,1)} %param.16), kind=kLoop, calls=%fused_computation.22 | loop fusion | flops 458752 | bytes 458752 | tf_op jit(solution)/shard_map/concatenate | solution.py:349
  17.6 20.6 %shard_map.76 = bf16[2,4,128,896]{3,2,1,0:T(8,128)(2,1)} custom-call(bf16[128,896]{1,0:T(8,128)(2,1)} %pad_maximum_fusion.x_ref), custom_call_target="tpu_custom_call" | custom-call | tf_op jit(solution)/shard_map/pallas_call | solution.py:125
  38.2 25.2 %shard_map.77 = (f32[1024,768]{1,0:T(8,128)}, f32[1024,128]{1,0:T(8,128)}) custom-call(bf16[1024,896]{1,0:T(8,128)(2,1)} %bitcast.15, bf16[4096,768]{1,0:T(8,128)(2,1)} %k_ref.1, bf16[128,768]{1,0:T(8,128)(2,1)} %scatter.16.f_ref), custom_call_target="tpu_custom_call" | custom-call | tf_op jit(solution)/shard_map/pallas_call | solution.py:62
  63.5 0.4 fusion.15
  63.9 1.1 fusion.9
  65.0 1.2 broadcast_in_dim.36.pos_ref
  66.2 49.4 %shard_map.78 = (f32[8,896]{1,0:T(8,128)}, f32[8,128]{1,0:T(8,128)}) custom-call(f32[2,64,8,768]{3,2,1,0:T(8,128)} %bitcast.18, f32[2,64,8,128]{3,2,1,0:T(8,128)} %bitcast.19, f32[8,128]{1,0:T(8,128)} %broadcast_in_dim.36.pos_ref), custom_call_target="tpu_custom_call" | custom-call | tf_op jit(solution)/shard_map/pallas_call | solution.py:305
  115.7 1.2 slice.104
  117.6 0.9 slice_reduce_fusion
  118.5 1.2 slice_convert_fusion
  119.7 0.5 fusion.13
  120.2 2.0 %fusion.1 = pred[4096]{0:T(1024)(128)(4,1)S(1)} fusion(s32[1024]{0:T(1024)S(1)} %fusion.13), kind=kLoop, calls=%fused_computation.3 | loop fusion | flops 8384512 | bytes 8192 | tf_op jit(solution)/shard_map/reduce_or | solution.py:392
  122.1 0.6 gather_fusion
  122.7 0.7 convert_subtract_fusion
  123.4 11.3 %broadcast_select_fusion = bf16[4096,768]{1,0:T(8,128)(2,1)} fusion(bf16[4096,768]{1,0:T(8,128)(2,1)} %k_ref.1, pred[4096]{0:T(1024)(128)(4,1)S(1)} %fusion.1, s32[1024]{0:T(1024)S(1)} %fusion.13, bf16[1024,896]{1,0:T(8,128)(2,1)S(1)} %copy-done.1), kind=kOutput, calls=%fused_computation.6 | convolution fusion | flops 6452936704 | bytes 14163968 | tf_op jit(solution)/shard_map/dot_general | solution.py:391
  (25 shorter events, 0.8 us)
Async XLA Ops:
  7.2 111.3 %all-gather.2.cloned.1.call-start = ((), (), s32[]{:S(2)}) async-start(), calls=%async_computation | async-start | bytes 1849344 | tf_op jit(solution)/shard_map/all_gather | solution.py:358
  38.2 25.2 %copy-start = (bf16[2,4,128,896]{3,2,1,0:T(8,128)(2,1)S(1)}, bf16[2,4,128,896]{3,2,1,0:T(8,128)(2,1)}, u32[]{:S(2)}) copy-start(bf16[2,4,128,896]{3,2,1,0:T(8,128)(2,1)} %shard_map.76) | copy-start | bytes 5505028
  38.2 25.7 %copy-start.2 = (bf16[8,768]{1,0:T(8,128)(2,1)S(1)}, bf16[8,768]{1,0:T(8,128)(2,1)}, u32[]{:S(2)}) copy-start(bf16[8,768]{1,0:T(8,128)(2,1)} %param.14) | copy-start | bytes 36868
  63.5 54.0 %copy-start.4 = (s32[128]{0:T(128)S(1)}, s32[128]{0:T(128)}, u32[]{:S(2)}) copy-start(s32[128]{0:T(128)} %param.17) | copy-start | bytes 1540
  115.6 7.1 %copy-start.3 = (f32[8,896]{1,0:T(8,128)S(1)}, f32[8,896]{1,0:T(8,128)}, u32[]{:S(2)}) copy-start(f32[8,896]{1,0:T(8,128)} %get-tuple-element.57) | copy-start | bytes 86020
  118.5 3.7 %slice-start = ((bf16[1024,896]{1,0:T(8,128)(2,1)}), bf16[1024,768]{1,0:T(8,128)(2,1)S(1)}, s32[]{:S(2)}) async-start(bf16[1024,896]{1,0:T(8,128)(2,1)} %all-gather.2.cloned.1.call-done), calls=%async_computation.1 | async-start | bytes 3145728 | tf_op jit(solution)/shard_map/slice | solution.py:361
  118.5 4.9 %copy-start.1 = (bf16[1024,896]{1,0:T(8,128)(2,1)S(1)}, bf16[1024,896]{1,0:T(8,128)(2,1)}, u32[]{:S(2)}) copy-start(bf16[1024,896]{1,0:T(8,128)(2,1)} %all-gather.2.cloned.1.call-done) | copy-start | bytes 5505028
Sparse Core Ops, SparseCore 0:
  11.4 69.0 all-gather.1

commit v14 on v12

--- a/solution.py
+++ b/solution.py
@@ -79,21 +79,27 @@
     )(queries, keys, fresh_padded)
 
 
-def gather_kernel(x_ref, o_ref, buf, sems):
+def gather_kernel(x_ref, f_ref, o_ref, fo_ref, buf, fbuf, sems):
     dp = lax.axis_index("dp")
     y, c = dp // 2, lax.rem(dp, 2)
     ys = lax.axis_size("dp") // 2
+    r = ys
     qi = lax.axis_index("queue")
+    mine_at = {"y": y, "z": qi // r, "x": lax.rem(qi, r)}
     partner = (dp + 1 - 2 * c, qi)
 
-    def along(k):
-        return (lax.rem(y + k, ys) * 2 + c, qi)
+    def along(axis, j):
+        at = dict(mine_at)
+        at[axis] = j
+        return (at["y"] * 2 + c, at["z"] * r + at["x"])
 
     barrier = pltpu.get_barrier_semaphore()
     pl.semaphore_signal(barrier, inc=1, device_id=partner, device_id_type=MESH)
-    for k in range(1, ys):
-        pl.semaphore_signal(barrier, inc=1, device_id=along(k), device_id_type=MESH)
-    pl.semaphore_wait(barrier, ys)
+    for axis in ("y", "x", "z"):
+        for k in range(1, r):
+            pl.semaphore_signal(barrier, inc=1, device_id=along(axis, lax.rem(mine_at[axis] + k, r)),
+                                device_id_type=MESH)
+    pl.semaphore_wait(barrier, 1 + 3 * (r - 1))
 
     mine = pltpu.make_async_copy(x_ref, buf.at[c, y], sems.at[4])
     mine.start()
@@ -102,10 +108,31 @@
             src_ref=x_ref, dst_ref=buf.at[c, y], send_sem=sems.at[0], recv_sem=sems.at[1],
             device_id=dst, device_id_type=MESH,
         )
-        for dst in [partner] + [along(k) for k in range(1, ys)]
+        for dst in [partner] + [along("y", lax.rem(y + k, ys)) for k in range(1, ys)]
     ]
     for copy in first:
         copy.start()
+
+    yi, zi, xi = mine_at["y"], mine_at["z"], mine_at["x"]
+
+    def fresh_round(i, axis, src, dst):
+        for k in range(1, r):
+            pltpu.make_async_remote_copy(
+                src_ref=src, dst_ref=dst, send_sem=sems.at[6 + 2 * i], recv_sem=sems.at[7 + 2 * i],
+                device_id=along(axis, lax.rem(mine_at[axis] + k, r)), device_id_type=MESH,
+            ).start()
+
+    own_fresh = pltpu.make_async_copy(f_ref, fbuf.at[yi, c, zi, xi], sems.at[5])
+    own_fresh.start()
+    fresh_round(0, "x", f_ref, fbuf.at[yi, c, zi, xi])
+    own_fresh.wait()
+    _wait_bytes(fbuf.at[0, 0, 0, pl.ds(0, r - 1)], fbuf.at[0, 0, 0, pl.ds(0, r - 1)],
+                sems.at[6], sems.at[7], along("x", lax.rem(xi + 1, r)))
+    fresh_round(1, "z", fbuf.at[yi, c, zi], fbuf.at[yi, c, zi])
+    _wait_bytes(fbuf.at[0, 0, pl.ds(0, r - 1)], fbuf.at[0, 0, pl.ds(0, r - 1)],
+                sems.at[8], sems.at[9], along("z", lax.rem(zi + 1, r)))
+    fresh_round(2, "y", fbuf.at[yi, c], fbuf.at[yi, c])
+
     _wait_bytes(buf.at[0], buf.at[0], sems.at[0], sems.at[1], partner)
     mine.wait()
     second = [
@@ -117,22 +144,35 @@
     ]
     for copy in second:
         copy.start()
+    _wait_bytes(fbuf.at[pl.ds(0, r - 1), 0], fbuf.at[pl.ds(0, r - 1), 0],
+                sems.at[10], sems.at[11], along("y", lax.rem(yi + 1, r)))
+    for j in range(r):
+        pltpu.make_async_remote_copy(
+            src_ref=fbuf.at[j, c], dst_ref=fbuf.at[j, c], send_sem=sems.at[12], recv_sem=sems.at[13],
+            device_id=partner, device_id_type=MESH,
+        ).start()
     _wait_bytes(buf.at[0, pl.ds(0, ys - 1)], buf.at[0, pl.ds(0, ys - 1)], sems.at[2], sems.at[3], partner)
+    _wait_bytes(fbuf.at[:, 0], fbuf.at[:, 0], sems.at[12], sems.at[13], partner)
     o_ref[...] = buf[...]
-
-
-def gather_dp(x, ys):
+    fo_ref[...] = fbuf[...]
+
+
+def gather_dp(x, fresh, ys):
     return pl.pallas_call(
         gather_kernel,
-        out_shape=jax.ShapeDtypeStruct((2, ys) + x.shape, x.dtype),
-        in_specs=[pl.BlockSpec(memory_space=pltpu.VMEM)],
-        out_specs=pl.BlockSpec(memory_space=pltpu.VMEM),
+        out_shape=(
+            jax.ShapeDtypeStruct((2, ys) + x.shape, x.dtype),
+            jax.ShapeDtypeStruct((ys, 2, ys, ys) + fresh.shape, fresh.dtype),
+        ),
+        in_specs=[pl.BlockSpec(memory_space=pltpu.VMEM), pl.BlockSpec(memory_space=pltpu.VMEM)],
+        out_specs=(pl.BlockSpec(memory_space=pltpu.VMEM), pl.BlockSpec(memory_space=pltpu.VMEM)),
         scratch_shapes=[
             pltpu.VMEM((2, ys) + x.shape, x.dtype),
-            pltpu.SemaphoreType.DMA((5,)),
+            pltpu.VMEM((ys, 2, ys, ys) + fresh.shape, fresh.dtype),
+            pltpu.SemaphoreType.DMA((14,)),
         ],
         compiler_params=pltpu.CompilerParams(collective_id=1, has_side_effects=True),
-    )(x)
+    )(x, fresh)
 
 
 def _merge(blocks, at):
@@ -346,18 +386,20 @@
     pos_code = jnp.zeros((queries.shape[0], STAT), jnp.bfloat16)
     pos_code = pos_code.at[:, 0].set((positives // 32).astype(jnp.bfloat16))
     pos_code = pos_code.at[:, 1].set((positives % 32).astype(jnp.bfloat16))
-    gathered = gather_dp(jnp.concatenate([queries, pos_code], axis=1), dp_size // 2)
+    digits = jnp.stack([slots // 16384, (slots // 128) % 128, slots % 128], axis=1)
+    code = jnp.zeros((slots.shape[0], STAT), jnp.bfloat16).at[:, :3].set(digits.astype(jnp.bfloat16))
+    gathered, fresh_ext = gather_dp(
+        jnp.concatenate([queries, pos_code], axis=1),
+        jnp.concatenate([fresh_keys, code], axis=1),
+        dp_size // 2,
+    )
+    fresh_ext = fresh_ext.reshape(n * fresh_keys.shape[0], d + STAT)
     total_rows = dp_size * queries.shape[0]
     own_rows = total_rows // n
     gathered = gathered.reshape(total_rows, d + STAT)
     all_queries = gathered[:, :d]
     pos_digits = gathered[:, d:d + 2].astype(jnp.int32)
     all_positives = pos_digits[:, 0] * 32 + pos_digits[:, 1]
-    digits = jnp.stack([slots // 16384, (slots // 128) % 128, slots % 128], axis=1)
-    code = jnp.zeros((slots.shape[0], STAT), jnp.bfloat16).at[:, :3].set(digits.astype(jnp.bfloat16))
-    fresh_ext = lax.all_gather(
-        jnp.concatenate([fresh_keys, code], axis=1), ("dp", "queue"), axis=0, tiled=True
-    )
     fresh_all = fresh_ext[:, :d]
     got = fresh_ext[:, d:d + 3].astype(jnp.int32)
     slots_all = got[:, 0] * 16384 + got[:, 1] * 128 + got[:, 2]

time: 144 us -> 143 us (level)
  between operations: 16 us -> 2.51 us
  Pallas kernels: 95.5 us -> 106 us
  other arithmetic: 13 us -> 15.4 us
    pallas_call x1, Pallas kernels: 20.6 us -> 34.1 us  [gather_dp(): pl.pallas_call(gather_kernel, out_shape=(jax.ShapeDtypeStruct((2, ys) + x...]
    pallas_call x1, Pallas kernels: 49.5 us -> 46.4 us  [combine(): pl.pallas_call(functools.partial(combine_kernel, d, side), out_shape=(jax...]
  transfers between devices with their start and end apart: 1 -> 0, of which waited for: 0 -> 0; matrix products, arithmetic and copies ran while one was open for 8% -> 0% of each run, Pallas kernels for 67% -> 0%
where the time goes in v14:
time: 143 us; the launch traced here: 142 us
  Pallas kernels  106 us (74%)
  other arithmetic  15.4 us (11%)
  matrix products  12.4 us (9%)
  local copies, waits for them, and re-layouts  6.13 us (4%)
  between operations  2.51 us (2%)
    pallas_call x1, Pallas kernels, combine(): pl.pallas_call(functools.partial(combine_kernel, d, side), out_shape=(jax...  46.4 us
    pallas_call x1, Pallas kernels, gather_dp(): pl.pallas_call(gather_kernel, out_shape=(jax.ShapeDtypeStruct((2, ys) + x...  34.1 us
    pallas_call x1, Pallas kernels, local_partials(): pl.pallas_call(partial_kernel, grid=(rows // block,), out_shape=(jax.Shap...  25.4 us
    dot_general x1, matrix products, shards(): jnp.dot(picks.astype(jnp.bfloat16), fresh_all, preferred_element_type=jnp...  11.3 us
    another operation x5, other arithmetic  4.6 us

profile of v14, /device:TPU:1, one launch (start us, length us, event | category | flops | bytes accessed | tf_op | source)
XLA Modules:
  0.0 142.3 jit_solution(6318932196662951128)
XLA Ops:
  0.6 0.6 compare_reduce_fusion.2
  1.3 0.6 compare_reduce_fusion.1
  1.9 0.6 compare_reduce_fusion
  2.6 2.0 %fusion.19 = (bf16[128,1]{0,1:T(2,128)(2,1)S(1)}, bf16[128,1]{0,1:T(2,128)(2,1)S(1)}) fusion(pred[]{:T(512)} %compare_reduce_fusion.1, s32[128]{0:T(128)} %param.17, pred[]{:T(512)} %compare_reduce_fusion.2), kind=kLoop, calls=%fused_computation.54 | loop fusion | flops 2944 | bytes 1026 | tf_op jit(solution)/shard_map/reshape.129
  4.5 0.7 compare_and_fusion
  5.3 0.7 convert_bitcast_fusion
  6.2 0.7 maximum_select_fusion
  7.0 1.3 fusion.17.f_ref
  8.7 1.6 %pad_maximum_fusion.x_ref = bf16[128,896]{1,0:T(8,128)(2,1)} fusion(bf16[128,128]{1,0:T(8,128)(2,1)S(1)} %scatter.15, bf16[128,768]{1,0:T(8,128)(2,1)} %param.16), kind=kLoop, calls=%fused_computation.22 | loop fusion | flops 458752 | bytes 458752 | tf_op jit(solution)/shard_map/concatenate | solution.py:392
  10.4 1.4 scatter.19.f_ref
  11.8 34.1 %shard_map.76 = (bf16[2,4,128,896]{3,2,1,0:T(8,128)(2,1)}, bf16[4,2,4,4,8,896]{5,4,3,2,1,0:T(8,128)(2,1)}) custom-call(bf16[128,896]{1,0:T(8,128)(2,1)} %pad_maximum_fusion.x_ref, bf16[8,896]{1,0:T(8,128)(2,1)} %fusion.17.f_ref), custom_call_target="tpu_custom_call" | custom-call | tf_op jit(solution)/shard_map/pallas_call | solution.py:161
  45.9 1.2 slice_convert_fusion
  47.0 0.5 fusion.13
  47.5 2.0 %fusion.1 = pred[4096]{0:T(1024)(128)(4,1)S(1)} fusion(s32[1024]{0:T(1024)S(1)} %fusion.13), kind=kLoop, calls=%fused_computation.3 | loop fusion | flops 8384512 | bytes 8192 | tf_op jit(solution)/shard_map/reduce_or | solution.py:434
  49.5 1.0 slice_convert_fusion.1
  50.9 1.1 fusion.9
  52.0 1.2 broadcast_in_dim.36.pos_ref
  53.4 0.6 gather_fusion
  53.9 25.4 %shard_map.77 = (f32[1024,768]{1,0:T(8,128)}, f32[1024,128]{1,0:T(8,128)}) custom-call(bf16[1024,896]{1,0:T(8,128)(2,1)} %bitcast.18, bf16[4096,768]{1,0:T(8,128)(2,1)} %k_ref.1, bf16[128,768]{1,0:T(8,128)(2,1)} %scatter.19.f_ref), custom_call_target="tpu_custom_call" | custom-call | tf_op jit(solution)/shard_map/pallas_call | solution.py:62
  79.4 46.4 %shard_map.78 = (f32[8,896]{1,0:T(8,128)}, f32[8,128]{1,0:T(8,128)}) custom-call(f32[2,64,8,768]{3,2,1,0:T(8,128)} %bitcast.16, f32[2,64,8,128]{3,2,1,0:T(8,128)} %bitcast.23, f32[8,128]{1,0:T(8,128)} %broadcast_in_dim.36.pos_ref), custom_call_target="tpu_custom_call" | custom-call | tf_op jit(solution)/shard_map/pallas_call | solution.py:345
  125.7 1.2 slice.104
  127.6 0.9 slice_reduce_fusion
  128.4 1.4 convert_subtract_fusion
  129.9 11.3 %broadcast_select_fusion = bf16[4096,768]{1,0:T(8,128)(2,1)} fusion(bf16[4096,768]{1,0:T(8,128)(2,1)} %k_ref.1, pred[4096]{0:T(1024)(128)(4,1)S(1)} %fusion.1, s32[1024]{0:T(1024)S(1)} %fusion.13, bf16[1024,896]{1,0:T(8,128)(2,1)S(1)} %bitcast.22), kind=kOutput, calls=%fused_computation.6 | convolution fusion | flops 6452936704 | bytes 14163968 | tf_op jit(solution)/shard_map/dot_general | solution.py:433
  (17 shorter events, 1.2 us)
Async XLA Ops:
  0.6 50.3 %copy-start.2 = (bf16[8,768]{1,0:T(8,128)(2,1)S(1)}, bf16[8,768]{1,0:T(8,128)(2,1)}, u32[]{:S(2)}) copy-start(bf16[8,768]{1,0:T(8,128)(2,1)} %param.14) | copy-start | bytes 36868
  45.8 5.0 %copy-start = (bf16[2,4,128,896]{3,2,1,0:T(8,128)(2,1)S(1)}, bf16[2,4,128,896]{3,2,1,0:T(8,128)(2,1)}, u32[]{:S(2)}) copy-start(bf16[2,4,128,896]{3,2,1,0:T(8,128)(2,1)} %get-tuple-element.57) | copy-start | bytes 5505028
  45.9 7.4 %copy-start.1 = (bf16[4,2,4,4,8,896]{5,4,3,2,1,0:T(8,128)(2,1)S(1)}, bf16[4,2,4,4,8,896]{5,4,3,2,1,0:T(8,128)(2,1)}, u32[]{:S(2)}) copy-start(bf16[4,2,4,4,8,896]{5,4,3,2,1,0:T(8,128)(2,1)} %get-tuple-element.61) | copy-start | bytes 5505028

commit v15 on v14

--- a/solution.py
+++ b/solution.py
@@ -390,7 +390,7 @@
     code = jnp.zeros((slots.shape[0], STAT), jnp.bfloat16).at[:, :3].set(digits.astype(jnp.bfloat16))
     gathered, fresh_ext = gather_dp(
         jnp.concatenate([queries, pos_code], axis=1),
-        jnp.concatenate([fresh_keys, code], axis=1),
+        jnp.concatenate([fresh_keys, code], axis=1).astype(jnp.float32),
         dp_size // 2,
     )
     fresh_ext = fresh_ext.reshape(n * fresh_keys.shape[0], d + STAT)
@@ -400,7 +400,7 @@
     all_queries = gathered[:, :d]
     pos_digits = gathered[:, d:d + 2].astype(jnp.int32)
     all_positives = pos_digits[:, 0] * 32 + pos_digits[:, 1]
-    fresh_all = fresh_ext[:, :d]
+    fresh_all = fresh_ext[:, :d].astype(jnp.bfloat16)
     got = fresh_ext[:, d:d + 3].astype(jnp.int32)
     slots_all = got[:, 0] * 16384 + got[:, 1] * 128 + got[:, 2]
 

time: 143 us -> 158 us (1.10)
  Pallas kernels: 106 us -> 118 us
  local copies, waits for them, and re-layouts: 6.13 us -> 8.08 us
    pallas_call x1, Pallas kernels: 34.1 us -> 45.8 us  [gather_dp(): pl.pallas_call(gather_kernel, out_shape=(jax.ShapeDtypeStruct((2, ys) + x...]
    slice x1, local copies, waits for them, and re-layouts: 0.1 us -> 2.04 us  [shards(): fresh_all = fresh_ext[:, :d].astype(jnp.bfloat16)]
where the time goes in v15:
time: 158 us; the launch traced here: 157 us
  Pallas kernels  118 us (75%)
  other arithmetic  15.4 us (10%)
  matrix products  13.4 us (8%)
  local copies, waits for them, and re-layouts  8.08 us (5%)
  between operations  2.51 us (2%)
    pallas_call x1, Pallas kernels, combine(): pl.pallas_call(functools.partial(combine_kernel, d, side), out_shape=(jax...  46.7 us
    pallas_call x1, Pallas kernels, gather_dp(): pl.pallas_call(gather_kernel, out_shape=(jax.ShapeDtypeStruct((2, ys) + x...  45.8 us
    pallas_call x1, Pallas kernels, local_partials(): pl.pallas_call(partial_kernel, grid=(rows // block,), out_shape=(jax.Shap...  25.4 us
    dot_general x1, matrix products, shards(): jnp.dot(picks.astype(jnp.bfloat16), fresh_all, preferred_element_type=jnp...  12.3 us
    another operation x5, other arithmetic  4.6 us

profile of v15, /device:TPU:1, one launch (start us, length us, event | category | flops | bytes accessed | tf_op | source)
XLA Modules:
  0.0 157.3 jit_solution(7145887649716106543)
XLA Ops:
  0.6 0.6 compare_reduce_fusion.2
  1.3 0.6 compare_reduce_fusion.1
  1.9 0.6 compare_reduce_fusion
  2.6 2.0 %fusion.20 = (bf16[128,1]{0,1:T(2,128)(2,1)S(1)}, bf16[128,1]{0,1:T(2,128)(2,1)S(1)}) fusion(pred[]{:T(512)} %compare_reduce_fusion.1, s32[128]{0:T(128)} %param.17, pred[]{:T(512)} %compare_reduce_fusion.2), kind=kLoop, calls=%fused_computation.56 | loop fusion | flops 2944 | bytes 1026 | tf_op jit(solution)/shard_map/reshape.129
  4.5 0.7 compare_and_fusion
  5.3 0.7 convert_bitcast_fusion
  6.2 0.7 maximum_select_fusion
  7.0 1.3 fusion.18.f_ref
  8.7 1.6 %pad_maximum_fusion.x_ref = bf16[128,896]{1,0:T(8,128)(2,1)} fusion(bf16[128,128]{1,0:T(8,128)(2,1)S(1)} %scatter.15, bf16[128,768]{1,0:T(8,128)(2,1)} %param.16), kind=kLoop, calls=%fused_computation.23 | loop fusion | flops 458752 | bytes 458752 | tf_op jit(solution)/shard_map/concatenate | solution.py:392
  10.4 1.4 scatter.19.f_ref
  11.8 45.8 %shard_map.76 = (bf16[2,4,128,896]{3,2,1,0:T(8,128)(2,1)}, f32[4,2,4,4,8,896]{5,4,3,2,1,0:T(8,128)}) custom-call(bf16[128,896]{1,0:T(8,128)(2,1)} %pad_maximum_fusion.x_ref, f32[8,896]{1,0:T(8,128)} %fusion.18.f_ref), custom_call_target="tpu_custom_call" | custom-call | tf_op jit(solution)/shard_map/pallas_call | solution.py:161
  57.6 1.2 slice_convert_fusion.1
  59.3 2.0 %fusion.1 = pred[4096]{0:T(1024)(128)(4,1)S(1)} fusion(s32[1024]{0:T(1024)S(1)} %fusion.13), kind=kLoop, calls=%fused_computation.3 | loop fusion | flops 8384512 | bytes 8192 | tf_op jit(solution)/shard_map/reduce_or | solution.py:434
  61.3 1.0 slice_convert_fusion.2
  62.7 1.1 fusion.9
  63.8 1.2 broadcast_in_dim.36.pos_ref
  65.0 2.0 %slice.151 = bf16[1024,768]{1,0:T(8,128)(2,1)S(1)} slice(f32[1024,896]{1,0:T(8,128)} %bitcast.21), slice={[0:1024], [0:768]} | slice | bytes 3145728 | tf_op jit(solution)/shard_map/slice | solution.py:403
  67.1 0.6 gather_fusion
  67.6 25.4 %shard_map.77 = (f32[1024,768]{1,0:T(8,128)}, f32[1024,128]{1,0:T(8,128)}) custom-call(bf16[1024,896]{1,0:T(8,128)(2,1)} %bitcast.18, bf16[4096,768]{1,0:T(8,128)(2,1)} %k_ref.1, bf16[128,768]{1,0:T(8,128)(2,1)} %scatter.19.f_ref), custom_call_target="tpu_custom_call" | custom-call | tf_op jit(solution)/shard_map/pallas_call | solution.py:62
  93.0 46.7 %shard_map.78 = (f32[8,896]{1,0:T(8,128)}, f32[8,128]{1,0:T(8,128)}) custom-call(f32[2,64,8,768]{3,2,1,0:T(8,128)} %bitcast.16, f32[2,64,8,128]{3,2,1,0:T(8,128)} %bitcast.23, f32[8,128]{1,0:T(8,128)} %broadcast_in_dim.36.pos_ref), custom_call_target="tpu_custom_call" | custom-call | tf_op jit(solution)/shard_map/pallas_call | solution.py:345
  139.7 1.2 slice.105
  141.6 0.9 slice_reduce_fusion
  142.4 1.4 convert_subtract_fusion
  143.8 12.3 %broadcast_select_fusion = bf16[4096,768]{1,0:T(8,128)(2,1)} fusion(bf16[4096,768]{1,0:T(8,128)(2,1)} %k_ref.1, pred[4096]{0:T(1024)(128)(4,1)S(1)} %fusion.1, s32[1024]{0:T(1024)S(1)} %fusion.13, f32[1024,896]{1,0:T(8,128)} %bitcast.22), kind=kOutput, calls=%fused_computation.6 | convolution fusion | flops 6452936704 | bytes 14163968 | tf_op jit(solution)/shard_map/dot_general | solution.py:433
  (15 shorter events, 1.6 us)
Async XLA Ops:
  0.6 62.0 %copy-start.1 = (bf16[8,768]{1,0:T(8,128)(2,1)S(1)}, bf16[8,768]{1,0:T(8,128)(2,1)}, u32[]{:S(2)}) copy-start(bf16[8,768]{1,0:T(8,128)(2,1)} %param.14) | copy-start | bytes 36868
  57.6 5.1 %copy-start = (bf16[2,4,128,896]{3,2,1,0:T(8,128)(2,1)S(1)}, bf16[2,4,128,896]{3,2,1,0:T(8,128)(2,1)}, u32[]{:S(2)}) copy-start(bf16[2,4,128,896]{3,2,1,0:T(8,128)(2,1)} %get-tuple-element.57) | copy-start | bytes 5505028

commit v16 on v14

--- a/solution.py
+++ b/solution.py
@@ -122,16 +122,16 @@
                 device_id=along(axis, lax.rem(mine_at[axis] + k, r)), device_id_type=MESH,
             ).start()
 
-    own_fresh = pltpu.make_async_copy(f_ref, fbuf.at[yi, c, zi, xi], sems.at[5])
+    own_fresh = pltpu.make_async_copy(f_ref, fbuf.at[c, xi, zi, yi], sems.at[5])
     own_fresh.start()
-    fresh_round(0, "x", f_ref, fbuf.at[yi, c, zi, xi])
+    fresh_round(0, "y", f_ref, fbuf.at[c, xi, zi, yi])
     own_fresh.wait()
     _wait_bytes(fbuf.at[0, 0, 0, pl.ds(0, r - 1)], fbuf.at[0, 0, 0, pl.ds(0, r - 1)],
-                sems.at[6], sems.at[7], along("x", lax.rem(xi + 1, r)))
-    fresh_round(1, "z", fbuf.at[yi, c, zi], fbuf.at[yi, c, zi])
+                sems.at[6], sems.at[7], along("y", lax.rem(yi + 1, r)))
+    fresh_round(1, "z", fbuf.at[c, xi, zi], fbuf.at[c, xi, zi])
     _wait_bytes(fbuf.at[0, 0, pl.ds(0, r - 1)], fbuf.at[0, 0, pl.ds(0, r - 1)],
                 sems.at[8], sems.at[9], along("z", lax.rem(zi + 1, r)))
-    fresh_round(2, "y", fbuf.at[yi, c], fbuf.at[yi, c])
+    fresh_round(2, "x", fbuf.at[c, xi], fbuf.at[c, xi])
 
     _wait_bytes(buf.at[0], buf.at[0], sems.at[0], sems.at[1], partner)
     mine.wait()
@@ -144,15 +144,14 @@
     ]
     for copy in second:
         copy.start()
-    _wait_bytes(fbuf.at[pl.ds(0, r - 1), 0], fbuf.at[pl.ds(0, r - 1), 0],
-                sems.at[10], sems.at[11], along("y", lax.rem(yi + 1, r)))
-    for j in range(r):
-        pltpu.make_async_remote_copy(
-            src_ref=fbuf.at[j, c], dst_ref=fbuf.at[j, c], send_sem=sems.at[12], recv_sem=sems.at[13],
-            device_id=partner, device_id_type=MESH,
-        ).start()
+    _wait_bytes(fbuf.at[0, pl.ds(0, r - 1)], fbuf.at[0, pl.ds(0, r - 1)],
+                sems.at[10], sems.at[11], along("x", lax.rem(xi + 1, r)))
+    pltpu.make_async_remote_copy(
+        src_ref=fbuf.at[c], dst_ref=fbuf.at[c], send_sem=sems.at[12], recv_sem=sems.at[13],
+        device_id=partner, device_id_type=MESH,
+    ).start()
     _wait_bytes(buf.at[0, pl.ds(0, ys - 1)], buf.at[0, pl.ds(0, ys - 1)], sems.at[2], sems.at[3], partner)
-    _wait_bytes(fbuf.at[:, 0], fbuf.at[:, 0], sems.at[12], sems.at[13], partner)
+    _wait_bytes(fbuf.at[0], fbuf.at[0], sems.at[12], sems.at[13], partner)
     o_ref[...] = buf[...]
     fo_ref[...] = fbuf[...]
 
@@ -162,13 +161,13 @@
         gather_kernel,
         out_shape=(
             jax.ShapeDtypeStruct((2, ys) + x.shape, x.dtype),
-            jax.ShapeDtypeStruct((ys, 2, ys, ys) + fresh.shape, fresh.dtype),
+            jax.ShapeDtypeStruct((2, ys, ys, ys) + fresh.shape, fresh.dtype),
         ),
         in_specs=[pl.BlockSpec(memory_space=pltpu.VMEM), pl.BlockSpec(memory_space=pltpu.VMEM)],
         out_specs=(pl.BlockSpec(memory_space=pltpu.VMEM), pl.BlockSpec(memory_space=pltpu.VMEM)),
         scratch_shapes=[
             pltpu.VMEM((2, ys) + x.shape, x.dtype),
-            pltpu.VMEM((ys, 2, ys, ys) + fresh.shape, fresh.dtype),
+            pltpu.VMEM((2, ys, ys, ys) + fresh.shape, fresh.dtype),
             pltpu.SemaphoreType.DMA((14,)),
         ],
         compiler_params=pltpu.CompilerParams(collective_id=1, has_side_effects=True),
@@ -393,7 +392,7 @@
         jnp.concatenate([fresh_keys, code], axis=1),
         dp_size // 2,
     )
-    fresh_ext = fresh_ext.reshape(n * fresh_keys.shape[0], d + STAT)
+    fresh_ext = fresh_ext.transpose(3, 0, 2, 1, 4, 5).reshape(n * fresh_keys.shape[0], d + STAT)
     total_rows = dp_size * queries.shape[0]
     own_rows = total_rows // n
     gathered = gathered.reshape(total_rows, d + STAT)

time: 143 us -> 149 us (1.042)
  Pallas kernels: 106 us -> 112 us
  other arithmetic: 15.4 us -> 13.3 us
  local copies, waits for them, and re-layouts: 6.13 us -> 7.95 us
    pallas_call x1, Pallas kernels: 34.1 us -> 40.9 us  [gather_dp(): pl.pallas_call(gather_kernel, out_shape=(jax.ShapeDtypeStruct((2, ys) + x...]
    transpose x0 -> x1, local copies, waits for them, and re-layouts: none -> 1.83 us  [shards(): fresh_ext.transpose(3, 0, 2, 1, 4, 5)]
where the time goes in v16:
time: 149 us
  Pallas kernels  112 us (75%)
  other arithmetic  13.3 us (9%)
  matrix products  12.5 us (8%)
  local copies, waits for them, and re-layouts  7.95 us (5%)
  between operations  2.52 us (2%)
    pallas_call x1, Pallas kernels, combine(): pl.pallas_call(functools.partial(combine_kernel, d, side), out_shape=(jax...  46.1 us
    pallas_call x1, Pallas kernels, gather_dp(): pl.pallas_call(gather_kernel, out_shape=(jax.ShapeDtypeStruct((2, ys) + x...  40.9 us
    pallas_call x1, Pallas kernels, local_partials(): pl.pallas_call(partial_kernel, grid=(rows // block,), out_shape=(jax.Shap...  25.4 us
    dot_general x1, matrix products, shards(): jnp.dot(picks.astype(jnp.bfloat16), fresh_all, preferred_element_type=jnp...  11.3 us
    another operation x5, other arithmetic  4.6 us

profile of v16, /device:TPU:1, one launch (start us, length us, event | category | flops | bytes accessed | tf_op | source)
XLA Modules:
  0.0 148.7 jit_solution(16118176104167480427)
XLA Ops:
  0.6 0.6 compare_reduce_fusion.2
  1.3 0.6 compare_reduce_fusion.1
  1.9 0.6 compare_reduce_fusion
  2.5 2.0 %fusion.19 = (bf16[128,1]{0,1:T(2,128)(2,1)S(1)}, bf16[128,1]{0,1:T(2,128)(2,1)S(1)}) fusion(pred[]{:T(512)} %compare_reduce_fusion.1, s32[128]{0:T(128)} %param.17, pred[]{:T(512)} %compare_reduce_fusion.2), kind=kLoop, calls=%fused_computation.54 | loop fusion | flops 2944 | bytes 1026 | tf_op jit(solution)/shard_map/reshape.129
  4.5 0.7 compare_and_fusion
  5.3 0.7 convert_bitcast_fusion
  6.2 0.7 maximum_select_fusion
  6.9 1.3 fusion.17.f_ref
  8.7 1.6 %pad_maximum_fusion.x_ref = bf16[128,896]{1,0:T(8,128)(2,1)} fusion(bf16[128,128]{1,0:T(8,128)(2,1)S(1)} %scatter.15, bf16[128,768]{1,0:T(8,128)(2,1)} %param.16), kind=kLoop, calls=%fused_computation.22 | loop fusion | flops 458752 | bytes 458752 | tf_op jit(solution)/shard_map/concatenate | solution.py:391
  10.4 1.4 scatter.19.f_ref
  11.8 40.9 %shard_map.76 = (bf16[2,4,128,896]{3,2,1,0:T(8,128)(2,1)}, bf16[2,4,4,4,8,896]{5,4,3,2,1,0:T(8,128)(2,1)}) custom-call(bf16[128,896]{1,0:T(8,128)(2,1)} %pad_maximum_fusion.x_ref, bf16[8,896]{1,0:T(8,128)(2,1)} %fusion.17.f_ref), custom_call_target="tpu_custom_call" | custom-call | tf_op jit(solution)/shard_map/pallas_call | solution.py:160
  52.7 1.8 %copy.24 = bf16[4,2,4,4,8,896]{5,4,3,2,1,0:T(8,128)(2,1)S(1)} copy(bf16[4,2,4,4,8,896]{5,4,0,2,3,1:T(8,128)(2,1)} %bitcast.24) | data formatting | bytes 3670016 | tf_op jit(solution)/shard_map/transpose | solution.py:395
  54.6 0.5 fusion.13
  55.1 2.0 %fusion.1 = pred[4096]{0:T(1024)(128)(4,1)S(1)} fusion(s32[1024]{0:T(1024)S(1)} %fusion.13), kind=kLoop, calls=%fused_computation.3 | loop fusion | flops 8384512 | bytes 8192 | tf_op jit(solution)/shard_map/reduce_or | solution.py:433
  57.2 0.4 fusion.15
  57.5 1.1 fusion.9
  58.7 1.2 broadcast_in_dim.36.pos_ref
  60.0 0.6 gather_fusion
  60.6 25.4 %shard_map.77 = (f32[1024,768]{1,0:T(8,128)}, f32[1024,128]{1,0:T(8,128)}) custom-call(bf16[1024,896]{1,0:T(8,128)(2,1)} %bitcast.21, bf16[4096,768]{1,0:T(8,128)(2,1)} %k_ref.1, bf16[128,768]{1,0:T(8,128)(2,1)} %scatter.19.f_ref), custom_call_target="tpu_custom_call" | custom-call | tf_op jit(solution)/shard_map/pallas_call | solution.py:62
  86.0 46.1 %shard_map.78 = (f32[8,896]{1,0:T(8,128)}, f32[8,128]{1,0:T(8,128)}) custom-call(f32[2,64,8,768]{3,2,1,0:T(8,128)} %bitcast.20, f32[2,64,8,128]{3,2,1,0:T(8,128)} %bitcast.25, f32[8,128]{1,0:T(8,128)} %broadcast_in_dim.36.pos_ref), custom_call_target="tpu_custom_call" | custom-call | tf_op jit(solution)/shard_map/pallas_call | solution.py:344
  132.1 1.2 slice.104
  133.9 0.9 slice_reduce_fusion
  134.8 1.4 convert_subtract_fusion
  136.2 11.3 %broadcast_select_fusion = bf16[4096,768]{1,0:T(8,128)(2,1)} fusion(bf16[4096,768]{1,0:T(8,128)(2,1)} %k_ref.1, pred[4096]{0:T(1024)(128)(4,1)S(1)} %fusion.1, s32[1024]{0:T(1024)S(1)} %fusion.13, bf16[1024,896]{1,0:T(8,128)(2,1)S(1)} %bitcast.19), kind=kOutput, calls=%fused_computation.6 | convolution fusion | flops 6452936704 | bytes 14163968 | tf_op jit(solution)/shard_map/dot_general | solution.py:432
  (16 shorter events, 1.0 us)
Async XLA Ops:
  52.7 4.4 %copy-start = (bf16[2,4,128,896]{3,2,1,0:T(8,128)(2,1)S(1)}, bf16[2,4,128,896]{3,2,1,0:T(8,128)(2,1)}, u32[]{:S(2)}) copy-start(bf16[2,4,128,896]{3,2,1,0:T(8,128)(2,1)} %get-tuple-element.57) | copy-start | bytes 5505028
  52.7 4.8 %copy-start.1 = (bf16[8,768]{1,0:T(8,128)(2,1)S(1)}, bf16[8,768]{1,0:T(8,128)(2,1)}, u32[]{:S(2)}) copy-start(bf16[8,768]{1,0:T(8,128)(2,1)} %param.14) | copy-start | bytes 36868

commit v17 on v14

--- a/solution.py
+++ b/solution.py
@@ -429,10 +429,10 @@
     mean_loss = loss_tile[0, 0] / total_rows
     held_rows = queue_keys.shape[0]
     local_slot = slots_all - device_index * held_rows
-    picks = jnp.arange(held_rows, dtype=jnp.int32)[:, None] == local_slot[None, :]
-    inserted = jnp.dot(picks.astype(jnp.bfloat16), fresh_all, preferred_element_type=jnp.float32)
-    replaced = jnp.any(picks, axis=1)
-    new_queue = jnp.where(replaced[:, None], inserted.astype(jnp.bfloat16), queue_keys)
+    inside = (local_slot >= 0) & (local_slot < held_rows)
+    spare = held_rows + jnp.arange(local_slot.shape[0], dtype=jnp.int32)
+    target = jnp.where(inside, local_slot, spare)
+    new_queue = queue_keys.at[target].set(fresh_all, mode="drop", unique_indices=True)
     return (query_grad, mean_loss, new_queue)
 
 

time: 143 us -> 142 us (level)
  local copies, waits for them, and re-layouts: 6.13 us -> 23.3 us
  matrix products: 12.4 us -> 1.12 us
  other arithmetic: 15.4 us -> 8.21 us
    scatter x0 -> x1, local copies, waits for them, and re-layouts: none -> 11.9 us  [shards(): queue_keys.at[target].set(fresh_all, mode='drop', unique_indices=True)]
    dot_general x1 -> x0, matrix products: 11.3 us -> none  [shards(): jnp.dot(picks.astype(jnp.bfloat16), fresh_all, preferred_element_type=jnp...]
    unnamed x6 -> x15, local copies, waits for them, and re-layouts: 0.01 us -> 6.01 us
    reduce_or x1 -> x0, other arithmetic: 1.97 us -> none  [shards(): replaced = jnp.any(picks, axis=1)]
where the time goes in v17:
time: 142 us; the launch traced here: 141 us
  Pallas kernels  106 us (75%)
  local copies, waits for them, and re-layouts  23.3 us (16%)
  other arithmetic  8.21 us (6%)
  between operations  2.58 us (2%)
    pallas_call x1, Pallas kernels, combine(): pl.pallas_call(functools.partial(combine_kernel, d, side), out_shape=(jax...  46.5 us
    pallas_call x1, Pallas kernels, gather_dp(): pl.pallas_call(gather_kernel, out_shape=(jax.ShapeDtypeStruct((2, ys) + x...  34.1 us
    pallas_call x1, Pallas kernels, local_partials(): pl.pallas_call(partial_kernel, grid=(rows // block,), out_shape=(jax.Shap...  25.4 us
    scatter x1, local copies, waits for them, and re-layouts, shards(): queue_keys.at[target].set(fresh_all, mode='drop', unique_indices=True)  11.9 us
    unnamed x15, local copies, waits for them, and re-layouts  6.01 us
    another operation x5, other arithmetic  4.06 us

profile of v17, /device:TPU:1, one launch (start us, length us, event | category | flops | bytes accessed | tf_op | source)
XLA Modules:
  0.0 141.2 jit_solution(16926219793954861840)
XLA Ops:
  0.7 5.9 %copy.21.k_ref = bf16[4096,768]{1,0:T(8,128)(2,1)} copy(bf16[4096,768]{1,0:T(8,128)(2,1)} %param.13) | data formatting | bytes 12582912
  6.9 0.6 compare_reduce_fusion
  7.6 0.7 maximum_select_fusion
  8.3 0.6 fusion.13.f_ref
  8.9 0.6 compare_reduce_fusion.1
  9.5 0.7 compare_reduce_fusion.2
  10.2 1.3 fusion.15
  11.6 0.1 copy.13
  11.9 0.2 scatter.21
  12.1 0.7 pad_maximum_fusion.x_ref
  12.8 34.1 %shard_map.76 = (bf16[2,4,128,896]{3,2,1,0:T(8,128)(2,1)}, bf16[4,2,4,4,8,896]{5,4,3,2,1,0:T(8,128)(2,1)}) custom-call(bf16[128,896]{1,0:T(8,128)(2,1)} %pad_maximum_fusion.x_ref, bf16[8,896]{1,0:T(8,128)(2,1)} %fusion.13.f_ref), custom_call_target="tpu_custom_call" | custom-call | tf_op jit(solution)/shard_map/pallas_call | solution.py:161
  46.9 1.1 slice_convert_fusion.1
  48.0 0.4 fusion.11
  48.5 1.1 fusion.5
  49.6 1.2 broadcast_in_dim.26.pos_ref
  50.8 0.7 scatter.30.f_ref
  51.5 25.4 %shard_map.77 = (f32[1024,768]{1,0:T(8,128)}, f32[1024,128]{1,0:T(8,128)}) custom-call(bf16[1024,896]{1,0:T(8,128)(2,1)} %bitcast.21, bf16[4096,768]{1,0:T(8,128)(2,1)} %copy.21.k_ref, bf16[128,768]{1,0:T(8,128)(2,1)} %scatter.30.f_ref), custom_call_target="tpu_custom_call" | custom-call | tf_op jit(solution)/shard_map/pallas_call | solution.py:62
  76.9 46.5 %shard_map.78 = (f32[8,896]{1,0:T(8,128)}, f32[8,128]{1,0:T(8,128)}) custom-call(f32[2,64,8,768]{3,2,1,0:T(8,128)} %bitcast.19, f32[2,64,8,128]{3,2,1,0:T(8,128)} %bitcast.23, f32[8,128]{1,0:T(8,128)} %broadcast_in_dim.26.pos_ref), custom_call_target="tpu_custom_call" | custom-call | tf_op jit(solution)/shard_map/pallas_call | solution.py:345
  123.4 0.9 slice_reduce_fusion
  124.6 0.6 gather_fusion
  125.1 0.7 convert_subtract_fusion
  125.8 1.2 slice.104
  127.7 0.5 fusion.8
  128.2 11.9 %scatter_custom_fusion = bf16[4096,768]{1,0:T(8,128)(2,1)} fusion(bf16[4096,768]{1,0:T(8,128)(2,1)} %copy.21.k_ref, s32[1024]{0:T(1024)S(1)} %fusion.8, bf16[1024,896]{1,0:T(8,128)(2,1)S(1)} %bitcast.18), kind=kCustom, calls=%fused_computation.61 | custom fusion | bytes 7864320 | tf_op jit(solution)/shard_map/scatter | solution.py:435
  (25 shorter events, 0.8 us)
Async XLA Ops:
  0.6 6.0 %copy-start.6 = (s32[8]{0:T(128)S(1)}, s32[8]{0:T(128)}, u32[]{:S(2)}) copy-start(s32[8]{0:T(128)} %param.15) | copy-start | bytes 100
  0.6 7.6 %copy-start.3 = (bf16[8,768]{1,0:T(8,128)(2,1)S(1)}, bf16[8,768]{1,0:T(8,128)(2,1)}, u32[]{:S(2)}) copy-start(bf16[8,768]{1,0:T(8,128)(2,1)} %param.14) | copy-start | bytes 36868
  0.7 9.6 %copy-start.5 = (s32[128]{0:T(128)S(1)}, s32[128]{0:T(128)}, u32[]{:S(2)}) copy-start(s32[128]{0:T(128)} %param.17) | copy-start | bytes 1540
  0.7 11.4 %copy-start.2 = (bf16[128,768]{1,0:T(8,128)(2,1)S(1)}, bf16[128,768]{1,0:T(8,128)(2,1)}, u32[]{:S(2)}) copy-start(bf16[128,768]{1,0:T(8,128)(2,1)} %param.16) | copy-start | bytes 589828
  46.9 1.6 %copy-start.1 = (bf16[2,4,128,896]{3,2,1,0:T(8,128)(2,1)S(1)}, bf16[2,4,128,896]{3,2,1,0:T(8,128)(2,1)}, u32[]{:S(2)}) copy-start(bf16[2,4,128,896]{3,2,1,0:T(8,128)(2,1)} %get-tuple-element.57) | copy-start | bytes 5505028
  76.9 47.5 %copy-start = (bf16[4,2,4,4,8,896]{5,4,3,2,1,0:T(8,128)(2,1)S(1)}, bf16[4,2,4,4,8,896]{5,4,3,2,1,0:T(8,128)(2,1)}, u32[]{:S(2)}) copy-start(bf16[4,2,4,4,8,896]{5,4,3,2,1,0:T(8,128)(2,1)} %get-tuple-element.61) | copy-start | bytes 5505028
  123.4 1.7 %copy-start.4 = (f32[8,896]{1,0:T(8,128)S(1)}, f32[8,896]{1,0:T(8,128)}, u32[]{:S(2)}) copy-start(f32[8,896]{1,0:T(8,128)} %get-tuple-element.60) | copy-start | bytes 86020

commit v18 on v17

--- a/solution.py
+++ b/solution.py
@@ -10,7 +10,7 @@
 MESH = pl.DeviceIdType.MESH
 STAT = 128
 FRESH_HELD = 8
-KEY_CHUNK = 512
+KEY_CHUNK = 1024
 
 
 def score_rows(query_rows, key_rows):

time: 142 us -> 142 us (level)
  no operation moved by 1% of the time
where the time goes in v18:
time: 142 us
  Pallas kernels  106 us (75%)
  local copies, waits for them, and re-layouts  23.3 us (16%)
  other arithmetic  8.21 us (6%)
  between operations  2.58 us (2%)
    pallas_call x1, Pallas kernels, combine(): pl.pallas_call(functools.partial(combine_kernel, d, side), out_shape=(jax...  46.5 us
    pallas_call x1, Pallas kernels, gather_dp(): pl.pallas_call(gather_kernel, out_shape=(jax.ShapeDtypeStruct((2, ys) + x...  34.1 us
    pallas_call x1, Pallas kernels, local_partials(): pl.pallas_call(partial_kernel, grid=(rows // block,), out_shape=(jax.Shap...  25.9 us
    scatter x1, local copies, waits for them, and re-layouts, shards(): queue_keys.at[target].set(fresh_all, mode='drop', unique_indices=True)  11.9 us
    unnamed x15, local copies, waits for them, and re-layouts  6.01 us
    another operation x5, other arithmetic  4.06 us

profile of v18, /device:TPU:1, one launch (start us, length us, event | category | flops | bytes accessed | tf_op | source)
XLA Modules:
  0.0 141.7 jit_solution(11864142107137695163)
XLA Ops:
  0.7 5.9 %copy.21.k_ref = bf16[4096,768]{1,0:T(8,128)(2,1)} copy(bf16[4096,768]{1,0:T(8,128)(2,1)} %param.13) | data formatting | bytes 12582912
  6.9 0.6 compare_reduce_fusion
  7.6 0.7 maximum_select_fusion
  8.3 0.6 fusion.13.f_ref
  8.9 0.6 compare_reduce_fusion.1
  9.5 0.7 compare_reduce_fusion.2
  10.2 1.3 fusion.15
  11.6 0.1 copy.13
  11.9 0.2 scatter.21
  12.1 0.7 pad_maximum_fusion.x_ref
  12.8 34.1 %shard_map.76 = (bf16[2,4,128,896]{3,2,1,0:T(8,128)(2,1)}, bf16[4,2,4,4,8,896]{5,4,3,2,1,0:T(8,128)(2,1)}) custom-call(bf16[128,896]{1,0:T(8,128)(2,1)} %pad_maximum_fusion.x_ref, bf16[8,896]{1,0:T(8,128)(2,1)} %fusion.13.f_ref), custom_call_target="tpu_custom_call" | custom-call | tf_op jit(solution)/shard_map/pallas_call | solution.py:161
  46.9 1.1 slice_convert_fusion.1
  48.0 0.4 fusion.11
  48.5 1.1 fusion.5
  49.6 1.2 broadcast_in_dim.26.pos_ref
  50.8 0.7 scatter.30.f_ref
  51.5 25.9 %shard_map.77 = (f32[1024,768]{1,0:T(8,128)}, f32[1024,128]{1,0:T(8,128)}) custom-call(bf16[1024,896]{1,0:T(8,128)(2,1)} %bitcast.21, bf16[4096,768]{1,0:T(8,128)(2,1)} %copy.21.k_ref, bf16[128,768]{1,0:T(8,128)(2,1)} %scatter.30.f_ref), custom_call_target="tpu_custom_call" | custom-call | tf_op jit(solution)/shard_map/pallas_call | solution.py:62
  77.4 46.5 %shard_map.78 = (f32[8,896]{1,0:T(8,128)}, f32[8,128]{1,0:T(8,128)}) custom-call(f32[2,64,8,768]{3,2,1,0:T(8,128)} %bitcast.19, f32[2,64,8,128]{3,2,1,0:T(8,128)} %bitcast.23, f32[8,128]{1,0:T(8,128)} %broadcast_in_dim.26.pos_ref), custom_call_target="tpu_custom_call" | custom-call | tf_op jit(solution)/shard_map/pallas_call | solution.py:345
  123.9 0.9 slice_reduce_fusion
  125.1 0.6 gather_fusion
  125.6 0.7 convert_subtract_fusion
  126.3 1.2 slice.104
  128.2 0.5 fusion.8
  128.7 11.9 %scatter_custom_fusion = bf16[4096,768]{1,0:T(8,128)(2,1)} fusion(bf16[4096,768]{1,0:T(8,128)(2,1)} %copy.21.k_ref, s32[1024]{0:T(1024)S(1)} %fusion.8, bf16[1024,896]{1,0:T(8,128)(2,1)S(1)} %bitcast.18), kind=kCustom, calls=%fused_computation.61 | custom fusion | bytes 7864320 | tf_op jit(solution)/shard_map/scatter | solution.py:435
  (25 shorter events, 0.8 us)
Async XLA Ops:
  0.6 6.0 %copy-start.6 = (s32[8]{0:T(128)S(1)}, s32[8]{0:T(128)}, u32[]{:S(2)}) copy-start(s32[8]{0:T(128)} %param.15) | copy-start | bytes 100
  0.6 7.6 %copy-start.3 = (bf16[8,768]{1,0:T(8,128)(2,1)S(1)}, bf16[8,768]{1,0:T(8,128)(2,1)}, u32[]{:S(2)}) copy-start(bf16[8,768]{1,0:T(8,128)(2,1)} %param.14) | copy-start | bytes 36868
  0.7 9.6 %copy-start.5 = (s32[128]{0:T(128)S(1)}, s32[128]{0:T(128)}, u32[]{:S(2)}) copy-start(s32[128]{0:T(128)} %param.17) | copy-start | bytes 1540
  0.7 11.4 %copy-start.2 = (bf16[128,768]{1,0:T(8,128)(2,1)S(1)}, bf16[128,768]{1,0:T(8,128)(2,1)}, u32[]{:S(2)}) copy-start(bf16[128,768]{1,0:T(8,128)(2,1)} %param.16) | copy-start | bytes 589828
  46.9 1.6 %copy-start.1 = (bf16[2,4,128,896]{3,2,1,0:T(8,128)(2,1)S(1)}, bf16[2,4,128,896]{3,2,1,0:T(8,128)(2,1)}, u32[]{:S(2)}) copy-start(bf16[2,4,128,896]{3,2,1,0:T(8,128)(2,1)} %get-tuple-element.57) | copy-start | bytes 5505028
  77.4 47.5 %copy-start = (bf16[4,2,4,4,8,896]{5,4,3,2,1,0:T(8,128)(2,1)S(1)}, bf16[4,2,4,4,8,896]{5,4,3,2,1,0:T(8,128)(2,1)}, u32[]{:S(2)}) copy-start(bf16[4,2,4,4,8,896]{5,4,3,2,1,0:T(8,128)(2,1)} %get-tuple-element.61) | copy-start | bytes 5505028
  123.9 1.7 %copy-start.4 = (f32[8,896]{1,0:T(8,128)S(1)}, f32[8,896]{1,0:T(8,128)}, u32[]{:S(2)}) copy-start(f32[8,896]{1,0:T(8,128)} %get-tuple-element.60) | copy-start | bytes 86020

commit v19 on v18

--- a/solution.py
+++ b/solution.py
@@ -10,7 +10,7 @@
 MESH = pl.DeviceIdType.MESH
 STAT = 128
 FRESH_HELD = 8
-KEY_CHUNK = 1024
+KEY_CHUNK = 256
 
 
 def score_rows(query_rows, key_rows):

time: 142 us -> 150 us (1.056)
  Pallas kernels: 106 us -> 115 us
    pallas_call x1, Pallas kernels: 25.9 us -> 33.9 us  [local_partials(): pl.pallas_call(partial_kernel, grid=(rows // block,), out_shape=(jax.Shap...]
where the time goes in v19:
time: 150 us
  Pallas kernels  115 us (77%)
  local copies, waits for them, and re-layouts  23.3 us (16%)
  other arithmetic  8.21 us (5%)
  between operations  2.58 us (2%)
    pallas_call x1, Pallas kernels, combine(): pl.pallas_call(functools.partial(combine_kernel, d, side), out_shape=(jax...  46.5 us
    pallas_call x1, Pallas kernels, gather_dp(): pl.pallas_call(gather_kernel, out_shape=(jax.ShapeDtypeStruct((2, ys) + x...  34.1 us
    pallas_call x1, Pallas kernels, local_partials(): pl.pallas_call(partial_kernel, grid=(rows // block,), out_shape=(jax.Shap...  33.9 us
    scatter x1, local copies, waits for them, and re-layouts, shards(): queue_keys.at[target].set(fresh_all, mode='drop', unique_indices=True)  11.9 us
    unnamed x15, local copies, waits for them, and re-layouts  6.01 us
    another operation x5, other arithmetic  4.06 us

profile of v19, /device:TPU:1, one launch (start us, length us, event | category | flops | bytes accessed | tf_op | source)
XLA Modules:
  0.0 149.8 jit_solution(14806397092522467386)
XLA Ops:
  0.7 5.9 %copy.21.k_ref = bf16[4096,768]{1,0:T(8,128)(2,1)} copy(bf16[4096,768]{1,0:T(8,128)(2,1)} %param.13) | data formatting | bytes 12582912
  6.9 0.6 compare_reduce_fusion
  7.6 0.7 maximum_select_fusion
  8.3 0.6 fusion.13.f_ref
  8.9 0.6 compare_reduce_fusion.1
  9.5 0.7 compare_reduce_fusion.2
  10.2 1.3 fusion.15
  11.6 0.1 copy.13
  11.9 0.2 scatter.21
  12.1 0.7 pad_maximum_fusion.x_ref
  12.8 34.1 %shard_map.76 = (bf16[2,4,128,896]{3,2,1,0:T(8,128)(2,1)}, bf16[4,2,4,4,8,896]{5,4,3,2,1,0:T(8,128)(2,1)}) custom-call(bf16[128,896]{1,0:T(8,128)(2,1)} %pad_maximum_fusion.x_ref, bf16[8,896]{1,0:T(8,128)(2,1)} %fusion.13.f_ref), custom_call_target="tpu_custom_call" | custom-call | tf_op jit(solution)/shard_map/pallas_call | solution.py:161
  46.9 1.1 slice_convert_fusion.1
  48.0 0.4 fusion.11
  48.5 1.1 fusion.5
  49.6 1.2 broadcast_in_dim.26.pos_ref
  50.8 0.7 scatter.30.f_ref
  51.5 33.9 %shard_map.77 = (f32[1024,768]{1,0:T(8,128)}, f32[1024,128]{1,0:T(8,128)}) custom-call(bf16[1024,896]{1,0:T(8,128)(2,1)} %bitcast.21, bf16[4096,768]{1,0:T(8,128)(2,1)} %copy.21.k_ref, bf16[128,768]{1,0:T(8,128)(2,1)} %scatter.30.f_ref), custom_call_target="tpu_custom_call" | custom-call | tf_op jit(solution)/shard_map/pallas_call | solution.py:62
  85.4 46.5 %shard_map.78 = (f32[8,896]{1,0:T(8,128)}, f32[8,128]{1,0:T(8,128)}) custom-call(f32[2,64,8,768]{3,2,1,0:T(8,128)} %bitcast.19, f32[2,64,8,128]{3,2,1,0:T(8,128)} %bitcast.23, f32[8,128]{1,0:T(8,128)} %broadcast_in_dim.26.pos_ref), custom_call_target="tpu_custom_call" | custom-call | tf_op jit(solution)/shard_map/pallas_call | solution.py:345
  132.0 0.9 slice_reduce_fusion
  133.1 0.6 gather_fusion
  133.7 0.7 convert_subtract_fusion
  134.4 1.2 slice.104
  136.3 0.5 fusion.8
  136.8 11.9 %scatter_custom_fusion = bf16[4096,768]{1,0:T(8,128)(2,1)} fusion(bf16[4096,768]{1,0:T(8,128)(2,1)} %copy.21.k_ref, s32[1024]{0:T(1024)S(1)} %fusion.8, bf16[1024,896]{1,0:T(8,128)(2,1)S(1)} %bitcast.18), kind=kCustom, calls=%fused_computation.61 | custom fusion | bytes 7864320 | tf_op jit(solution)/shard_map/scatter | solution.py:435
  (25 shorter events, 0.8 us)
Async XLA Ops:
  0.6 6.0 %copy-start.6 = (s32[8]{0:T(128)S(1)}, s32[8]{0:T(128)}, u32[]{:S(2)}) copy-start(s32[8]{0:T(128)} %param.15) | copy-start | bytes 100
  0.6 7.6 %copy-start.3 = (bf16[8,768]{1,0:T(8,128)(2,1)S(1)}, bf16[8,768]{1,0:T(8,128)(2,1)}, u32[]{:S(2)}) copy-start(bf16[8,768]{1,0:T(8,128)(2,1)} %param.14) | copy-start | bytes 36868
  0.7 9.6 %copy-start.5 = (s32[128]{0:T(128)S(1)}, s32[128]{0:T(128)}, u32[]{:S(2)}) copy-start(s32[128]{0:T(128)} %param.17) | copy-start | bytes 1540
  0.7 11.4 %copy-start.2 = (bf16[128,768]{1,0:T(8,128)(2,1)S(1)}, bf16[128,768]{1,0:T(8,128)(2,1)}, u32[]{:S(2)}) copy-start(bf16[128,768]{1,0:T(8,128)(2,1)} %param.16) | copy-start | bytes 589828
  46.9 1.6 %copy-start.1 = (bf16[2,4,128,896]{3,2,1,0:T(8,128)(2,1)S(1)}, bf16[2,4,128,896]{3,2,1,0:T(8,128)(2,1)}, u32[]{:S(2)}) copy-start(bf16[2,4,128,896]{3,2,1,0:T(8,128)(2,1)} %get-tuple-element.57) | copy-start | bytes 5505028
  85.4 47.5 %copy-start = (bf16[4,2,4,4,8,896]{5,4,3,2,1,0:T(8,128)(2,1)S(1)}, bf16[4,2,4,4,8,896]{5,4,3,2,1,0:T(8,128)(2,1)}, u32[]{:S(2)}) copy-start(bf16[4,2,4,4,8,896]{5,4,3,2,1,0:T(8,128)(2,1)} %get-tuple-element.61) | copy-start | bytes 5505028
  132.0 1.7 %copy-start.4 = (f32[8,896]{1,0:T(8,128)S(1)}, f32[8,896]{1,0:T(8,128)}, u32[]{:S(2)}) copy-start(f32[8,896]{1,0:T(8,128)} %get-tuple-element.60) | copy-start | bytes 86020

commit v20 on v17

--- a/solution.py
+++ b/solution.py
@@ -383,11 +383,10 @@
     assert fresh_keys.shape[0] == FRESH_HELD
     assert queue_size == (dp_size // 2) ** 2
     d = queries.shape[1]
-    pos_code = jnp.zeros((queries.shape[0], STAT), jnp.bfloat16)
-    pos_code = pos_code.at[:, 0].set((positives // 32).astype(jnp.bfloat16))
-    pos_code = pos_code.at[:, 1].set((positives % 32).astype(jnp.bfloat16))
+    pos_code = jnp.stack([positives // 32, positives % 32], axis=1).astype(jnp.bfloat16)
+    pos_code = jnp.pad(pos_code, ((0, 0), (0, STAT - 2)))
     digits = jnp.stack([slots // 16384, (slots // 128) % 128, slots % 128], axis=1)
-    code = jnp.zeros((slots.shape[0], STAT), jnp.bfloat16).at[:, :3].set(digits.astype(jnp.bfloat16))
+    code = jnp.pad(digits.astype(jnp.bfloat16), ((0, 0), (0, STAT - 3)))
     gathered, fresh_ext = gather_dp(
         jnp.concatenate([queries, pos_code], axis=1),
         jnp.concatenate([fresh_keys, code], axis=1),
@@ -405,7 +404,7 @@
     slots_all = got[:, 0] * 16384 + got[:, 1] * 128 + got[:, 2]
 
     device_index = _device_index()
-    fresh_padded = jnp.zeros((STAT, d), fresh_keys.dtype).at[:fresh_keys.shape[0]].set(fresh_keys)
+    fresh_padded = jnp.pad(fresh_keys, ((0, STAT - fresh_keys.shape[0]), (0, 0)))
     local_pulled, stats = local_partials(gathered, queue_keys, fresh_padded, min(256, total_rows))
     fresh_scores = score_rows(all_queries, fresh_keys)
     fresh_ids = device_index * fresh_keys.shape[0] + jnp.arange(fresh_keys.shape[0], dtype=jnp.int32)

time: 142 us -> 137 us (0.965)
  other arithmetic: 8.21 us -> 4.25 us
    another operation x5 -> x2, other arithmetic: 4.06 us -> 0.02 us  [shards(): jnp.stack([positives // 32, positives % 32], axis=1).astype(jnp.bfloat16)]
where the time goes in v20:
time: 137 us
  Pallas kernels  106 us (77%)
  local copies, waits for them, and re-layouts  23 us (17%)
  other arithmetic  4.25 us (3%)
  between operations  2.56 us (2%)
    pallas_call x1, Pallas kernels, combine(): pl.pallas_call(functools.partial(combine_kernel, d, side), out_shape=(jax...  46.5 us
    pallas_call x1, Pallas kernels, gather_dp(): pl.pallas_call(gather_kernel, out_shape=(jax.ShapeDtypeStruct((2, ys) + x...  34.1 us
    pallas_call x1, Pallas kernels, local_partials(): pl.pallas_call(partial_kernel, grid=(rows // block,), out_shape=(jax.Shap...  25.4 us
    scatter x1, local copies, waits for them, and re-layouts, shards(): queue_keys.at[target].set(fresh_all, mode='drop', unique_indices=True)  11.9 us
    unnamed x15, local copies, waits for them, and re-layouts  6.01 us

profile of v20, /device:TPU:1, one launch (start us, length us, event | category | flops | bytes accessed | tf_op | source)
XLA Modules:
  0.0 136.9 jit_solution(13504994327948453897)
XLA Ops:
  0.7 5.9 %copy.24.k_ref = bf16[4096,768]{1,0:T(8,128)(2,1)} copy(bf16[4096,768]{1,0:T(8,128)(2,1)} %param.5) | data formatting | bytes 12582912
  6.6 0.1 copy.19
  6.7 0.1 copy.20
  6.8 0.1 copy.21
  6.9 0.1 fusion.18
  7.0 0.6 pad_maximum_fusion.f_ref
  7.6 0.1 copy.18
  7.8 0.7 fusion.13.x_ref
  8.5 34.1 %shard_map.76 = (bf16[2,4,128,896]{3,2,1,0:T(8,128)(2,1)}, bf16[4,2,4,4,8,896]{5,4,3,2,1,0:T(8,128)(2,1)}) custom-call(bf16[128,896]{1,0:T(8,128)(2,1)} %fusion.13.x_ref, bf16[8,896]{1,0:T(8,128)(2,1)} %pad_maximum_fusion.f_ref), custom_call_target="tpu_custom_call" | custom-call | tf_op jit(solution)/shard_map/pallas_call | solution.py:161
  42.6 1.1 slice_convert_fusion.1
  43.7 0.4 fusion.11
  44.2 1.1 fusion.5
  45.3 1.2 broadcast_in_dim.23.pos_ref
  46.5 0.7 pad.14.f_ref
  47.2 25.4 %shard_map.77 = (f32[1024,768]{1,0:T(8,128)}, f32[1024,128]{1,0:T(8,128)}) custom-call(bf16[1024,896]{1,0:T(8,128)(2,1)} %bitcast.21, bf16[4096,768]{1,0:T(8,128)(2,1)} %copy.24.k_ref, bf16[128,768]{1,0:T(8,128)(2,1)} %pad.14.f_ref), custom_call_target="tpu_custom_call" | custom-call | tf_op jit(solution)/shard_map/pallas_call | solution.py:62
  72.6 46.5 %shard_map.78 = (f32[8,896]{1,0:T(8,128)}, f32[8,128]{1,0:T(8,128)}) custom-call(f32[2,64,8,768]{3,2,1,0:T(8,128)} %bitcast.19, f32[2,64,8,128]{3,2,1,0:T(8,128)} %bitcast.23, f32[8,128]{1,0:T(8,128)} %broadcast_in_dim.23.pos_ref), custom_call_target="tpu_custom_call" | custom-call | tf_op jit(solution)/shard_map/pallas_call | solution.py:345
  119.1 0.9 slice_reduce_fusion
  120.1 0.1 compare_and_fusion
  120.2 0.1 slice.54
  120.3 0.6 gather_fusion
  120.9 0.7 convert_subtract_fusion
  121.5 1.2 slice.43
  123.5 0.5 fusion.8
  124.0 11.9 %scatter_custom_fusion = bf16[4096,768]{1,0:T(8,128)(2,1)} fusion(bf16[4096,768]{1,0:T(8,128)(2,1)} %copy.24.k_ref, s32[1024]{0:T(1024)S(1)} %fusion.8, bf16[1024,896]{1,0:T(8,128)(2,1)S(1)} %bitcast.18), kind=kCustom, calls=%fused_computation.61 | custom fusion | bytes 7864320 | tf_op jit(solution)/shard_map/scatter | solution.py:434
  (20 shorter events, 0.2 us)
Async XLA Ops:
  0.6 6.0 %copy-start.5 = (s32[8]{0:T(128)S(1)}, s32[8]{0:T(128)}, u32[]{:S(2)}) copy-start(s32[8]{0:T(128)} %param.7) | copy-start | bytes 100
  0.6 6.4 %copy-start.3 = (bf16[8,768]{1,0:T(8,128)(2,1)S(1)}, bf16[8,768]{1,0:T(8,128)(2,1)}, u32[]{:S(2)}) copy-start(bf16[8,768]{1,0:T(8,128)(2,1)} %param.6) | copy-start | bytes 36868
  0.7 7.0 %copy-start.6 = (s32[128]{0:T(128)S(1)}, s32[128]{0:T(128)}, u32[]{:S(2)}) copy-start(s32[128]{0:T(128)} %param.9) | copy-start | bytes 1540
  0.7 7.1 %copy-start.2 = (bf16[128,768]{1,0:T(8,128)(2,1)S(1)}, bf16[128,768]{1,0:T(8,128)(2,1)}, u32[]{:S(2)}) copy-start(bf16[128,768]{1,0:T(8,128)(2,1)} %param.8) | copy-start | bytes 589828
  42.6 1.6 %copy-start.1 = (bf16[2,4,128,896]{3,2,1,0:T(8,128)(2,1)S(1)}, bf16[2,4,128,896]{3,2,1,0:T(8,128)(2,1)}, u32[]{:S(2)}) copy-start(bf16[2,4,128,896]{3,2,1,0:T(8,128)(2,1)} %get-tuple-element.9) | copy-start | bytes 5505028
  72.6 47.5 %copy-start = (bf16[4,2,4,4,8,896]{5,4,3,2,1,0:T(8,128)(2,1)S(1)}, bf16[4,2,4,4,8,896]{5,4,3,2,1,0:T(8,128)(2,1)}, u32[]{:S(2)}) copy-start(bf16[4,2,4,4,8,896]{5,4,3,2,1,0:T(8,128)(2,1)} %get-tuple-element.13) | copy-start | bytes 5505028
  119.1 1.7 %copy-start.4 = (f32[8,896]{1,0:T(8,128)S(1)}, f32[8,896]{1,0:T(8,128)}, u32[]{:S(2)}) copy-start(f32[8,896]{1,0:T(8,128)} %get-tuple-element.12) | copy-start | bytes 86020

commit v21 on v20

--- a/solution.py
+++ b/solution.py
@@ -414,7 +414,7 @@
     combined, loss_tile = combine(
         local_pulled.reshape(halves + (d,)),
         stats.reshape(halves + (STAT,)),
-        jnp.full((8, 128), positive_total, jnp.float32),
+        positive_total.reshape(1, 1),
         d,
         dp_size // 2,
     )

time: 137 us -> 136 us (level)
  no operation moved by 1% of the time
where the time goes in v21:
time: 136 us
  Pallas kernels  106 us (78%)
  local copies, waits for them, and re-layouts  21.8 us (16%)
  other arithmetic  4.25 us (3%)
  between operations  2.56 us (2%)
    pallas_call x1, Pallas kernels, combine(): pl.pallas_call(functools.partial(combine_kernel, d, side), out_shape=(jax...  46.7 us
    pallas_call x1, Pallas kernels, gather_dp(): pl.pallas_call(gather_kernel, out_shape=(jax.ShapeDtypeStruct((2, ys) + x...  34.1 us
    pallas_call x1, Pallas kernels, local_partials(): pl.pallas_call(partial_kernel, grid=(rows // block,), out_shape=(jax.Shap...  25.4 us
    scatter x1, local copies, waits for them, and re-layouts, shards(): queue_keys.at[target].set(fresh_all, mode='drop', unique_indices=True)  11.9 us
    unnamed x15, local copies, waits for them, and re-layouts  6.01 us

profile of v21, /device:TPU:1, one launch (start us, length us, event | category | flops | bytes accessed | tf_op | source)
XLA Modules:
  0.0 135.9 jit_solution(15896674186747471146)
XLA Ops:
  0.7 5.9 %copy.24.k_ref = bf16[4096,768]{1,0:T(8,128)(2,1)} copy(bf16[4096,768]{1,0:T(8,128)(2,1)} %param.5) | data formatting | bytes 12582912
  6.6 0.1 copy.19
  6.7 0.1 copy.20
  6.8 0.1 copy.21
  6.9 0.1 fusion.18
  7.0 0.6 pad_maximum_fusion.f_ref
  7.6 0.1 copy.18
  7.8 0.7 fusion.13.x_ref
  8.5 34.1 %shard_map.76 = (bf16[2,4,128,896]{3,2,1,0:T(8,128)(2,1)}, bf16[4,2,4,4,8,896]{5,4,3,2,1,0:T(8,128)(2,1)}) custom-call(bf16[128,896]{1,0:T(8,128)(2,1)} %fusion.13.x_ref, bf16[8,896]{1,0:T(8,128)(2,1)} %pad_maximum_fusion.f_ref), custom_call_target="tpu_custom_call" | custom-call | tf_op jit(solution)/shard_map/pallas_call | solution.py:161
  42.6 1.1 slice_convert_fusion.1
  43.7 0.4 fusion.11
  44.2 1.1 fusion.5
  45.3 0.7 pad.14.f_ref
  46.0 25.4 %shard_map.77 = (f32[1024,768]{1,0:T(8,128)}, f32[1024,128]{1,0:T(8,128)}) custom-call(bf16[1024,896]{1,0:T(8,128)(2,1)} %bitcast.22, bf16[4096,768]{1,0:T(8,128)(2,1)} %copy.24.k_ref, bf16[128,768]{1,0:T(8,128)(2,1)} %pad.14.f_ref), custom_call_target="tpu_custom_call" | custom-call | tf_op jit(solution)/shard_map/pallas_call | solution.py:62
  71.4 46.7 %shard_map.78 = (f32[8,896]{1,0:T(8,128)}, f32[8,128]{1,0:T(8,128)}) custom-call(f32[2,64,8,768]{3,2,1,0:T(8,128)} %bitcast.20, f32[2,64,8,128]{3,2,1,0:T(8,128)} %bitcast.24, f32[1,1]{1,0:T(1,128)} %bitcast.8.pos_ref), custom_call_target="tpu_custom_call" | custom-call | tf_op jit(solution)/shard_map/pallas_call | solution.py:345
  118.1 0.9 slice_reduce_fusion
  119.0 0.1 compare_and_fusion
  119.1 0.1 slice.54
  119.2 0.6 gather_fusion
  119.8 0.7 convert_subtract_fusion
  120.5 1.2 slice.43
  122.3 0.1 slice_convert_fusion
  122.4 0.5 fusion.8
  122.9 11.9 %scatter_custom_fusion = bf16[4096,768]{1,0:T(8,128)(2,1)} fusion(bf16[4096,768]{1,0:T(8,128)(2,1)} %copy.24.k_ref, s32[1024]{0:T(1024)S(1)} %fusion.8, bf16[1024,896]{1,0:T(8,128)(2,1)S(1)} %bitcast.19), kind=kCustom, calls=%fused_computation.61 | custom fusion | bytes 7864320 | tf_op jit(solution)/shard_map/scatter | solution.py:434
  (19 shorter events, 0.1 us)
Async XLA Ops:
  0.6 6.0 %copy-start.5 = (s32[8]{0:T(128)S(1)}, s32[8]{0:T(128)}, u32[]{:S(2)}) copy-start(s32[8]{0:T(128)} %param.7) | copy-start | bytes 100
  0.6 6.4 %copy-start.3 = (bf16[8,768]{1,0:T(8,128)(2,1)S(1)}, bf16[8,768]{1,0:T(8,128)(2,1)}, u32[]{:S(2)}) copy-start(bf16[8,768]{1,0:T(8,128)(2,1)} %param.6) | copy-start | bytes 36868
  0.7 7.0 %copy-start.6 = (s32[128]{0:T(128)S(1)}, s32[128]{0:T(128)}, u32[]{:S(2)}) copy-start(s32[128]{0:T(128)} %param.9) | copy-start | bytes 1540
  0.7 7.1 %copy-start.2 = (bf16[128,768]{1,0:T(8,128)(2,1)S(1)}, bf16[128,768]{1,0:T(8,128)(2,1)}, u32[]{:S(2)}) copy-start(bf16[128,768]{1,0:T(8,128)(2,1)} %param.8) | copy-start | bytes 589828
  42.6 1.6 %copy-start.1 = (bf16[2,4,128,896]{3,2,1,0:T(8,128)(2,1)S(1)}, bf16[2,4,128,896]{3,2,1,0:T(8,128)(2,1)}, u32[]{:S(2)}) copy-start(bf16[2,4,128,896]{3,2,1,0:T(8,128)(2,1)} %get-tuple-element.9) | copy-start | bytes 5505028
  71.4 47.7 %copy-start = (bf16[4,2,4,4,8,896]{5,4,3,2,1,0:T(8,128)(2,1)S(1)}, bf16[4,2,4,4,8,896]{5,4,3,2,1,0:T(8,128)(2,1)}, u32[]{:S(2)}) copy-start(bf16[4,2,4,4,8,896]{5,4,3,2,1,0:T(8,128)(2,1)} %get-tuple-element.13) | copy-start | bytes 5505028
  118.1 1.7 %copy-start.4 = (f32[8,896]{1,0:T(8,128)S(1)}, f32[8,896]{1,0:T(8,128)}, u32[]{:S(2)}) copy-start(f32[8,896]{1,0:T(8,128)} %get-tuple-element.12) | copy-start | bytes 86020
